TPU v7x, 32 devices: a whole 2x2x4 slice. The times are simulated.
32 devices in a mesh: ctx: 16 (over z, y, core), wsh: 2 (over x).
Axes of the slice: x: 2, y: 2, z: 4, core: 2. Of those that a mesh axis runs over, the one named last changes fastest.
Arguments:
- tokens: bfloat16 [4, 4096, 768], P('wsh', 'ctx'), may hold values from -6 to 6
- first_values: bfloat16 [4, 4096, 384], P('wsh', 'ctx'), may hold values from -6 to 6
- teacher: bfloat16 [4, 4096, 768], P('wsh', 'ctx'), may hold values from -20 to 20
- segment_ids: int32 [4, 4096], P('wsh'), may hold values from 0 to 3, never falling along the last dimension, each value on 1 to 2048 neighbouring positions
- lengths: int32 [4], P('wsh'), may hold values from 2049 to 4096, as said below
- ln1_gain: bfloat16 [768], P('wsh'), may hold values from 0.5 to 1.5
- ln1_bias: bfloat16 [768], P('wsh'), may hold values from -1 to 1
- w_qkv: bfloat16 [768, 1920], P('wsh'), may hold values from -0.21875 to 0.21875
- qv_bias: bfloat16 [1152], P('wsh'), may hold values from -1 to 1
- w_out: bfloat16 [768, 768], P('wsh'), may hold values from -1.75 to 1.75
- b_out: bfloat16 [768], P('wsh'), may hold values from -1 to 1
- ln2_gain: bfloat16 [768], P('wsh'), may hold values from 0.5 to 1.5
- ln2_bias: bfloat16 [768], P('wsh'), may hold values from -1 to 1
- w_fc: bfloat16 [768, 3072], P('wsh'), may hold values from -0.21875 to 0.21875
- b_fc: bfloat16 [3072], P('wsh'), may hold values from -1 to 1
- w_proj: bfloat16 [3072, 768], P('wsh'), may hold values from -0.109375 to 0.109375
- b_proj: bfloat16 [768], P('wsh'), may hold values from -1 to 1
Outputs:
- loss: float32 [], replicated
- output: bfloat16 [4, 4096, 768], P('wsh', 'ctx')
- grad_tokens: float32 [4, 4096, 768], P('wsh', 'ctx')
- grad_first: float32 [4, 4096, 384], P('wsh', 'ctx')
- grad_ln1_gain: float32 [768], P('wsh')
- grad_ln1_bias: float32 [768], P('wsh')
- grad_w_qkv: float32 [768, 1920], P('wsh')
- grad_qv_bias: float32 [1152], P('wsh')
- grad_w_out: float32 [768, 768], P('wsh')
- grad_b_out: float32 [768], P('wsh')
- grad_ln2_gain: float32 [768], P('wsh')
- grad_ln2_bias: float32 [768], P('wsh')
- grad_w_fc: float32 [768, 3072], P('wsh')
- grad_b_fc: float32 [3072], P('wsh')
- grad_w_proj: float32 [3072, 768], P('wsh')
- grad_b_proj: float32 [768], P('wsh')
Inputs may be any that keep to these rules, and one draw needn't show every extreme that they name: `segment_ids`: along each sequence the ids never fall; every document (run of one id) has 1 to 2048 tokens, and some document has exactly 2048. `lengths`: in each group of 2 consecutive sequences, one is valid in full.
All inputs are finite; a program needn't handle non-finite values.
Results may differ from a plain program's by a relative error of at most 0.013.
Values may be sent and summed in bfloat16 or wider, within the bound.
A program may use at most 192 MiB of HBM per device.

v0:
```python
import jax
import jax.numpy as jnp
from jax import lax
from jax.sharding import PartitionSpec as P

D = 768
HEADS = 12
HEAD = 64
DOC_MAX = 2048
VW = 384


EPS = 1e-05
NEG = -1e30


def passed_along(value, axis, steps):
    count = lax.axis_size(axis)
    initial, last = (max(0, -steps), min(count, count - steps))
    return lax.ppermute(value, axis, [(source, source + steps) for source in range(initial, last)])


def from_behind(value, axis, steps):
    count = lax.axis_size(axis)
    pairs = [(source, (source + steps) % count) for source in range(count)]
    return lax.ppermute(value, axis, pairs)


def norm_layer(values, gain_vec, offset):
    average = jnp.mean(values, axis=-1, keepdims=True)
    centred = values - average
    variance = jnp.mean(centred * centred, axis=-1, keepdims=True)
    return centred * lax.rsqrt(variance + EPS) * gain_vec + offset


def smooth_gate(values):
    return jax.nn.gelu(values, approximate=True)


def split_heads(array):
    return array.reshape(array.shape[0], array.shape[1], HEADS, HEAD)


def block_scores(query_heads, key_heads, allowed, score_scale):
    scores = (
        jnp.einsum("bqhd,bkhd->bqhk", query_heads, key_heads, preferred_element_type=jnp.float32)
        * score_scale
    )
    return jnp.where(allowed[:, :, None, :], scores, NEG)


def local(
    tokens,
    first_values,
    teacher,
    segment_ids,
    lengths,
    ln1_gain,
    ln1_bias,
    w_qkv,
    qv_bias,
    w_out,
    b_out,
    ln2_gain,
    ln2_bias,
    w_fc,
    b_fc,
    w_proj,
    b_proj,
):
    seq_count = tokens.shape[0]
    slice_len = tokens.shape[1]
    row_count = seq_count * slice_len
    ctx_size = lax.axis_size("ctx")
    ctx_index = lax.axis_index("ctx")
    reach_steps = (DOC_MAX - 2) // slice_len + 1
    score_scale = HEAD ** (-0.5)
    step_list = jnp.arange(1, reach_steps + 1, dtype=jnp.int32)
    (
        norm1_gain,
        norm1_shift,
        qkv_weight,
        qv_shift,
        out_weight,
        out_shift,
        norm2_gain,
        norm2_shift,
        fc_weight,
        fc_shift,
        proj_weight,
        proj_shift,
    ) = (
        lax.all_gather(ln1_gain, "wsh", axis=0, tiled=True),
        lax.all_gather(ln1_bias, "wsh", axis=0, tiled=True),
        lax.all_gather(w_qkv, "wsh", axis=0, tiled=True),
        lax.all_gather(qv_bias, "wsh", axis=0, tiled=True),
        lax.all_gather(w_out, "wsh", axis=0, tiled=True),
        lax.all_gather(b_out, "wsh", axis=0, tiled=True),
        lax.all_gather(ln2_gain, "wsh", axis=0, tiled=True),
        lax.all_gather(ln2_bias, "wsh", axis=0, tiled=True),
        lax.all_gather(w_fc, "wsh", axis=0, tiled=True),
        lax.all_gather(b_fc, "wsh", axis=0, tiled=True),
        lax.all_gather(w_proj, "wsh", axis=0, tiled=True),
        lax.all_gather(b_proj, "wsh", axis=0, tiled=True),
    )
    first_pos = ctx_index * slice_len
    query_pos = first_pos + jnp.arange(slice_len, dtype=jnp.int32)
    seg_query = lax.dynamic_slice_in_dim(segment_ids, first_pos, slice_len, 1)

    def mask_for(step_back):
        source_pos = (ctx_index - step_back) % ctx_size * slice_len
        seg_key = lax.dynamic_slice_in_dim(segment_ids, source_pos, slice_len, 1)
        key_pos = source_pos + jnp.arange(slice_len, dtype=jnp.int32)
        causal = key_pos[None, :] <= query_pos[:, None]
        own_key = key_pos[None, :] == query_pos[:, None]
        in_length = key_pos[None, None, :] < lengths[:, None, None]
        return (
            (seg_query[:, :, None] == seg_key[:, None, :])
            & causal[None]
            & (in_length | own_key[None])
        )

    inputs = tokens.reshape(row_count, D).astype(jnp.float32)
    normed1, norm1_back = jax.vjp(
        norm_layer, inputs, norm1_gain.astype(jnp.float32), norm1_shift.astype(jnp.float32)
    )
    normed1_low = normed1.astype(jnp.bfloat16)
    projected = jnp.dot(normed1_low, qkv_weight, preferred_element_type=jnp.float32)
    shift_wide = qv_shift.astype(jnp.float32)
    query_rows = (projected[:, :D] + shift_wide[:D]).astype(jnp.bfloat16)
    key_rows = projected[:, D : 2 * D].astype(jnp.bfloat16)
    fresh_rows = (projected[:, 2 * D :] + shift_wide[D:]).astype(jnp.bfloat16)
    value_rows = jnp.concatenate([fresh_rows, first_values.reshape(row_count, D - VW)], axis=1)
    query_heads = query_rows.reshape(seq_count, slice_len, HEADS, HEAD)
    own_block = jnp.stack(
        [key_rows.reshape(seq_count, slice_len, D), value_rows.reshape(seq_count, slice_len, D)]
    )

    def max_sum(state, block, step_back):
        allowed = mask_for(step_back)
        top_in, total_in = state
        scores = block_scores(query_heads, split_heads(block[0]), allowed, score_scale)
        new_top = jnp.maximum(top_in, jnp.max(scores, axis=-1))
        expo = jnp.exp(scores - new_top[..., None]) * allowed[:, :, None, :]
        return (new_top, total_in * jnp.exp(top_in - new_top) + jnp.sum(expo, axis=-1))

    start_state = (
        jnp.full((seq_count, slice_len, HEADS), NEG, jnp.float32),
        jnp.zeros((seq_count, slice_len, HEADS), jnp.float32),
    )
    state = max_sum(start_state, own_block, 0)

    def first_step(carry, step_back):
        block, state_now = carry
        block = passed_along(block, "ctx", 1)
        return ((block, max_sum(state_now, block, step_back)), None)

    (unused_block, state), kept = lax.scan(first_step, (own_block, state), step_list)
    log_total = state[0] + jnp.log(state[1])

    def attend(accum, block, step_back):
        allowed = mask_for(step_back)
        scores = block_scores(query_heads, split_heads(block[0]), allowed, score_scale)
        probs = (jnp.exp(scores - log_total[..., None]) * allowed[:, :, None, :]).astype(
            jnp.bfloat16
        )
        return accum + jnp.einsum(
            "bqhk,bkhd->bqhd", probs, split_heads(block[1]), preferred_element_type=jnp.float32
        )

    accum = attend(jnp.zeros((seq_count, slice_len, HEADS, HEAD), jnp.float32), own_block, 0)

    def second_again(carry, step_back):
        block, accum_now = carry
        block = passed_along(block, "ctx", 1)
        return ((block, attend(accum_now, block, step_back)), None)

    (unused_block, accum), unused = lax.scan(second_again, (own_block, accum), step_list)
    attended_wide = accum.reshape(row_count, D)
    attended_low = attended_wide.astype(jnp.bfloat16)
    resid = (
        inputs
        + jnp.dot(attended_low, out_weight, preferred_element_type=jnp.float32)
        + out_shift.astype(jnp.float32)
    )
    normed2, norm2_back = jax.vjp(
        norm_layer, resid, norm2_gain.astype(jnp.float32), norm2_shift.astype(jnp.float32)
    )
    normed2_low = normed2.astype(jnp.bfloat16)
    pre_act = jnp.dot(normed2_low, fc_weight, preferred_element_type=jnp.float32) + fc_shift.astype(
        jnp.float32
    )
    activ, gelu_back = jax.vjp(smooth_gate, pre_act)
    activ_low = activ.astype(jnp.bfloat16)
    out_wide = (
        resid
        + jnp.dot(activ_low, proj_weight, preferred_element_type=jnp.float32)
        + proj_shift.astype(jnp.float32)
    )
    valid_rows = (query_pos[None, :] < lengths[:, None]).astype(jnp.float32)
    deviation = (
        out_wide.reshape(seq_count, slice_len, D) - teacher.astype(jnp.float32)
    ) * valid_rows[:, :, None]
    squares, valid_count = lax.psum(
        (jnp.sum(deviation * deviation), jnp.sum(valid_rows)), ("ctx", "wsh")
    )
    loss = squares / (valid_count * D)
    grad_output = deviation.reshape(row_count, D)
    grad_mixed = grad_output.astype(jnp.bfloat16)
    grad_proj_w = jnp.einsum("rf,rd->fd", activ_low, grad_mixed, preferred_element_type=jnp.float32)
    grad_proj_b = jnp.sum(grad_mixed.astype(jnp.float32), axis=0)
    grad_activ = jnp.einsum(
        "rd,fd->rf", grad_mixed, proj_weight, preferred_element_type=jnp.float32
    )
    grad_pre = gelu_back(grad_activ)[0].astype(jnp.bfloat16)
    grad_fc_w = jnp.einsum("rd,rf->df", normed2_low, grad_pre, preferred_element_type=jnp.float32)
    grad_fc_b = jnp.sum(grad_pre.astype(jnp.float32), axis=0)
    grad_normed2 = jnp.einsum("rf,df->rd", grad_pre, fc_weight, preferred_element_type=jnp.float32)
    grad_resid_norm, grad_g2, grad_b2 = norm2_back(grad_normed2)
    grad_resid = grad_output + grad_resid_norm
    grad_branch = grad_resid.astype(jnp.bfloat16)
    grad_out_w = jnp.einsum(
        "rd,re->de", attended_low, grad_branch, preferred_element_type=jnp.float32
    )
    grad_out_b = jnp.sum(grad_branch.astype(jnp.float32), axis=0)
    grad_attended = jnp.einsum(
        "re,de->rd", grad_branch, out_weight, preferred_element_type=jnp.float32
    ).astype(jnp.bfloat16)
    grad_heads = grad_attended.reshape(seq_count, slice_len, HEADS, HEAD)
    delta = jnp.sum(grad_heads.astype(jnp.float32) * accum, axis=-1)

    def backward_block(block, step_back):
        allowed = mask_for(step_back)
        key_heads = split_heads(block[0])
        value_heads = split_heads(block[1])
        scores = block_scores(query_heads, key_heads, allowed, score_scale)
        probs = jnp.exp(scores - log_total[..., None]) * allowed[:, :, None, :]
        grad_probs = jnp.einsum(
            "bqhd,bkhd->bqhk", grad_heads, value_heads, preferred_element_type=jnp.float32
        )
        grad_scores = (probs * (grad_probs - delta[..., None])).astype(jnp.bfloat16)
        grad_query = (
            jnp.einsum(
                "bqhk,bkhd->bqhd", grad_scores, key_heads, preferred_element_type=jnp.float32
            )
            * score_scale
        )
        grad_keys = (
            jnp.einsum(
                "bqhk,bqhd->bkhd", grad_scores, query_heads, preferred_element_type=jnp.float32
            )
            * score_scale
        )
        grad_values = jnp.einsum(
            "bqhk,bqhd->bkhd",
            probs.astype(jnp.bfloat16),
            grad_heads,
            preferred_element_type=jnp.float32,
        )
        pair = jnp.stack(
            [
                grad_keys.reshape(seq_count, slice_len, D),
                grad_values.reshape(seq_count, slice_len, D),
            ]
        )
        return (grad_query.reshape(seq_count, slice_len, D), pair)

    query_grad, travel = backward_block(own_block, 0)

    def backward_step(carry, inputs_step):
        block, query_acc, travel_acc = carry
        travel_acc = from_behind(travel_acc.astype(jnp.bfloat16), "ctx", 1).astype(travel_acc.dtype)
        block = passed_along(block, "ctx", 1)
        grad_query, grad_pair = backward_block(block, inputs_step)
        return ((block, query_acc + grad_query, travel_acc + grad_pair), None)

    (unused_block, query_grad, travel), unused = lax.scan(
        backward_step, (own_block, query_grad, travel), step_list
    )
    travel = from_behind(travel.astype(jnp.bfloat16), "ctx", -reach_steps).astype(travel.dtype)
    grad_keys_own = travel[0].reshape(row_count, D)
    grad_values_own = travel[1].reshape(row_count, D)
    grad_first = grad_values_own[:, VW:]
    grad_query_low = query_grad.reshape(row_count, D).astype(jnp.bfloat16)
    grad_fresh_low = grad_values_own[:, :VW].astype(jnp.bfloat16)
    grad_projected = jnp.concatenate(
        [grad_query_low, grad_keys_own.astype(jnp.bfloat16), grad_fresh_low], axis=1
    )
    grad_qkv_w = jnp.einsum(
        "rd,rc->dc", normed1_low, grad_projected, preferred_element_type=jnp.float32
    )
    grad_qv_b = jnp.concatenate(
        [
            jnp.sum(grad_query_low.astype(jnp.float32), axis=0),
            jnp.sum(grad_fresh_low.astype(jnp.float32), axis=0),
        ]
    )
    grad_normed1 = jnp.einsum(
        "rc,dc->rd", grad_projected, qkv_weight, preferred_element_type=jnp.float32
    )
    grad_input_norm, grad_g1, grad_b1 = norm1_back(grad_normed1)
    grad_inputs = grad_resid + grad_input_norm
    grads = (
        grad_g1,
        grad_b1,
        grad_qkv_w,
        grad_qv_b,
        grad_out_w,
        grad_out_b,
        grad_g2,
        grad_b2,
        grad_fc_w,
        grad_fc_b,
        grad_proj_w,
        grad_proj_b,
    )
    shares = (
        lax.psum_scatter(
            grads[0].astype(jnp.bfloat16), "wsh", scatter_dimension=0, tiled=True
        ).astype(jnp.float32),
        lax.psum_scatter(
            grads[1].astype(jnp.bfloat16), "wsh", scatter_dimension=0, tiled=True
        ).astype(jnp.float32),
        lax.psum_scatter(
            grads[2].astype(jnp.bfloat16), "wsh", scatter_dimension=0, tiled=True
        ).astype(jnp.float32),
        lax.psum_scatter(
            grads[3].astype(jnp.bfloat16), "wsh", scatter_dimension=0, tiled=True
        ).astype(jnp.float32),
        lax.psum_scatter(
            grads[4].astype(jnp.bfloat16), "wsh", scatter_dimension=0, tiled=True
        ).astype(jnp.float32),
        lax.psum_scatter(
            grads[5].astype(jnp.bfloat16), "wsh", scatter_dimension=0, tiled=True
        ).astype(jnp.float32),
        lax.psum_scatter(
            grads[6].astype(jnp.bfloat16), "wsh", scatter_dimension=0, tiled=True
        ).astype(jnp.float32),
        lax.psum_scatter(
            grads[7].astype(jnp.bfloat16), "wsh", scatter_dimension=0, tiled=True
        ).astype(jnp.float32),
        lax.psum_scatter(
            grads[8].astype(jnp.bfloat16), "wsh", scatter_dimension=0, tiled=True
        ).astype(jnp.float32),
        lax.psum_scatter(
            grads[9].astype(jnp.bfloat16), "wsh", scatter_dimension=0, tiled=True
        ).astype(jnp.float32),
        lax.psum_scatter(
            grads[10].astype(jnp.bfloat16), "wsh", scatter_dimension=0, tiled=True
        ).astype(jnp.float32),
        lax.psum_scatter(
            grads[11].astype(jnp.bfloat16), "wsh", scatter_dimension=0, tiled=True
        ).astype(jnp.float32),
    )
    totals = tuple(
        lax.psum(
            (
                shares[0],
                shares[1],
                shares[2],
                shares[3],
                shares[4],
                shares[5],
                shares[6],
                shares[7],
                shares[8],
                shares[9],
                shares[10],
                shares[11],
            ),
            "ctx",
        )
    )
    return (
        loss,
        out_wide.reshape(seq_count, slice_len, D).astype(jnp.bfloat16),
        grad_inputs.reshape(seq_count, slice_len, D),
        grad_first.reshape(seq_count, slice_len, D - VW),
    ) + tuple(totals)


def solution(mesh):
    in_specs = (
        P("wsh", "ctx", None),
        P("wsh", "ctx", None),
        P("wsh", "ctx", None),
        P("wsh", None),
        P("wsh"),
        P("wsh"),
        P("wsh"),
        P("wsh", None),
        P("wsh"),
        P("wsh", None),
        P("wsh"),
        P("wsh"),
        P("wsh"),
        P("wsh", None),
        P("wsh"),
        P("wsh", None),
        P("wsh"),
    )
    out_specs = (
        P(),
        P("wsh", "ctx", None),
        P("wsh", "ctx", None),
        P("wsh", "ctx", None),
        P("wsh"),
        P("wsh"),
        P("wsh", None),
        P("wsh"),
        P("wsh", None),
        P("wsh"),
        P("wsh"),
        P("wsh"),
        P("wsh", None),
        P("wsh"),
        P("wsh", None),
        P("wsh"),
    )
    return jax.shard_map(local, mesh=mesh, in_specs=in_specs, out_specs=out_specs, check_vma=False)
```

profile of v0, /device:TPU:1, one launch (start us, length us, event | category | flops | bytes accessed | tf_op | source)
XLA Modules:
  0.0 1483.3 jit_solution(588035543067010941)
XLA Ops:
  47.5 7.2 all-gather.12.cloned.1.call-done
  75.4 207.3 %while.49 = (s32[]{:T(128)}, bf16[2,2,256,768]{2,3,1,0:T(8,128)(2,1)}, f32[2,256,12]{1,2,0:T(8,128)S(1)}, f32[2,256,12]{1,2,0:T(8,128)S(1)}, s32[2,256]{1,0:T(2,...) while((s32[]{:T(128)}, ...), condition=%wide.region_7.8_spmd.clone, body=%wide.region_4.7_spmd.clone.sunk | while | flops 214709264 | bytes 27203980 | solution.py:158
  82.1 15.2 %collective-permute-done = bf16[2,2,256,768]{2,3,1,0:T(8,128)(2,1)S(1)} collective-permute-done((bf16[2,2,256,768]{2,3,1,0:T(8,128)(2,1)}, bf16[2,2,256,768]{2,3,1,0:T(8,128)(2,1)S(1)}, u32[]{:S(2)}, u32[]{:S(2)}) %collective-permute-start) | collective-permute-done | bytes 1572896 | tf_op jit(solution)/shard_map/while/body/eval_jaxpr/ppermute | solution.py:20
  108.0 15.2 %collective-permute-done = bf16[2,2,256,768]{2,3,1,0:T(8,128)(2,1)S(1)} collective-permute-done((bf16[2,2,256,768]{2,3,1,0:T(8,128)(2,1)}, bf16[2,2,256,768]{2,3,1,0:T(8,128)(2,1)S(1)}, u32[]{:S(2)}, u32[]{:S(2)}) %collective-permute-start) | collective-permute-done | bytes 1572896 | tf_op jit(solution)/shard_map/while/body/eval_jaxpr/ppermute | solution.py:20
  133.9 15.2 %collective-permute-done = bf16[2,2,256,768]{2,3,1,0:T(8,128)(2,1)S(1)} collective-permute-done((bf16[2,2,256,768]{2,3,1,0:T(8,128)(2,1)}, bf16[2,2,256,768]{2,3,1,0:T(8,128)(2,1)S(1)}, u32[]{:S(2)}, u32[]{:S(2)}) %collective-permute-start) | collective-permute-done | bytes 1572896 | tf_op jit(solution)/shard_map/while/body/eval_jaxpr/ppermute | solution.py:20
  159.8 15.2 %collective-permute-done = bf16[2,2,256,768]{2,3,1,0:T(8,128)(2,1)S(1)} collective-permute-done((bf16[2,2,256,768]{2,3,1,0:T(8,128)(2,1)}, bf16[2,2,256,768]{2,3,1,0:T(8,128)(2,1)S(1)}, u32[]{:S(2)}, u32[]{:S(2)}) %collective-permute-start) | collective-permute-done | bytes 1572896 | tf_op jit(solution)/shard_map/while/body/eval_jaxpr/ppermute | solution.py:20
  185.7 15.2 %collective-permute-done = bf16[2,2,256,768]{2,3,1,0:T(8,128)(2,1)S(1)} collective-permute-done((bf16[2,2,256,768]{2,3,1,0:T(8,128)(2,1)}, bf16[2,2,256,768]{2,3,1,0:T(8,128)(2,1)S(1)}, u32[]{:S(2)}, u32[]{:S(2)}) %collective-permute-start) | collective-permute-done | bytes 1572896 | tf_op jit(solution)/shard_map/while/body/eval_jaxpr/ppermute | solution.py:20
  211.7 15.2 %collective-permute-done = bf16[2,2,256,768]{2,3,1,0:T(8,128)(2,1)S(1)} collective-permute-done((bf16[2,2,256,768]{2,3,1,0:T(8,128)(2,1)}, bf16[2,2,256,768]{2,3,1,0:T(8,128)(2,1)S(1)}, u32[]{:S(2)}, u32[]{:S(2)}) %collective-permute-start) | collective-permute-done | bytes 1572896 | tf_op jit(solution)/shard_map/while/body/eval_jaxpr/ppermute | solution.py:20
  237.6 15.2 %collective-permute-done = bf16[2,2,256,768]{2,3,1,0:T(8,128)(2,1)S(1)} collective-permute-done((bf16[2,2,256,768]{2,3,1,0:T(8,128)(2,1)}, bf16[2,2,256,768]{2,3,1,0:T(8,128)(2,1)S(1)}, u32[]{:S(2)}, u32[]{:S(2)}) %collective-permute-start) | collective-permute-done | bytes 1572896 | tf_op jit(solution)/shard_map/while/body/eval_jaxpr/ppermute | solution.py:20
  263.5 15.2 %collective-permute-done = bf16[2,2,256,768]{2,3,1,0:T(8,128)(2,1)S(1)} collective-permute-done((bf16[2,2,256,768]{2,3,1,0:T(8,128)(2,1)}, bf16[2,2,256,768]{2,3,1,0:T(8,128)(2,1)S(1)}, u32[]{:S(2)}, u32[]{:S(2)}) %collective-permute-start) | collective-permute-done | bytes 1572896 | tf_op jit(solution)/shard_map/while/body/eval_jaxpr/ppermute | solution.py:20
  282.7 5.9 convolution_bitcast_fusion
  288.6 238.6 %while.50 = (s32[]{:T(128)}, bf16[2,2,256,768]{2,3,1,0:T(8,128)(2,1)}, f32[2,256,12,64]{1,3,2,0:T(8,128)}, s32[2,256]{1,0:T(2,128)S(1)}, s32[8]{0:T(128)S(1)}, /...) while((s32[]{:T(128)}, ...), condition=%wide.region_9.10_spmd.clone, body=%wide.region_8.9_spmd.clone.sunk | while | flops 411698208 | bytes 19700108 | solution.py:178
  296.1 14.4 collective-permute-done.1
  311.8 5.5 bitcast_add_fusion.6
  325.9 14.4 collective-permute-done.1
  341.6 5.5 bitcast_add_fusion.6
  355.8 14.4 collective-permute-done.1
  371.4 5.5 bitcast_add_fusion.6
  385.6 14.4 collective-permute-done.1
  401.3 5.5 bitcast_add_fusion.6
  415.4 14.4 collective-permute-done.1
  431.1 5.5 bitcast_add_fusion.6
  445.2 14.4 collective-permute-done.1
  460.9 5.5 bitcast_add_fusion.6
  475.0 14.4 collective-permute-done.1
  490.7 5.5 bitcast_add_fusion.6
  504.8 14.4 collective-permute-done.1
  520.5 5.5 bitcast_add_fusion.6
  533.4 7.2 fusion.77
  540.7 8.0 add_add_fusion.3
  552.5 7.1 fusion.82
  570.5 4.6 fusion.69
  575.1 4.4 fusion.39
  584.7 338.0 %while.51 = (s32[]{:T(128)}, bf16[2,2,256,768]{2,3,1,0:T(8,128)(2,1)}, f32[2,256,768]{1,2,0:T(8,128)}, bf16[2,2,256,768]{2,3,1,0:T(8,128)(2,1)}, s32[2,256]{1,0:...) while((s32[]{:T(128)}, ...), condition=%wide.region_20.21_spmd.clone, body=%wide.region_19.20_spmd.clone.sunk | while | flops 1030620160 | bytes 86465048 | solution.py:277
  589.1 12.8 collective-permute-start.3
  616.3 7.3 collective-permute-done.3
  626.7 4.4 collective-permute-start.2
  631.1 13.6 collective-permute-start.3
  658.3 7.3 collective-permute-done.3
  668.7 4.4 collective-permute-start.2
  673.1 14.5 collective-permute-start.3
  700.3 7.3 collective-permute-done.3
  715.1 15.4 %collective-permute-start.3 = (bf16[2,2,256,768]{2,3,1,0:T(8,128)(2,1)}, bf16[2,2,256,768]{2,3,1,0:T(8,128)(2,1)}, u32[]{:S(2)}, u32[]{:S(2)}) collective-permute-start(bf16[2,2,256,768]{2,3,1,0:T(8,128)(2,1)} %get-tuple-element.1185), channel_id=1, source_target_pairs={{0,2},{2,4},{4,6},{6,8},{8,10},{10,12},{12,14},{14,16},{16,18},{18... | collective-permute-start | bytes 4718600 | tf_op jit(solution)/shard_map/while/body/eval_jaxpr/ppermute | solution.py:26
  742.4 7.2 collective-permute-done.3
  752.7 4.4 collective-permute-start.2
  757.1 16.3 %collective-permute-start.3 = (bf16[2,2,256,768]{2,3,1,0:T(8,128)(2,1)}, bf16[2,2,256,768]{2,3,1,0:T(8,128)(2,1)}, u32[]{:S(2)}, u32[]{:S(2)}) collective-permute-start(bf16[2,2,256,768]{2,3,1,0:T(8,128)(2,1)} %get-tuple-element.1185), channel_id=1, source_target_pairs={{0,2},{2,4},{4,6},{6,8},{8,10},{10,12},{12,14},{14,16},{16,18},{18... | collective-permute-start | bytes 4718600 | tf_op jit(solution)/shard_map/while/body/eval_jaxpr/ppermute | solution.py:26
  785.3 6.3 collective-permute-done.3
  794.7 4.4 collective-permute-start.2
  799.0 17.2 %collective-permute-start.3 = (bf16[2,2,256,768]{2,3,1,0:T(8,128)(2,1)}, bf16[2,2,256,768]{2,3,1,0:T(8,128)(2,1)}, u32[]{:S(2)}, u32[]{:S(2)}) collective-permute-start(bf16[2,2,256,768]{2,3,1,0:T(8,128)(2,1)} %get-tuple-element.1185), channel_id=1, source_target_pairs={{0,2},{2,4},{4,6},{6,8},{8,10},{10,12},{12,14},{14,16},{16,18},{18... | collective-permute-start | bytes 4718600 | tf_op jit(solution)/shard_map/while/body/eval_jaxpr/ppermute | solution.py:26
  828.1 5.7 collective-permute-done.3
  837.0 4.4 collective-permute-start.2
  841.3 17.7 %collective-permute-start.3 = (bf16[2,2,256,768]{2,3,1,0:T(8,128)(2,1)}, bf16[2,2,256,768]{2,3,1,0:T(8,128)(2,1)}, u32[]{:S(2)}, u32[]{:S(2)}) collective-permute-start(bf16[2,2,256,768]{2,3,1,0:T(8,128)(2,1)} %get-tuple-element.1185), channel_id=1, source_target_pairs={{0,2},{2,4},{4,6},{6,8},{8,10},{10,12},{12,14},{14,16},{16,18},{18... | collective-permute-start | bytes 4718600 | tf_op jit(solution)/shard_map/while/body/eval_jaxpr/ppermute | solution.py:26
  871.0 5.7 collective-permute-done.3
  879.8 4.4 collective-permute-start.2
  884.2 17.7 %collective-permute-start.3 = (bf16[2,2,256,768]{2,3,1,0:T(8,128)(2,1)}, bf16[2,2,256,768]{2,3,1,0:T(8,128)(2,1)}, u32[]{:S(2)}, u32[]{:S(2)}) collective-permute-start(bf16[2,2,256,768]{2,3,1,0:T(8,128)(2,1)} %get-tuple-element.1185), channel_id=1, source_target_pairs={{0,2},{2,4},{4,6},{6,8},{8,10},{10,12},{12,14},{14,16},{16,18},{18... | collective-permute-start | bytes 4718600 | tf_op jit(solution)/shard_map/while/body/eval_jaxpr/ppermute | solution.py:26
  913.9 5.7 collective-permute-done.3
  929.9 49.7 %collective-permute-done.4 = bf16[2,2,256,768]{3,2,1,0:T(8,128)(2,1)} collective-permute-done((bf16[2,2,256,768]{3,2,1,0:T(8,128)(2,1)}, bf16[2,2,256,768]{3,2,1,0:T(8,128)(2,1)}, u32[]{:S(2)}, u32[]{:S(2)}) %collective-permute-start.4) | collective-permute-done | bytes 1572896 | tf_op jit(solution)/shard_map/ppermute | solution.py:26
  986.8 7.4 convolution_convert_fusion.1
  995.4 9.1 convolution_convert_fusion
  1007.6 71.1 %all-reduce.9 = (f32[]{:T(128)}, f32[]{:T(128)}) all-reduce(f32[]{:T(128)} %get-tuple-element.783, f32[]{:T(128)} %fusion.68), channel_id=1, replica_groups=mesh['ctx'=16,'wsh'=2] {'ctx','wsh'}, use_global_device_ids=true, to_apply=%region_13.14 | all-reduce | flops 2 | bytes 16 | tf_op jit(solution)/shard_map/psum | solution.py:204
  1090.2 7.5 all-reduce.11
  1102.0 20.7 %reduce-scatter.9.cloned.1.call-done = bf16[384,3072]{1,0:T(8,128)(2,1)} async-done(((bf16[768,3072]{1,0:T(8,128)(2,1)}), bf16[384,3072]{1,0:T(8,128)(2,1)}) %reduce-scatter.9.cloned.1.call-update) | async-done | bytes 2359312 | tf_op jit(solution)/shard_map/reduce_scatter | solution.py:342
  1122.6 63.0 %reduce-scatter.11.cloned.1.call-done = bf16[1536,768]{1,0:T(8,128)(2,1)} async-done(((bf16[3072,768]{1,0:T(8,128)(2,1)}), bf16[1536,768]{1,0:T(8,128)(2,1)}) %reduce-scatter.11.cloned.1.call-update) | async-done | bytes 2359312 | tf_op jit(solution)/shard_map/reduce_scatter | solution.py:348
  1185.7 289.4 %all-reduce.13 = (f32[384]{0:T(512)}, f32[384]{0:T(512)}, f32[384,1920]{1,0:T(8,128)}, f32[576]{0:T(1024)}, f32[384,768]{1,0:T(8,128)}, /*index=5*/f32[384]{0:T(...) all-reduce(f32[384]{0:T(512)S(1)} %dynamic-slice_convert_fusion.7, ...), channel_id=1, replica_groups=mesh['ctx'=16,'wsh'=2] {'ctx'}, use_global_device_ids=true, to_apply=%region_25.26 | all-reduce | flops 3395904 | bytes 20384256 | tf_op jit(solution)/shard_map/psum | solution.py:356
  (675 shorter events, 396.9 us)
Async XLA Ops:
  7.2 47.5 %all-gather.12.cloned.1.call-start = ((), (), s32[]{:S(2)}) async-start(), calls=%async_computation.4 | async-start | bytes 4423680 | tf_op jit(solution)/shard_map/all_gather | solution.py:95
  8.0 13.2 copy-start.19
  8.0 522.6 %all-gather.14.cloned.1.call-start = ((), (), s32[]{:S(2)}) async-start(), calls=%async_computation.5 | async-start | bytes 1769472 | tf_op jit(solution)/shard_map/all_gather | solution.py:97
  8.7 12.7 copy-start.65
  8.7 16.2 %copy-start.66 = (bf16[384]{0:T(512)(128)(2,1)S(1)}, bf16[384]{0:T(512)(128)(2,1)}, u32[]{:S(2)}) copy-start(bf16[384]{0:T(512)(128)(2,1)} %param.28) | copy-start | bytes 2308
  8.7 19.8 %copy-start.5 = (bf16[2,256,768]{2,1,0:T(8,128)(2,1)S(1)}, bf16[2,256,768]{2,1,0:T(8,128)(2,1)}, u32[]{:S(2)}) copy-start(bf16[2,256,768]{2,1,0:T(8,128)(2,1)} %param.23) | copy-start | bytes 2359300
  8.8 524.6 %all-gather.16.cloned.1.call-start = ((), (), s32[]{:S(2)}) async-start(), calls=%async_computation.6 | async-start | bytes 7077888 | tf_op jit(solution)/shard_map/all_gather | solution.py:101
  9.5 19.7 %copy-start.67 = (bf16[384]{0:T(512)(128)(2,1)S(1)}, bf16[384]{0:T(512)(128)(2,1)}, u32[]{:S(2)}) copy-start(bf16[384]{0:T(512)(128)(2,1)} %param.39) | copy-start | bytes 2308
  9.5 23.8 %copy-start.68 = (bf16[384]{0:T(512)(128)(2,1)S(1)}, bf16[384]{0:T(512)(128)(2,1)}, u32[]{:S(2)}) copy-start(bf16[384]{0:T(512)(128)(2,1)} %param.35) | copy-start | bytes 2308
  9.5 27.9 %copy-start.69 = (bf16[384]{0:T(512)(128)(2,1)S(1)}, bf16[384]{0:T(512)(128)(2,1)}, u32[]{:S(2)}) copy-start(bf16[384]{0:T(512)(128)(2,1)} %param.34) | copy-start | bytes 2308
  9.5 31.5 %copy-start.59 = (bf16[1536]{0:T(1024)(128)(2,1)S(1)}, bf16[1536]{0:T(1024)(128)(2,1)}, u32[]{:S(2)}) copy-start(bf16[1536]{0:T(1024)(128)(2,1)} %param.37) | copy-start | bytes 9220
  9.5 531.1 %all-gather.18.cloned.1.call-start = ((), (), s32[]{:S(2)}) async-start(), calls=%async_computation.7 | async-start | bytes 7077888 | tf_op jit(solution)/shard_map/all_gather | solution.py:103
  10.1 1091.9 %reduce-scatter.7.cloned.1.call-start = ((), (), s32[]{:S(2)}) async-start(), calls=%async_computation.9 | async-start | bytes 1769472 | tf_op jit(solution)/shard_map/reduce_scatter | solution.py:330
  10.2 35.9 %copy-start.45 = (s32[256]{0:T(256)}, s32[256]{0:T(256)S(1)}, u32[]{:S(2)}) copy-start(s32[256]{0:T(256)S(1)} %get-tuple-element.803) | copy-start | bytes 3076
  28.5 29.8 %copy-start.37 = (f32[768]{0:T(1024)}, f32[768]{0:T(1024)S(1)}, u32[]{:S(2)}) copy-start(f32[768]{0:T(1024)S(1)} %reshape.645) | copy-start | bytes 9220
  29.1 11.9 copy-start.43
  29.1 29.2 %copy-start.39 = (f32[512]{0:T(512)}, f32[512]{0:T(512)S(1)}, u32[]{:S(2)}) copy-start(f32[512]{0:T(512)S(1)} %rsqrt.20) | copy-start | bytes 6148
  29.2 29.2 %copy-start.41 = (f32[1,2,2,128]{3,1,2,0:T(2,128)}, f32[1,2,2,128]{3,1,2,0:T(2,128)S(1)}, u32[]{:S(2)}) copy-start(f32[1,2,2,128]{3,1,2,0:T(2,128)S(1)} %copy.126) | copy-start | bytes 6148
  41.0 522.1 %copy-start.46 = (f32[768]{0:T(1024)}, f32[768]{0:T(1024)S(1)}, u32[]{:S(2)}) copy-start(f32[768]{0:T(1024)S(1)} %reshape.648) | copy-start | bytes 9220
  75.6 21.7 %collective-permute-start = (bf16[2,2,256,768]{2,3,1,0:T(8,128)(2,1)}, bf16[2,2,256,768]{2,3,1,0:T(8,128)(2,1)S(1)}, u32[]{:S(2)}, u32[]{:S(2)}) collective-permute-start(bf16[2,2,256,768]{2,3,1,0:T(8,128)(2,1)} %get-tuple-element.1078), channel_id=1, source_target_pairs={{0,2},{2,4},{4,6},{6,8},{8,10},{10,12},{12,14},{14,16},{16,18},{18... | collective-permute-start | bytes 4718600 | tf_op jit(solution)/shard_map/while/body/eval_jaxpr/ppermute | solution.py:20
  101.3 21.9 %collective-permute-start = (bf16[2,2,256,768]{2,3,1,0:T(8,128)(2,1)}, bf16[2,2,256,768]{2,3,1,0:T(8,128)(2,1)S(1)}, u32[]{:S(2)}, u32[]{:S(2)}) collective-permute-start(bf16[2,2,256,768]{2,3,1,0:T(8,128)(2,1)} %get-tuple-element.1078), channel_id=1, source_target_pairs={{0,2},{2,4},{4,6},{6,8},{8,10},{10,12},{12,14},{14,16},{16,18},{18... | collective-permute-start | bytes 4718600 | tf_op jit(solution)/shard_map/while/body/eval_jaxpr/ppermute | solution.py:20
  127.2 21.9 %collective-permute-start = (bf16[2,2,256,768]{2,3,1,0:T(8,128)(2,1)}, bf16[2,2,256,768]{2,3,1,0:T(8,128)(2,1)S(1)}, u32[]{:S(2)}, u32[]{:S(2)}) collective-permute-start(bf16[2,2,256,768]{2,3,1,0:T(8,128)(2,1)} %get-tuple-element.1078), channel_id=1, source_target_pairs={{0,2},{2,4},{4,6},{6,8},{8,10},{10,12},{12,14},{14,16},{16,18},{18... | collective-permute-start | bytes 4718600 | tf_op jit(solution)/shard_map/while/body/eval_jaxpr/ppermute | solution.py:20
  153.1 21.9 %collective-permute-start = (bf16[2,2,256,768]{2,3,1,0:T(8,128)(2,1)}, bf16[2,2,256,768]{2,3,1,0:T(8,128)(2,1)S(1)}, u32[]{:S(2)}, u32[]{:S(2)}) collective-permute-start(bf16[2,2,256,768]{2,3,1,0:T(8,128)(2,1)} %get-tuple-element.1078), channel_id=1, source_target_pairs={{0,2},{2,4},{4,6},{6,8},{8,10},{10,12},{12,14},{14,16},{16,18},{18... | collective-permute-start | bytes 4718600 | tf_op jit(solution)/shard_map/while/body/eval_jaxpr/ppermute | solution.py:20
  179.0 21.9 %collective-permute-start = (bf16[2,2,256,768]{2,3,1,0:T(8,128)(2,1)}, bf16[2,2,256,768]{2,3,1,0:T(8,128)(2,1)S(1)}, u32[]{:S(2)}, u32[]{:S(2)}) collective-permute-start(bf16[2,2,256,768]{2,3,1,0:T(8,128)(2,1)} %get-tuple-element.1078), channel_id=1, source_target_pairs={{0,2},{2,4},{4,6},{6,8},{8,10},{10,12},{12,14},{14,16},{16,18},{18... | collective-permute-start | bytes 4718600 | tf_op jit(solution)/shard_map/while/body/eval_jaxpr/ppermute | solution.py:20
  204.9 21.9 %collective-permute-start = (bf16[2,2,256,768]{2,3,1,0:T(8,128)(2,1)}, bf16[2,2,256,768]{2,3,1,0:T(8,128)(2,1)S(1)}, u32[]{:S(2)}, u32[]{:S(2)}) collective-permute-start(bf16[2,2,256,768]{2,3,1,0:T(8,128)(2,1)} %get-tuple-element.1078), channel_id=1, source_target_pairs={{0,2},{2,4},{4,6},{6,8},{8,10},{10,12},{12,14},{14,16},{16,18},{18... | collective-permute-start | bytes 4718600 | tf_op jit(solution)/shard_map/while/body/eval_jaxpr/ppermute | solution.py:20
  230.9 21.9 %collective-permute-start = (bf16[2,2,256,768]{2,3,1,0:T(8,128)(2,1)}, bf16[2,2,256,768]{2,3,1,0:T(8,128)(2,1)S(1)}, u32[]{:S(2)}, u32[]{:S(2)}) collective-permute-start(bf16[2,2,256,768]{2,3,1,0:T(8,128)(2,1)} %get-tuple-element.1078), channel_id=1, source_target_pairs={{0,2},{2,4},{4,6},{6,8},{8,10},{10,12},{12,14},{14,16},{16,18},{18... | collective-permute-start | bytes 4718600 | tf_op jit(solution)/shard_map/while/body/eval_jaxpr/ppermute | solution.py:20
  256.8 21.9 %collective-permute-start = (bf16[2,2,256,768]{2,3,1,0:T(8,128)(2,1)}, bf16[2,2,256,768]{2,3,1,0:T(8,128)(2,1)S(1)}, u32[]{:S(2)}, u32[]{:S(2)}) collective-permute-start(bf16[2,2,256,768]{2,3,1,0:T(8,128)(2,1)} %get-tuple-element.1078), channel_id=1, source_target_pairs={{0,2},{2,4},{4,6},{6,8},{8,10},{10,12},{12,14},{14,16},{16,18},{18... | collective-permute-start | bytes 4718600 | tf_op jit(solution)/shard_map/while/body/eval_jaxpr/ppermute | solution.py:20
  288.6 21.9 %collective-permute-start.1 = (bf16[2,2,256,768]{2,3,1,0:T(8,128)(2,1)}, bf16[2,2,256,768]{2,3,1,0:T(8,128)(2,1)S(1)}, u32[]{:S(2)}, u32[]{:S(2)}) collective-permute-start(bf16[2,2,256,768]{2,3,1,0:T(8,128)(2,1)} %get-tuple-element.1129), channel_id=1, source_target_pairs={{0,2},{2,4},{4,6},{6,8},{8,10},{10,12},{12,14},{14,16},{16,18},{18... | collective-permute-start | bytes 4718600 | tf_op jit(solution)/shard_map/while/body/eval_jaxpr/ppermute | solution.py:20
  318.4 21.9 %collective-permute-start.1 = (bf16[2,2,256,768]{2,3,1,0:T(8,128)(2,1)}, bf16[2,2,256,768]{2,3,1,0:T(8,128)(2,1)S(1)}, u32[]{:S(2)}, u32[]{:S(2)}) collective-permute-start(bf16[2,2,256,768]{2,3,1,0:T(8,128)(2,1)} %get-tuple-element.1129), channel_id=1, source_target_pairs={{0,2},{2,4},{4,6},{6,8},{8,10},{10,12},{12,14},{14,16},{16,18},{18... | collective-permute-start | bytes 4718600 | tf_op jit(solution)/shard_map/while/body/eval_jaxpr/ppermute | solution.py:20
  348.2 21.9 %collective-permute-start.1 = (bf16[2,2,256,768]{2,3,1,0:T(8,128)(2,1)}, bf16[2,2,256,768]{2,3,1,0:T(8,128)(2,1)S(1)}, u32[]{:S(2)}, u32[]{:S(2)}) collective-permute-start(bf16[2,2,256,768]{2,3,1,0:T(8,128)(2,1)} %get-tuple-element.1129), channel_id=1, source_target_pairs={{0,2},{2,4},{4,6},{6,8},{8,10},{10,12},{12,14},{14,16},{16,18},{18... | collective-permute-start | bytes 4718600 | tf_op jit(solution)/shard_map/while/body/eval_jaxpr/ppermute | solution.py:20
  378.1 21.9 %collective-permute-start.1 = (bf16[2,2,256,768]{2,3,1,0:T(8,128)(2,1)}, bf16[2,2,256,768]{2,3,1,0:T(8,128)(2,1)S(1)}, u32[]{:S(2)}, u32[]{:S(2)}) collective-permute-start(bf16[2,2,256,768]{2,3,1,0:T(8,128)(2,1)} %get-tuple-element.1129), channel_id=1, source_target_pairs={{0,2},{2,4},{4,6},{6,8},{8,10},{10,12},{12,14},{14,16},{16,18},{18... | collective-permute-start | bytes 4718600 | tf_op jit(solution)/shard_map/while/body/eval_jaxpr/ppermute | solution.py:20
  407.9 21.9 %collective-permute-start.1 = (bf16[2,2,256,768]{2,3,1,0:T(8,128)(2,1)}, bf16[2,2,256,768]{2,3,1,0:T(8,128)(2,1)S(1)}, u32[]{:S(2)}, u32[]{:S(2)}) collective-permute-start(bf16[2,2,256,768]{2,3,1,0:T(8,128)(2,1)} %get-tuple-element.1129), channel_id=1, source_target_pairs={{0,2},{2,4},{4,6},{6,8},{8,10},{10,12},{12,14},{14,16},{16,18},{18... | collective-permute-start | bytes 4718600 | tf_op jit(solution)/shard_map/while/body/eval_jaxpr/ppermute | solution.py:20
  437.7 21.9 %collective-permute-start.1 = (bf16[2,2,256,768]{2,3,1,0:T(8,128)(2,1)}, bf16[2,2,256,768]{2,3,1,0:T(8,128)(2,1)S(1)}, u32[]{:S(2)}, u32[]{:S(2)}) collective-permute-start(bf16[2,2,256,768]{2,3,1,0:T(8,128)(2,1)} %get-tuple-element.1129), channel_id=1, source_target_pairs={{0,2},{2,4},{4,6},{6,8},{8,10},{10,12},{12,14},{14,16},{16,18},{18... | collective-permute-start | bytes 4718600 | tf_op jit(solution)/shard_map/while/body/eval_jaxpr/ppermute | solution.py:20
  467.5 21.9 %collective-permute-start.1 = (bf16[2,2,256,768]{2,3,1,0:T(8,128)(2,1)}, bf16[2,2,256,768]{2,3,1,0:T(8,128)(2,1)S(1)}, u32[]{:S(2)}, u32[]{:S(2)}) collective-permute-start(bf16[2,2,256,768]{2,3,1,0:T(8,128)(2,1)} %get-tuple-element.1129), channel_id=1, source_target_pairs={{0,2},{2,4},{4,6},{6,8},{8,10},{10,12},{12,14},{14,16},{16,18},{18... | collective-permute-start | bytes 4718600 | tf_op jit(solution)/shard_map/while/body/eval_jaxpr/ppermute | solution.py:20
  497.3 21.9 %collective-permute-start.1 = (bf16[2,2,256,768]{2,3,1,0:T(8,128)(2,1)}, bf16[2,2,256,768]{2,3,1,0:T(8,128)(2,1)S(1)}, u32[]{:S(2)}, u32[]{:S(2)}) collective-permute-start(bf16[2,2,256,768]{2,3,1,0:T(8,128)(2,1)} %get-tuple-element.1129), channel_id=1, source_target_pairs={{0,2},{2,4},{4,6},{6,8},{8,10},{10,12},{12,14},{14,16},{16,18},{18... | collective-permute-start | bytes 4718600 | tf_op jit(solution)/shard_map/while/body/eval_jaxpr/ppermute | solution.py:20
  533.0 30.1 %copy-start.13 = (f32[512,768]{1,0:T(8,128)}, f32[512,768]{1,0:T(8,128)S(1)}, u32[]{:S(2)}) copy-start(f32[512,768]{1,0:T(8,128)S(1)} %get-tuple-element.800) | copy-start | bytes 4718596
  533.3 29.8 %copy-start.49 = (f32[512]{0:T(512)}, f32[512]{0:T(512)S(1)}, u32[]{:S(2)}) copy-start(f32[512]{0:T(512)S(1)} %fusion.64) | copy-start | bytes 6148
  540.7 10.0 copy-start.73
  549.6 14.2 copy-start.3
  584.8 22.0 %collective-permute-start.2 = (bf16[2,2,256,768]{2,3,1,0:T(8,128)(2,1)}, bf16[2,2,256,768]{2,3,1,0:T(8,128)(2,1)S(1)}, u32[]{:S(2)}, u32[]{:S(2)}) collective-permute-start(bf16[2,2,256,768]{2,3,1,0:T(8,128)(2,1)} %get-tuple-element.1183), channel_id=1, source_target_pairs={{0,2},{2,4},{4,6},{6,8},{8,10},{10,12},{12,14},{14,16},{16,18},{18... | collective-permute-start | bytes 4718600 | tf_op jit(solution)/shard_map/while/body/eval_jaxpr/ppermute | solution.py:20
  589.1 34.5 %collective-permute-start.3 = (bf16[2,2,256,768]{2,3,1,0:T(8,128)(2,1)}, bf16[2,2,256,768]{2,3,1,0:T(8,128)(2,1)}, u32[]{:S(2)}, u32[]{:S(2)}) collective-permute-start(bf16[2,2,256,768]{2,3,1,0:T(8,128)(2,1)} %get-tuple-element.1185), channel_id=1, source_target_pairs={{0,2},{2,4},{4,6},{6,8},{8,10},{10,12},{12,14},{14,16},{16,18},{18... | collective-permute-start | bytes 4718600 | tf_op jit(solution)/shard_map/while/body/eval_jaxpr/ppermute | solution.py:26
  626.7 22.0 %collective-permute-start.2 = (bf16[2,2,256,768]{2,3,1,0:T(8,128)(2,1)}, bf16[2,2,256,768]{2,3,1,0:T(8,128)(2,1)S(1)}, u32[]{:S(2)}, u32[]{:S(2)}) collective-permute-start(bf16[2,2,256,768]{2,3,1,0:T(8,128)(2,1)} %get-tuple-element.1183), channel_id=1, source_target_pairs={{0,2},{2,4},{4,6},{6,8},{8,10},{10,12},{12,14},{14,16},{16,18},{18... | collective-permute-start | bytes 4718600 | tf_op jit(solution)/shard_map/while/body/eval_jaxpr/ppermute | solution.py:20
  631.1 34.5 %collective-permute-start.3 = (bf16[2,2,256,768]{2,3,1,0:T(8,128)(2,1)}, bf16[2,2,256,768]{2,3,1,0:T(8,128)(2,1)}, u32[]{:S(2)}, u32[]{:S(2)}) collective-permute-start(bf16[2,2,256,768]{2,3,1,0:T(8,128)(2,1)} %get-tuple-element.1185), channel_id=1, source_target_pairs={{0,2},{2,4},{4,6},{6,8},{8,10},{10,12},{12,14},{14,16},{16,18},{18... | collective-permute-start | bytes 4718600 | tf_op jit(solution)/shard_map/while/body/eval_jaxpr/ppermute | solution.py:26
  668.7 22.0 %collective-permute-start.2 = (bf16[2,2,256,768]{2,3,1,0:T(8,128)(2,1)}, bf16[2,2,256,768]{2,3,1,0:T(8,128)(2,1)S(1)}, u32[]{:S(2)}, u32[]{:S(2)}) collective-permute-start(bf16[2,2,256,768]{2,3,1,0:T(8,128)(2,1)} %get-tuple-element.1183), channel_id=1, source_target_pairs={{0,2},{2,4},{4,6},{6,8},{8,10},{10,12},{12,14},{14,16},{16,18},{18... | collective-permute-start | bytes 4718600 | tf_op jit(solution)/shard_map/while/body/eval_jaxpr/ppermute | solution.py:20
  673.1 34.5 %collective-permute-start.3 = (bf16[2,2,256,768]{2,3,1,0:T(8,128)(2,1)}, bf16[2,2,256,768]{2,3,1,0:T(8,128)(2,1)}, u32[]{:S(2)}, u32[]{:S(2)}) collective-permute-start(bf16[2,2,256,768]{2,3,1,0:T(8,128)(2,1)} %get-tuple-element.1185), channel_id=1, source_target_pairs={{0,2},{2,4},{4,6},{6,8},{8,10},{10,12},{12,14},{14,16},{16,18},{18... | collective-permute-start | bytes 4718600 | tf_op jit(solution)/shard_map/while/body/eval_jaxpr/ppermute | solution.py:26
  710.7 22.2 %collective-permute-start.2 = (bf16[2,2,256,768]{2,3,1,0:T(8,128)(2,1)}, bf16[2,2,256,768]{2,3,1,0:T(8,128)(2,1)S(1)}, u32[]{:S(2)}, u32[]{:S(2)}) collective-permute-start(bf16[2,2,256,768]{2,3,1,0:T(8,128)(2,1)} %get-tuple-element.1183), channel_id=1, source_target_pairs={{0,2},{2,4},{4,6},{6,8},{8,10},{10,12},{12,14},{14,16},{16,18},{18... | collective-permute-start | bytes 4718600 | tf_op jit(solution)/shard_map/while/body/eval_jaxpr/ppermute | solution.py:20
  715.1 34.5 %collective-permute-start.3 = (bf16[2,2,256,768]{2,3,1,0:T(8,128)(2,1)}, bf16[2,2,256,768]{2,3,1,0:T(8,128)(2,1)}, u32[]{:S(2)}, u32[]{:S(2)}) collective-permute-start(bf16[2,2,256,768]{2,3,1,0:T(8,128)(2,1)} %get-tuple-element.1185), channel_id=1, source_target_pairs={{0,2},{2,4},{4,6},{6,8},{8,10},{10,12},{12,14},{14,16},{16,18},{18... | collective-permute-start | bytes 4718600 | tf_op jit(solution)/shard_map/while/body/eval_jaxpr/ppermute | solution.py:26
  752.7 23.1 %collective-permute-start.2 = (bf16[2,2,256,768]{2,3,1,0:T(8,128)(2,1)}, bf16[2,2,256,768]{2,3,1,0:T(8,128)(2,1)S(1)}, u32[]{:S(2)}, u32[]{:S(2)}) collective-permute-start(bf16[2,2,256,768]{2,3,1,0:T(8,128)(2,1)} %get-tuple-element.1183), channel_id=1, source_target_pairs={{0,2},{2,4},{4,6},{6,8},{8,10},{10,12},{12,14},{14,16},{16,18},{18... | collective-permute-start | bytes 4718600 | tf_op jit(solution)/shard_map/while/body/eval_jaxpr/ppermute | solution.py:20
  757.1 34.5 %collective-permute-start.3 = (bf16[2,2,256,768]{2,3,1,0:T(8,128)(2,1)}, bf16[2,2,256,768]{2,3,1,0:T(8,128)(2,1)}, u32[]{:S(2)}, u32[]{:S(2)}) collective-permute-start(bf16[2,2,256,768]{2,3,1,0:T(8,128)(2,1)} %get-tuple-element.1185), channel_id=1, source_target_pairs={{0,2},{2,4},{4,6},{6,8},{8,10},{10,12},{12,14},{14,16},{16,18},{18... | collective-permute-start | bytes 4718600 | tf_op jit(solution)/shard_map/while/body/eval_jaxpr/ppermute | solution.py:26
  794.7 24.0 %collective-permute-start.2 = (bf16[2,2,256,768]{2,3,1,0:T(8,128)(2,1)}, bf16[2,2,256,768]{2,3,1,0:T(8,128)(2,1)S(1)}, u32[]{:S(2)}, u32[]{:S(2)}) collective-permute-start(bf16[2,2,256,768]{2,3,1,0:T(8,128)(2,1)} %get-tuple-element.1183), channel_id=1, source_target_pairs={{0,2},{2,4},{4,6},{6,8},{8,10},{10,12},{12,14},{14,16},{16,18},{18... | collective-permute-start | bytes 4718600 | tf_op jit(solution)/shard_map/while/body/eval_jaxpr/ppermute | solution.py:20
  799.0 34.8 %collective-permute-start.3 = (bf16[2,2,256,768]{2,3,1,0:T(8,128)(2,1)}, bf16[2,2,256,768]{2,3,1,0:T(8,128)(2,1)}, u32[]{:S(2)}, u32[]{:S(2)}) collective-permute-start(bf16[2,2,256,768]{2,3,1,0:T(8,128)(2,1)} %get-tuple-element.1185), channel_id=1, source_target_pairs={{0,2},{2,4},{4,6},{6,8},{8,10},{10,12},{12,14},{14,16},{16,18},{18... | collective-permute-start | bytes 4718600 | tf_op jit(solution)/shard_map/while/body/eval_jaxpr/ppermute | solution.py:26
  837.0 24.5 %collective-permute-start.2 = (bf16[2,2,256,768]{2,3,1,0:T(8,128)(2,1)}, bf16[2,2,256,768]{2,3,1,0:T(8,128)(2,1)S(1)}, u32[]{:S(2)}, u32[]{:S(2)}) collective-permute-start(bf16[2,2,256,768]{2,3,1,0:T(8,128)(2,1)} %get-tuple-element.1183), channel_id=1, source_target_pairs={{0,2},{2,4},{4,6},{6,8},{8,10},{10,12},{12,14},{14,16},{16,18},{18... | collective-permute-start | bytes 4718600 | tf_op jit(solution)/shard_map/while/body/eval_jaxpr/ppermute | solution.py:20
  841.3 35.4 %collective-permute-start.3 = (bf16[2,2,256,768]{2,3,1,0:T(8,128)(2,1)}, bf16[2,2,256,768]{2,3,1,0:T(8,128)(2,1)}, u32[]{:S(2)}, u32[]{:S(2)}) collective-permute-start(bf16[2,2,256,768]{2,3,1,0:T(8,128)(2,1)} %get-tuple-element.1185), channel_id=1, source_target_pairs={{0,2},{2,4},{4,6},{6,8},{8,10},{10,12},{12,14},{14,16},{16,18},{18... | collective-permute-start | bytes 4718600 | tf_op jit(solution)/shard_map/while/body/eval_jaxpr/ppermute | solution.py:26
  879.8 24.5 %collective-permute-start.2 = (bf16[2,2,256,768]{2,3,1,0:T(8,128)(2,1)}, bf16[2,2,256,768]{2,3,1,0:T(8,128)(2,1)S(1)}, u32[]{:S(2)}, u32[]{:S(2)}) collective-permute-start(bf16[2,2,256,768]{2,3,1,0:T(8,128)(2,1)} %get-tuple-element.1183), channel_id=1, source_target_pairs={{0,2},{2,4},{4,6},{6,8},{8,10},{10,12},{12,14},{14,16},{16,18},{18... | collective-permute-start | bytes 4718600 | tf_op jit(solution)/shard_map/while/body/eval_jaxpr/ppermute | solution.py:20
  884.2 35.4 %collective-permute-start.3 = (bf16[2,2,256,768]{2,3,1,0:T(8,128)(2,1)}, bf16[2,2,256,768]{2,3,1,0:T(8,128)(2,1)}, u32[]{:S(2)}, u32[]{:S(2)}) collective-permute-start(bf16[2,2,256,768]{2,3,1,0:T(8,128)(2,1)} %get-tuple-element.1185), channel_id=1, source_target_pairs={{0,2},{2,4},{4,6},{6,8},{8,10},{10,12},{12,14},{14,16},{16,18},{18... | collective-permute-start | bytes 4718600 | tf_op jit(solution)/shard_map/while/body/eval_jaxpr/ppermute | solution.py:26
  925.4 54.2 %collective-permute-start.4 = (bf16[2,2,256,768]{3,2,1,0:T(8,128)(2,1)}, bf16[2,2,256,768]{3,2,1,0:T(8,128)(2,1)}, u32[]{:S(2)}, u32[]{:S(2)}) collective-permute-start(bf16[2,2,256,768]{3,2,1,0:T(8,128)(2,1)} %copy.117), channel_id=1, source_target_pairs={{0,16},{2,18},{4,20},{6,22},{8,24},{10,26},{12,28},{14,30},{16,0},... | collective-permute-start | bytes 4718600 | tf_op jit(solution)/shard_map/ppermute | solution.py:26
  929.5 172.4 %reduce-scatter.5.cloned.1.call-start = ((), (), s32[]{:S(2)}) async-start(), calls=%async_computation.8 | async-start | bytes 4423680 | tf_op jit(solution)/shard_map/reduce_scatter | solution.py:324
  929.9 52.8 %copy-start.24 = (bf16[512,768]{1,0:T(8,128)(2,1)S(1)}, bf16[512,768]{1,0:T(8,128)(2,1)}, u32[]{:S(2)}) copy-start(bf16[512,768]{1,0:T(8,128)(2,1)} %copy-done.23) | copy-start | bytes 2359300
  986.1 136.5 %reduce-scatter.9.cloned.1.call-start = ((), (), s32[]{:S(2)}) async-start(), calls=%async_computation.10 | async-start | bytes 7077888 | tf_op jit(solution)/shard_map/reduce_scatter | solution.py:342
  994.3 191.4 %reduce-scatter.11.cloned.1.call-start = ((), (), s32[]{:S(2)}) async-start(), calls=%async_computation.11 | async-start | bytes 7077888 | tf_op jit(solution)/shard_map/reduce_scatter | solution.py:348
  1004.5 79.7 %copy-start.6 = (bf16[2,256,768]{2,1,0:T(8,128)(2,1)S(1)}, bf16[2,256,768]{2,1,0:T(8,128)(2,1)}, u32[]{:S(2)}) copy-start(bf16[2,256,768]{2,1,0:T(8,128)(2,1)} %param.23) | copy-start | bytes 2359300
  1004.5 79.7 %copy-start.38 = (f32[768]{0:T(1024)S(1)}, f32[768]{0:T(1024)}, u32[]{:S(2)}) copy-start(f32[768]{0:T(1024)} %copy-done.37) | copy-start | bytes 9220
  1004.5 79.7 %copy-start.42 = (f32[1,2,2,128]{3,1,2,0:T(2,128)S(1)}, f32[1,2,2,128]{3,1,2,0:T(2,128)}, u32[]{:S(2)}) copy-start(f32[1,2,2,128]{3,1,2,0:T(2,128)} %copy-done.41) | copy-start | bytes 6148
  1088.2 10.0 copy-start.4
  (75 other events, 256.1 us)
Sparse Core Ops, SparseCore 0:
  9.6 45.1 all-gather.11
  56.3 22.8 all-gather.13
  80.6 62.6 all-gather.15
  144.7 62.6 all-gather.17
  929.7 82.9 reduce-scatter.6
  1015.4 43.1 reduce-scatter.4
  1061.5 61.1 reduce-scatter.8
  1125.6 59.9 reduce-scatter.10
where the time goes:
time: 1490 us; the launch traced here: 1480 us
  waiting for transfers between devices  438 us (29%)
  blocking collectives  397 us (27%)
  starting transfers between devices  231 us (16%)
  matrix products  189 us (13%)
  local copies, waits for them, and re-layouts  104 us (7%)
  other arithmetic  86 us (6%)
  between operations  20.4 us (1%)
  loops' own time  18.2 us (1%)
    psum x1, blocking collectives, local(): lax.psum((shares[0], shares[1], shares[2], shares[3], shares[4], shares[5...  289 us
    ppermute x24, waiting for transfers between devices, passed_along(): lax.ppermute(value, axis, [(source, source + steps) for source in range(i...  242 us
    ppermute x9, starting transfers between devices, from_behind(): return lax.ppermute(value, axis, pairs)  127 us
    ppermute x24, starting transfers between devices, passed_along(): lax.ppermute(value, axis, [(source, source + steps) for source in range(i...  103 us
    ppermute x9, waiting for transfers between devices, from_behind(): return lax.ppermute(value, axis, pairs)  102 us
    psum x1, blocking collectives, local(): lax.psum((jnp.sum(deviation * deviation), jnp.sum(valid_rows)), ('ctx', '...  71.1 us
    reduce_scatter x1, waiting for transfers between devices, local(): lax.psum_scatter(grads[10].astype(jnp.bfloat16), 'wsh', scatter_dimension...  63 us
    dot_general x9, matrix products, attend(): jnp.einsum('bqhk,bkhd->bqhd', probs, split_heads(block[1]), preferred_ele...  49.8 us
  transfers between devices with their start and end apart: 41, of which 31 were waited for; matrix products, arithmetic and copies ran while one was open for 20% of the time, Pallas kernels for 0%

commit v1 on v0

v1 whole, which is shorter than its diff:
```python
import functools

import jax
import jax.numpy as jnp
from jax import lax
from jax.experimental import pallas as pl
from jax.experimental.pallas import tpu as pltpu
from jax.sharding import PartitionSpec as P

D = 768
HEADS = 12
HEAD = 64
DOC_MAX = 2048
VW = 384

EPS = 1e-05
NEG = -1e30

CHIPS = 8
GROUP = 2 * CHIPS
SEQS = 2
PER_SEQ = CHIPS // SEQS
UNITS = SEQS * HEADS // CHIPS
R = UNITS * HEAD
MESH = pl.DeviceIdType.MESH
DMA = pltpu.SemaphoreType.DMA


def norm_layer(values, gain_vec, offset):
    average = jnp.mean(values, axis=-1, keepdims=True)
    centred = values - average
    variance = jnp.mean(centred * centred, axis=-1, keepdims=True)
    return centred * lax.rsqrt(variance + EPS) * gain_vec + offset


def smooth_gate(values):
    return jax.nn.gelu(values, approximate=True)


def where_am_i():
    index, wsh = lax.axis_index("ctx"), lax.axis_index("wsh")
    base = index // GROUP * GROUP
    chip, core = index % GROUP // 2, index % 2

    def same_core(other):
        return (base + 2 * other + core, wsh)

    return chip, core, same_core, (base + 2 * chip + 1 - core, wsh)


def greet(peers):
    barrier = pltpu.get_barrier_semaphore()
    for peer in peers:
        pl.semaphore_signal(barrier, inc=1, device_id=peer, device_id_type=MESH)
    pl.semaphore_wait(barrier, len(peers))


def remote(src, dst, send, recv, peer):
    return pltpu.make_async_remote_copy(
        src_ref=src, dst_ref=dst, send_sem=send, recv_sem=recv, device_id=peer, device_id_type=MESH
    )


def lanes_of(chip, width):
    return pl.ds(pl.multiple_of(chip // PER_SEQ * width, width), width)


def rows_of(chip, first):
    return pl.ds(pl.multiple_of(first + chip % PER_SEQ * R, R), R)


def scatter_kernel(src, q_all, kv_all, send, recv, fsend, frecv, own):
    chip, core, same_core, sibling = where_am_i()
    width = q_all.shape[2]
    greet([same_core((chip + i) % CHIPS) for i in range(1, CHIPS)] + [sibling])
    block = 2 * chip + core

    def pieces(target):
        lanes = lanes_of(target, width)
        return (
            (src.at[rows_of(target, D), lanes], kv_all.at[block, pl.ds(0, R)]),
            (src.at[rows_of(target, 2 * D), lanes], kv_all.at[block, pl.ds(R, R)]),
            (src.at[rows_of(target, 0), lanes], q_all.at[chip]),
        )

    copies = []
    for i in range(1, CHIPS):
        target = (chip + i) % CHIPS
        copies.append(
            [
                remote(a, b, send.at[n, i], recv.at[n, i], same_core(target))
                for n, (a, b) in enumerate(pieces(target))
            ]
        )
        for copy in copies[-1]:
            copy.start()
    local = [pltpu.make_async_copy(a, b, own.at[n]) for n, (a, b) in enumerate(pieces(chip))]
    for copy in local:
        copy.start()
    for copy in local:
        copy.wait()
    forwards = []
    for i in range(CHIPS):
        if i:
            copies[i - 1][0].wait_recv()
            copies[i - 1][1].wait_recv()
        came = 2 * ((chip + CHIPS - i) % CHIPS) + core
        forwards.append(remote(kv_all.at[came], kv_all.at[came], fsend.at[i], frecv.at[i], sibling))
        forwards[-1].start()
    for i in range(1, CHIPS):
        copies[i - 1][2].wait_recv()
    for batch in copies:
        for copy in batch:
            copy.wait_send()
    for copy in forwards:
        copy.wait()


def home_kernel(src, dst, send, recv, own):
    chip, core, same_core, sibling = where_am_i()
    width = src.shape[2]
    greet([same_core((chip + i) % CHIPS) for i in range(1, CHIPS)])
    place = dst.at[rows_of(chip, 0), lanes_of(chip, width)]
    copies = []
    for i in range(1, CHIPS):
        target = (chip + i) % CHIPS
        copies.append(remote(src.at[target], place, send.at[i], recv.at[i], same_core(target)))
        copies[-1].start()
    local = pltpu.make_async_copy(src.at[chip], place, own)
    local.start()
    local.wait()
    for copy in copies:
        copy.wait()


def away_kernel(src, dst, send, recv, own):
    chip, core, same_core, sibling = where_am_i()
    width = dst.shape[2]
    greet([same_core((chip + i) % CHIPS) for i in range(1, CHIPS)])
    copies = []
    for i in range(1, CHIPS):
        target = (chip + i) % CHIPS
        piece = src.at[rows_of(target, 0), lanes_of(target, width)]
        copies.append(remote(piece, dst.at[chip], send.at[i], recv.at[i], same_core(target)))
        copies[-1].start()
    local = pltpu.make_async_copy(
        src.at[rows_of(chip, 0), lanes_of(chip, width)], dst.at[chip], own
    )
    local.start()
    local.wait()
    for copy in copies:
        copy.wait()


def return_kernel(dq, dkv, dst, give, take, final, send, recv, fsend, frecv, own):
    chip, core, same_core, sibling = where_am_i()
    width = dq.shape[2]
    greet([same_core((chip + i) % CHIPS) for i in range(1, CHIPS)] + [sibling])
    lanes = lanes_of(chip, width)
    halves = []
    for i in range(CHIPS):
        target = (chip + i) % CHIPS
        give[target] = dkv[2 * target + 1 - core].astype(jnp.bfloat16)
        halves.append(
            remote(give.at[target], take.at[target], fsend.at[i], frecv.at[i], sibling)
        )
        halves[-1].start()
    copies = []
    for i in range(1, CHIPS):
        target = (chip + i) % CHIPS
        copies.append(
            remote(
                dq.at[target],
                dst.at[rows_of(chip, 0), lanes],
                send.at[0, i],
                recv.at[0, i],
                same_core(target),
            )
        )
        copies[-1].start()
    local = [pltpu.make_async_copy(dq.at[chip], dst.at[rows_of(chip, 0), lanes], own.at[0])]
    local[0].start()
    for i in list(range(1, CHIPS)) + [0]:
        target = (chip + i) % CHIPS
        halves[i].wait_recv()
        final[target] = (dkv[2 * target + core] + take[target].astype(jnp.float32)).astype(
            jnp.bfloat16
        )
        for n in (1, 2):
            piece = final.at[target, pl.ds((n - 1) * R, R)]
            place = dst.at[rows_of(chip, n * D), lanes]
            if i:
                copies.append(
                    remote(piece, place, send.at[n, i], recv.at[n, i], same_core(target))
                )
                copies[-1].start()
            else:
                local.append(pltpu.make_async_copy(piece, place, own.at[n]))
                local[-1].start()
    for copy in local:
        copy.wait()
    for copy in halves:
        copy.wait_send()
    for copy in copies:
        copy.wait()


ANY = pl.BlockSpec(memory_space=pl.ANY)
VMEM = pl.BlockSpec(memory_space=pltpu.VMEM)
SMEM = pl.BlockSpec(memory_space=pltpu.SMEM)


def comm_params(number):
    return pltpu.CompilerParams(
        collective_id=number, has_side_effects=True, vmem_limit_bytes=48 << 20
    )


def scatter_heads(src, width):
    return pl.pallas_call(
        scatter_kernel,
        name="scatter_heads",
        out_shape=(
            jax.ShapeDtypeStruct((CHIPS, R, width), jnp.bfloat16),
            jax.ShapeDtypeStruct((GROUP, 2 * R, width), jnp.bfloat16),
        ),
        in_specs=[ANY],
        out_specs=(ANY, ANY),
        scratch_shapes=[
            DMA((3, CHIPS)),
            DMA((3, CHIPS)),
            DMA((CHIPS,)),
            DMA((CHIPS,)),
            DMA((3,)),
        ],
        compiler_params=comm_params(0),
    )(src)


def send_home(src):
    width = src.shape[2]
    return pl.pallas_call(
        home_kernel,
        name="send_home",
        out_shape=jax.ShapeDtypeStruct((D, SEQS * width), jnp.bfloat16),
        in_specs=[ANY],
        out_specs=ANY,
        scratch_shapes=[DMA((CHIPS,)), DMA((CHIPS,)), DMA],
        compiler_params=comm_params(1),
    )(src)


def send_away(src, width):
    return pl.pallas_call(
        away_kernel,
        name="send_away",
        out_shape=jax.ShapeDtypeStruct((CHIPS, R, width), jnp.bfloat16),
        in_specs=[ANY],
        out_specs=ANY,
        scratch_shapes=[DMA((CHIPS,)), DMA((CHIPS,)), DMA],
        compiler_params=comm_params(2),
    )(src)


def return_heads(dq, dkv):
    width = dq.shape[2]
    pair = pltpu.VMEM((CHIPS, 2 * R, width), jnp.bfloat16)
    return pl.pallas_call(
        return_kernel,
        name="return_heads",
        out_shape=jax.ShapeDtypeStruct((3 * D, SEQS * width), jnp.bfloat16),
        in_specs=[ANY, VMEM],
        out_specs=ANY,
        scratch_shapes=[
            pair,
            pair,
            pair,
            DMA((3, CHIPS)),
            DMA((3, CHIPS)),
            DMA((CHIPS,)),
            DMA((CHIPS,)),
            DMA((3,)),
        ],
        compiler_params=comm_params(3),
    )(dq, dkv)


def over_rows(left, right):
    return lax.dot_general(
        left, right, (((0,), (0,)), ((), ())), preferred_element_type=jnp.float32
    )


def over_lanes(left, right):
    return lax.dot_general(
        left, right, (((1,), (1,)), ((), ())), preferred_element_type=jnp.float32
    )


def head_rows(h, first=0):
    return slice(first + h * HEAD, first + (h + 1) * HEAD)


def forward_kernel(halo, info, q, kv, lo, out_wide, out_low, logs, top, total, accum):
    width = q.shape[2]
    core, length = info[CHIPS], info[CHIPS + 1]
    rows = lax.broadcasted_iota(jnp.int32, (width, width), 0)
    columns = lax.broadcasted_iota(jnp.int32, (1, width), 1)

    def one_query_block(j, unused):
        own = halo + 2 * j + core
        position = own * width + columns
        first = lo[j, 0:1, :]
        last = jnp.minimum(position, length - 1)

        diag = rows + own * width
        allowed = ((diag >= first) & (diag <= last)) | (diag == position)
        for h in range(UNITS):
            scores = over_rows(kv[own, head_rows(h), :], q[j, head_rows(h), :])
            scores = jnp.where(allowed, scores, NEG)
            peak = jnp.max(scores, axis=0, keepdims=True)
            expo = jnp.exp(scores - peak)
            top[h : h + 1, :] = peak
            total[h : h + 1, :] = jnp.sum(expo, axis=0, keepdims=True)
            accum[head_rows(h), :] = jnp.dot(
                kv[own, head_rows(h, R), :],
                expo.astype(jnp.bfloat16),
                preferred_element_type=jnp.float32,
            )

        def one_key_block(kb, unused):
            at = rows + kb * width
            allowed = (at >= first) & (at <= last)
            for h in range(UNITS):
                scores = over_rows(kv[kb, head_rows(h), :], q[j, head_rows(h), :])
                scores = jnp.where(allowed, scores, NEG)
                before = top[h : h + 1, :]
                peak = jnp.maximum(before, jnp.max(scores, axis=0, keepdims=True))
                expo = jnp.exp(scores - peak)
                shrink = jnp.exp(before - peak)
                top[h : h + 1, :] = peak
                total[h : h + 1, :] = total[h : h + 1, :] * shrink + jnp.sum(
                    expo, axis=0, keepdims=True
                )
                accum[head_rows(h), :] = accum[head_rows(h), :] * shrink + jnp.dot(
                    kv[kb, head_rows(h, R), :],
                    expo.astype(jnp.bfloat16),
                    preferred_element_type=jnp.float32,
                )
            return unused

        stop = jnp.minimum(own, (length + width - 1) // width)
        lax.fori_loop(info[j], stop, one_key_block, 0)
        for h in range(UNITS):
            result = accum[head_rows(h), :] / total[h : h + 1, :]
            out_wide[j, head_rows(h), :] = result
            out_low[j, head_rows(h), :] = result.astype(jnp.bfloat16)
            logs[j, h : h + 1, :] = top[h : h + 1, :] + jnp.log(total[h : h + 1, :])
        return unused

    lax.fori_loop(0, CHIPS, one_query_block, 0)


def attention_forward(info, q, kv, lo, halo):
    width = q.shape[2]
    return pl.pallas_call(
        functools.partial(forward_kernel, halo),
        name="attention_forward",
        out_shape=(
            jax.ShapeDtypeStruct((CHIPS, R, width), jnp.float32),
            jax.ShapeDtypeStruct((CHIPS, R, width), jnp.bfloat16),
            jax.ShapeDtypeStruct((CHIPS, 8, width), jnp.float32),
        ),
        in_specs=[SMEM, VMEM, VMEM, VMEM],
        out_specs=(VMEM, VMEM, VMEM),
        scratch_shapes=[
            pltpu.VMEM((8, width), jnp.float32),
            pltpu.VMEM((8, width), jnp.float32),
            pltpu.VMEM((R, width), jnp.float32),
        ],
        compiler_params=pltpu.CompilerParams(vmem_limit_bytes=48 << 20),
    )(info, q, kv, lo)


def backward_kernel(halo, info, q, kv, lo, grad, wide, logs, dq, dkv, query_acc, deltas):
    width = q.shape[2]
    core, length = info[CHIPS], info[CHIPS + 1]
    rows = lax.broadcasted_iota(jnp.int32, (width, width), 0)
    columns = lax.broadcasted_iota(jnp.int32, (1, width), 1)
    dkv[...] = jnp.zeros_like(dkv)

    def one_query_block(j, unused):
        own = halo + 2 * j + core
        position = own * width + columns
        first = lo[j, 0:1, :]
        last = jnp.minimum(position, length - 1)
        for h in range(UNITS):
            deltas[h : h + 1, :] = jnp.sum(
                grad[j, head_rows(h), :].astype(jnp.float32) * wide[j, head_rows(h), :],
                axis=0,
                keepdims=True,
            )
        query_acc[...] = jnp.zeros_like(query_acc)

        def block(kb, allowed):
            for h in range(UNITS):
                key, value = kv[kb, head_rows(h), :], kv[kb, head_rows(h, R), :]
                query, wanted = q[j, head_rows(h), :], grad[j, head_rows(h), :]
                scores = over_rows(key, query)
                probs = jnp.where(allowed, jnp.exp(scores - logs[j, h : h + 1, :]), 0.0)
                grad_probs = over_rows(value, wanted)
                grad_scores = (probs * (grad_probs - deltas[h : h + 1, :])).astype(jnp.bfloat16)
                dkv[kb, head_rows(h, R), :] += over_lanes(wanted, probs.astype(jnp.bfloat16))
                dkv[kb, head_rows(h), :] += over_lanes(query, grad_scores)
                query_acc[head_rows(h), :] += jnp.dot(
                    key, grad_scores, preferred_element_type=jnp.float32
                )

        diag = rows + own * width
        block(own, ((diag >= first) & (diag <= last)) | (diag == position))

        def one_key_block(kb, unused):
            at = rows + kb * width
            block(kb, (at >= first) & (at <= last))
            return unused

        stop = jnp.minimum(own, (length + width - 1) // width)
        lax.fori_loop(info[j], stop, one_key_block, 0)
        dq[j] = (query_acc[...] * HEAD ** (-0.5)).astype(jnp.bfloat16)
        return unused

    lax.fori_loop(0, CHIPS, one_query_block, 0)


def attention_backward(info, q, kv, lo, grad, wide, logs, halo):
    width = q.shape[2]
    return pl.pallas_call(
        functools.partial(backward_kernel, halo),
        name="attention_backward",
        out_shape=(
            jax.ShapeDtypeStruct((CHIPS, R, width), jnp.bfloat16),
            jax.ShapeDtypeStruct((halo + GROUP, 2 * R, width), jnp.float32),
        ),
        in_specs=[SMEM] + [VMEM] * 6,
        out_specs=(VMEM, VMEM),
        scratch_shapes=[
            pltpu.VMEM((R, width), jnp.float32),
            pltpu.VMEM((8, width), jnp.float32),
        ],
        compiler_params=pltpu.CompilerParams(vmem_limit_bytes=56 << 20),
    )(info, q, kv, lo, grad, wide, logs)


def local(
    tokens,
    first_values,
    teacher,
    segment_ids,
    lengths,
    ln1_gain,
    ln1_bias,
    w_qkv,
    qv_bias,
    w_out,
    b_out,
    ln2_gain,
    ln2_bias,
    w_fc,
    b_fc,
    w_proj,
    b_proj,
):
    seq_count, width = tokens.shape[0], tokens.shape[1]
    row_count = seq_count * width
    ctx_size = lax.axis_size("ctx")
    ctx_index = lax.axis_index("ctx")
    groups = ctx_size // GROUP
    halo = pl.cdiv(DOC_MAX - 1, width) if groups > 1 else 0
    assert seq_count == SEQS and ctx_size % GROUP == 0 and halo <= GROUP
    chip, core = ctx_index % GROUP // 2, ctx_index % 2
    (
        norm1_gain,
        norm1_shift,
        qkv_weight,
        qv_shift,
        out_weight,
        out_shift,
        norm2_gain,
        norm2_shift,
        fc_weight,
        fc_shift,
        proj_weight,
        proj_shift,
    ) = (
        lax.all_gather(part, "wsh", axis=0, tiled=True)
        for part in (
            ln1_gain,
            ln1_bias,
            w_qkv,
            qv_bias,
            w_out,
            b_out,
            ln2_gain,
            ln2_bias,
            w_fc,
            b_fc,
            w_proj,
            b_proj,
        )
    )
    query_pos = ctx_index * width + jnp.arange(width, dtype=jnp.int32)

    window = (halo + GROUP) * width
    start = ctx_index // GROUP * GROUP * width - halo * width
    ids = lax.dynamic_index_in_dim(segment_ids, chip // PER_SEQ, 0, keepdims=False)
    if halo:
        ids = jnp.concatenate([jnp.full((halo * width,), -1, jnp.int32), ids])
    ids = lax.dynamic_slice_in_dim(ids, start + halo * width, window, 0)
    mine = lax.dynamic_index_in_dim(
        ids[halo * width :].reshape(CHIPS, 2, width), core, 1, keepdims=False
    )
    lo = jnp.sum((ids[None, None, :] < mine[:, :, None]).astype(jnp.int32), axis=-1)
    length = lax.dynamic_index_in_dim(lengths, chip // PER_SEQ, 0, keepdims=False) - start
    info = jnp.concatenate([lo[:, 0] // width, jnp.stack([core, length])]).astype(jnp.int32)
    lo = jnp.broadcast_to(lo[:, None, :], (CHIPS, 8, width))

    inputs = tokens.reshape(row_count, D).astype(jnp.float32)
    normed1, norm1_back = jax.vjp(
        norm_layer, inputs, norm1_gain.astype(jnp.float32), norm1_shift.astype(jnp.float32)
    )
    normed1_low = normed1.astype(jnp.bfloat16)
    projected = lax.dot_general(
        qkv_weight, normed1_low, (((0,), (1,)), ((), ())), preferred_element_type=jnp.float32
    )
    shift_wide = qv_shift.astype(jnp.float32)[:, None]
    sent = jnp.concatenate(
        [
            (projected[:D] + shift_wide[:D]).astype(jnp.bfloat16) * HEAD ** (-0.5),
            projected[D : 2 * D].astype(jnp.bfloat16),
            (projected[2 * D :] + shift_wide[D:]).astype(jnp.bfloat16),
            first_values.reshape(row_count, D - VW).T,
        ],
        axis=0,
    )
    q_all, kv_all = scatter_heads(sent, width)
    if halo:
        ahead = [(i, i + GROUP) for i in range(ctx_size - GROUP)]
        kv_all = jnp.concatenate(
            [lax.ppermute(kv_all[GROUP - halo :], "ctx", ahead), kv_all], axis=0
        )
    out_wide, out_low, logs = attention_forward(info, q_all, kv_all, lo, halo)
    attended = send_home(out_low)
    resid = inputs + over_rows(attended, out_weight) + out_shift.astype(jnp.float32)
    normed2, norm2_back = jax.vjp(
        norm_layer, resid, norm2_gain.astype(jnp.float32), norm2_shift.astype(jnp.float32)
    )
    normed2_low = normed2.astype(jnp.bfloat16)
    pre_act = jnp.dot(normed2_low, fc_weight, preferred_element_type=jnp.float32) + fc_shift.astype(
        jnp.float32
    )
    activ, gelu_back = jax.vjp(smooth_gate, pre_act)
    activ_low = activ.astype(jnp.bfloat16)
    result = (
        resid
        + jnp.dot(activ_low, proj_weight, preferred_element_type=jnp.float32)
        + proj_shift.astype(jnp.float32)
    )
    valid_rows = (query_pos[None, :] < lengths[:, None]).astype(jnp.float32)
    deviation = (
        result.reshape(seq_count, width, D) - teacher.astype(jnp.float32)
    ) * valid_rows[:, :, None]
    squares, valid_count = lax.psum(
        (jnp.sum(deviation * deviation), jnp.sum(valid_rows)), ("ctx", "wsh")
    )
    loss = squares / (valid_count * D)
    grad_output = deviation.reshape(row_count, D)
    grad_mixed = grad_output.astype(jnp.bfloat16)
    grad_proj_w = over_rows(activ_low, grad_mixed)
    grad_proj_b = jnp.sum(grad_mixed.astype(jnp.float32), axis=0)
    grad_activ = over_lanes(grad_mixed, proj_weight)
    grad_pre = gelu_back(grad_activ)[0].astype(jnp.bfloat16)
    grad_fc_w = over_rows(normed2_low, grad_pre)
    grad_fc_b = jnp.sum(grad_pre.astype(jnp.float32), axis=0)
    grad_normed2 = over_lanes(grad_pre, fc_weight)
    grad_resid_norm, grad_g2, grad_b2 = norm2_back(grad_normed2)
    grad_resid = grad_output + grad_resid_norm
    grad_branch = grad_resid.astype(jnp.bfloat16)
    grad_out_w = jnp.dot(attended, grad_branch, preferred_element_type=jnp.float32)
    grad_out_b = jnp.sum(grad_branch.astype(jnp.float32), axis=0)
    grad_attended = over_lanes(out_weight, grad_branch).astype(jnp.bfloat16)
    grad_all = send_away(grad_attended, width)
    dq, dkv = attention_backward(info, q_all, kv_all, lo, grad_all, out_wide, logs, halo)
    if halo:
        behind = [(i + GROUP, i) for i in range(ctx_size - GROUP)]
        over = lax.ppermute(dkv[:halo].astype(jnp.bfloat16), "ctx", behind)
        dkv = dkv[halo:].at[GROUP - halo :].add(over.astype(jnp.float32))
    grads_t = return_heads(dq, dkv)
    grad_projected = grads_t[: 2 * D + VW]
    grad_first = grads_t[2 * D + VW :].T.astype(jnp.float32)
    grad_qkv_w = lax.dot_general(
        normed1_low, grad_projected, (((0,), (1,)), ((), ())), preferred_element_type=jnp.float32
    )
    grad_sums = jnp.sum(grad_projected.astype(jnp.float32), axis=1)
    grad_qv_b = jnp.concatenate([grad_sums[:D], grad_sums[2 * D :]])
    grad_normed1 = lax.dot_general(
        grad_projected, qkv_weight, (((0,), (1,)), ((), ())), preferred_element_type=jnp.float32
    )
    grad_input_norm, grad_g1, grad_b1 = norm1_back(grad_normed1)
    grad_inputs = grad_resid + grad_input_norm
    grads = (
        grad_g1,
        grad_b1,
        grad_qkv_w,
        grad_qv_b,
        grad_out_w,
        grad_out_b,
        grad_g2,
        grad_b2,
        grad_fc_w,
        grad_fc_b,
        grad_proj_w,
        grad_proj_b,
    )
    shares = tuple(
        lax.psum_scatter(
            part.astype(jnp.bfloat16), "wsh", scatter_dimension=0, tiled=True
        ).astype(jnp.float32)
        for part in grads
    )
    totals = tuple(lax.psum(shares, "ctx"))
    return (
        loss,
        result.reshape(seq_count, width, D).astype(jnp.bfloat16),
        grad_inputs.reshape(seq_count, width, D),
        grad_first.reshape(seq_count, width, D - VW),
    ) + totals


def solution(mesh):
    whole, rows, vector = P("wsh", "ctx", None), P("wsh", None), P("wsh")
    in_specs = (whole, whole, whole, rows, vector) + (
        vector,
        vector,
        rows,
        vector,
        rows,
        vector,
        vector,
        vector,
        rows,
        vector,
        rows,
        vector,
    )
    out_specs = (P(), whole, whole, whole) + in_specs[5:]
    return jax.shard_map(local, mesh=mesh, in_specs=in_specs, out_specs=out_specs, check_vma=False)
```

time: 1490 us -> 831 us (0.56)
  waiting for transfers between devices: 438 us -> 125 us
  starting transfers between devices: 231 us -> 0.57 us
  Pallas kernels: 0 us -> 211 us
  matrix products: 189 us -> 57.9 us
  local copies, waits for them, and re-layouts: 104 us -> 13.9 us
  other arithmetic: 86 us -> 16.8 us
  blocking collectives: 397 us -> 376 us
  loops' own time: 18.2 us -> 0 us
    ppermute x33 -> x0, waiting for transfers between devices: 345 us -> none  [the longest x24 242 us: passed_along(): lax.ppermute(value, axis, [(source, source + steps) for source in range(i...]
    ppermute x33 -> x0, starting transfers between devices: 230 us -> none  [the longest x9 127 us: from_behind(): return lax.ppermute(value, axis, pairs)]
    pallas_call x0 -> x6, Pallas kernels: none -> 211 us  [the longest x1 52.5 us: return_heads(): pl.pallas_call(return_kernel, name='return_heads', out_shape=jax.ShapeDty...]
    dot_general x72 -> x10, matrix products: 173 us -> 43 us  [the longest x3 18.5 us: over_rows(): lax.dot_general(left, right, (((0,), (0,)), ((), ())), preferred_element_...]
    while x82 -> x0, local copies, waits for them, and re-layouts: 37.2 us -> none
    all_gather x4, waiting for transfers between devices: 7.25 us -> 37.9 us  [local(): lax.all_gather(part, 'wsh', axis=0, tiled=True)]
    dynamic_slice x49 -> x4, local copies, waits for them, and re-layouts: 31.4 us -> 1.81 us  [the longest x2 1.21 us: local(): lax.dynamic_index_in_dim(segment_ids, chip // PER_SEQ, 0, keepdims=False)]
    add x76 -> x1, other arithmetic: 27.8 us -> 0.01 us  [local(): query_pos = ctx_index * width + jnp.arange(width, dtype=jnp.int32)]
  transfers between devices with their start and end apart: 41 -> 8, of which waited for: 31 -> 4; matrix products, arithmetic and copies ran while one was open for 20% -> 7% of each run, Pallas kernels for 0% -> 26%
where the time goes in v1:
time: 831 us; the launch traced here: 823 us
  blocking collectives  376 us (45%)
  Pallas kernels  211 us (25%)
  waiting for transfers between devices  125 us (15%)
  matrix products  57.9 us (7%)
  between operations  21.1 us (3%)
  other arithmetic  16.8 us (2%)
  local copies, waits for them, and re-layouts  13.9 us (2%)
    psum x1, blocking collectives, local(): totals = tuple(lax.psum(shares, 'ctx'))  289 us
    reduce_scatter x4, waiting for transfers between devices, local(): lax.psum_scatter(part.astype(jnp.bfloat16), 'wsh', scatter_dimension=0, t...  84.8 us
    pallas_call x1, Pallas kernels, return_heads(): pl.pallas_call(return_kernel, name='return_heads', out_shape=jax.ShapeDty...  52.5 us
    psum x1, blocking collectives, local(): lax.psum((jnp.sum(deviation * deviation), jnp.sum(valid_rows)), ('ctx', '...  50.6 us
    pallas_call x1, Pallas kernels, scatter_heads(): pl.pallas_call(scatter_kernel, name='scatter_heads', out_shape=(jax.Shape...  40.9 us
    all_gather x4, waiting for transfers between devices, local(): lax.all_gather(part, 'wsh', axis=0, tiled=True)  37.9 us
    pallas_call x1, Pallas kernels, attention_backward(): pl.pallas_call(functools.partial(backward_kernel, halo), name='attention_...  37 us
    pallas_call x1, Pallas kernels, attention_forward(): pl.pallas_call(functools.partial(forward_kernel, halo), name='attention_f...  32.3 us
  transfers between devices with their start and end apart: 8, of which 4 were waited for; matrix products, arithmetic and copies ran while one was open for 7% of the time, Pallas kernels for 26%

profile of v1, /device:TPU:1, one launch (start us, length us, event | category | flops | bytes accessed | tf_op | source)
XLA Modules:
  0.0 822.9 jit_solution(8691836409885813882)
XLA Ops:
  7.2 0.7 all-gather.12.cloned.1.call-update
  8.0 0.7 all-gather.14.cloned.1.call-update
  8.8 0.7 all-gather.16.cloned.1.call-update
  9.5 0.5 all-gather.18.cloned.1.call-update
  10.2 0.6 fusion.39
  11.8 4.3 all-reduce
  16.1 3.2 all-gather.2
  19.4 0.6 dynamic_slice.15
  19.9 0.5 broadcast.204
  20.5 0.7 fusion.38
  21.5 3.5 all-gather.1
  25.0 3.5 all-gather
  28.8 0.4 fusion.18
  29.2 3.5 all-gather.6
  32.8 3.5 all-gather.4
  36.3 3.5 all-gather.3
  39.9 3.6 all-gather.5
  44.2 3.4 convert_reduce_fusion
  47.9 0.4 fusion.14
  48.3 6.5 all-gather.12.cloned.1.call-done
  54.7 3.6 convolution_bitcast_fusion
  58.9 40.9 %scatter_heads.1 = (bf16[8,192,256]{2,1,0:T(8,128)(2,1)S(1)}, bf16[16,384,256]{2,1,0:T(8,128)(2,1)}) custom-call(bf16[2304,512]{1,0:T(8,128)(2,1)S(1)} %pad_maximum_fusion.src), custom_call_target="tpu_custom_call" | custom-call | tf_op jit(solution)/shard_map/scatter_heads/pallas_call | solution.py:220
  99.8 32.3 %attention_forward.1 = (f32[8,192,256]{2,1,0:T(8,128)S(1)}, bf16[8,192,256]{2,1,0:T(8,128)(2,1)S(1)}, f32[8,8,256]{2,1,0:T(8,128)S(1)}) custom-call(s32[10]{0:T(128)S(1)} %pad_add_fusion.info, bf16[8,192,256]{2,1,0:T(8,128)(2,1)S(1)} %get-tuple-element.23.q, bf16[16,384,256]{2,1,0:T(8,128)(2,1)} %get-tuple-element.24.kv, s32[8,8,256]{2,1,0:T(8,128)S(1)} %broadcast_in_dim.10.lo), custom_call_target="tpu_custom_call" | custom-call | tf_op jit(solution)/shard_map/attention_forward/pallas_call | solution.py:366
  132.2 1.1 copy-done.2
  133.3 0.6 copy-done.5
  133.9 32.2 %send_home.1 = bf16[768,512]{1,0:T(8,128)(2,1)S(1)} custom-call(bf16[8,192,256]{2,1,0:T(8,128)(2,1)S(1)} %get-tuple-element.25.src), custom_call_target="tpu_custom_call" | custom-call | tf_op jit(solution)/shard_map/send_home/pallas_call | solution.py:242
  166.2 2.2 fusion.40
  168.4 0.3 multiply_reduce_fusion.3
  168.7 7.3 fusion.31
  176.0 31.4 %all-gather.18.cloned.1.call-done = bf16[3072,768]{1,0:T(8,128)(2,1)} async-done(((bf16[1536,768]{1,0:T(8,128)(2,1)}), bf16[3072,768]{1,0:T(8,128)(2,1)}) %all-gather.18.cloned.1.call-update) | async-done | bytes 4718608 | tf_op jit(solution)/shard_map/all_gather | solution.py:495
  207.4 7.6 add_add_fusion.3
  215.0 0.3 convert_reduce_fusion.2
  215.3 0.8 copy-done.12
  216.2 1.0 bitcast_convert_fusion
  217.2 1.6 copy-done.31
  218.8 6.8 fusion.33
  225.6 3.0 multiply_reduce_fusion
  228.6 0.6 fusion.37
  229.6 0.9 copy-done.10
  230.5 1.8 convolution_convert_fusion.3
  232.3 2.1 fusion.23.src
  234.4 16.2 %send_away.1.grad = bf16[8,192,256]{2,1,0:T(8,128)(2,1)S(1)} custom-call(bf16[768,512]{1,0:T(8,128)(2,1)S(1)} %fusion.23.src), custom_call_target="tpu_custom_call" | custom-call | tf_op jit(solution)/shard_map/send_away/pallas_call | solution.py:254
  250.7 0.9 copy-done
  251.5 37.0 %attention_backward.1 = (bf16[8,192,256]{2,1,0:T(8,128)(2,1)}, f32[16,384,256]{2,1,0:T(8,128)}) custom-call(s32[10]{0:T(128)} %copy-done.6, bf16[8,192,256]{2,1,0:T(8,128)(2,1)} %copy-done.1, bf16[16,384,256]{2,1,0:T(8,128)(2,1)} %get-tuple-element.24.kv, s32[8,8,256]{2,1,0:T(8,128)} %copy-done.4, bf16[8,192,256]{2,1,0:T(8,128)(2,1)} %copy-done, ...), custom_call_target="tpu_custom_call" | custom-call | tf_op jit(solution)/shard_map/attention_backward/pallas_call | solution.py:437
  288.6 1.1 copy-done.3
  289.7 52.5 %return_heads.1 = bf16[2304,512]{1,0:T(8,128)(2,1)S(1)} custom-call(bf16[8,192,256]{2,1,0:T(8,128)(2,1)S(1)} %copy-done.3, f32[16,384,256]{2,1,0:T(8,128)} %get-tuple-element.29.dkv), custom_call_target="tpu_custom_call" | custom-call | tf_op jit(solution)/shard_map/return_heads/pallas_call | solution.py:268
  342.3 3.4 convolution_convert_fusion.2
  345.8 7.4 convolution_convert_fusion.1
  353.2 0.3 reduce-scatter.11.cloned.1.call-start
  353.5 8.9 %convolution_convert_fusion = bf16[3072,768]{1,0:T(8,128)(2,1)} fusion(bf16[512,768]{1,0:T(8,128)(2,1)} %copy-done.15, f32[512,3072]{1,0:T(8,128)} %fusion.31, f32[3072]{0:T(1024)S(1)} %bitcast.97), kind=kOutput, calls=%fused_computation.11 | convolution fusion | flops 2434007040 | bytes 11808768 | tf_op jit(solution)/shard_map/dot_general | solution.py:289
  364.4 0.7 fusion.29
  365.1 50.6 %all-reduce.9 = (f32[]{:T(128)}, f32[]{:T(128)}) all-reduce(f32[]{:T(128)} %get-tuple-element.136, f32[]{:T(128)} %fusion.29), channel_id=1, replica_groups=mesh['ctx'=16,'wsh'=2] {'ctx','wsh'}, use_global_device_ids=true, to_apply=%region_6.7 | all-reduce | flops 2 | bytes 16 | tf_op jit(solution)/shard_map/psum | solution.py:572
  415.6 0.3 slice_reduce_fusion
  416.0 1.0 convert_bitcast_fusion
  417.0 2.4 copy.54
  420.7 3.8 fusion.32
  424.5 1.1 copy-done.14
  425.7 0.8 fusion.15
  426.5 7.5 all-reduce.11
  434.4 2.4 bitcast_convert_fusion.1
  436.8 3.4 add_add_fusion.2
  440.3 21.9 %reduce-scatter.9.cloned.1.call-done = bf16[384,3072]{1,0:T(8,128)(2,1)} async-done(((bf16[768,3072]{1,0:T(8,128)(2,1)}), bf16[384,3072]{1,0:T(8,128)(2,1)}) %reduce-scatter.9.cloned.1.call-update) | async-done | bytes 2359312 | tf_op jit(solution)/shard_map/reduce_scatter | solution.py:625
  462.1 62.9 %reduce-scatter.11.cloned.1.call-done = bf16[1536,768]{1,0:T(8,128)(2,1)} async-done(((bf16[3072,768]{1,0:T(8,128)(2,1)}), bf16[1536,768]{1,0:T(8,128)(2,1)}) %reduce-scatter.11.cloned.1.call-update) | async-done | bytes 2359312 | tf_op jit(solution)/shard_map/reduce_scatter | solution.py:625
  525.1 289.4 %all-reduce.13 = (f32[384]{0:T(512)}, f32[384]{0:T(512)}, f32[384,1920]{1,0:T(8,128)}, f32[576]{0:T(1024)}, f32[384,768]{1,0:T(8,128)}, /*index=5*/f32[384]{0:T(...) all-reduce(f32[384]{0:T(512)S(1)} %get-tuple-element.150, ...), channel_id=1, replica_groups=mesh['ctx'=16,'wsh'=2] {'ctx'}, use_global_device_ids=true, to_apply=%region_15.16 | all-reduce | flops 3395904 | bytes 20384256 | tf_op jit(solution)/shard_map/psum | solution.py:630
  (138 shorter events, 3.0 us)
Async XLA Ops:
  7.2 47.5 %all-gather.12.cloned.1.call-start = ((), (), s32[]{:S(2)}) async-start(), calls=%async_computation.4 | async-start | bytes 4423680 | tf_op jit(solution)/shard_map/all_gather | solution.py:495
  7.9 158.3 %all-gather.14.cloned.1.call-start = ((), (), s32[]{:S(2)}) async-start(), calls=%async_computation.5 | async-start | bytes 1769472 | tf_op jit(solution)/shard_map/all_gather | solution.py:495
  8.7 1.6 copy-start.22
  8.7 2.8 copy-start.23
  8.7 7.4 copy-start.25
  8.7 10.6 %copy-start.24 = (s32[2]{0:T(128)S(1)}, s32[2]{0:T(128)}, u32[]{:S(2)}) copy-start(s32[2]{0:T(128)} %param.21) | copy-start | bytes 28
  8.7 11.7 %copy-start.20 = (s32[2,4096]{1,0:T(2,128)S(1)}, s32[2,4096]{1,0:T(2,128)}, u32[]{:S(2)}) copy-start(s32[2,4096]{1,0:T(2,128)} %param.20) | copy-start | bytes 98308
  8.7 12.5 %copy-start.19 = (bf16[2,256,384]{2,1,0:T(8,128)(2,1)S(1)}, bf16[2,256,384]{2,1,0:T(8,128)(2,1)}, u32[]{:S(2)}) copy-start(bf16[2,256,384]{2,1,0:T(8,128)(2,1)} %param.18) | copy-start | bytes 1179652
  8.7 160.0 %all-gather.16.cloned.1.call-start = ((), (), s32[]{:S(2)}) async-start(), calls=%async_computation.6 | async-start | bytes 7077888 | tf_op jit(solution)/shard_map/all_gather | solution.py:495
  9.5 12.0 %copy-start.26 = (bf16[384]{0:T(512)(128)(2,1)S(1)}, bf16[384]{0:T(512)(128)(2,1)}, u32[]{:S(2)}) copy-start(bf16[384]{0:T(512)(128)(2,1)} %param.23) | copy-start | bytes 2308
  9.5 15.5 %copy-start.27 = (bf16[384]{0:T(512)(128)(2,1)S(1)}, bf16[384]{0:T(512)(128)(2,1)}, u32[]{:S(2)}) copy-start(bf16[384]{0:T(512)(128)(2,1)} %param.22) | copy-start | bytes 2308
  9.5 19.1 %copy-start.9 = (bf16[2,256,768]{2,1,0:T(8,128)(2,1)S(1)}, bf16[2,256,768]{2,1,0:T(8,128)(2,1)}, u32[]{:S(2)}) copy-start(bf16[2,256,768]{2,1,0:T(8,128)(2,1)} %param.17) | copy-start | bytes 2359300
  9.5 197.9 %all-gather.18.cloned.1.call-start = ((), (), s32[]{:S(2)}) async-start(), calls=%async_computation.7 | async-start | bytes 7077888 | tf_op jit(solution)/shard_map/all_gather | solution.py:495
  10.1 19.1 %copy-start.28 = (bf16[384]{0:T(512)(128)(2,1)S(1)}, bf16[384]{0:T(512)(128)(2,1)}, u32[]{:S(2)}) copy-start(bf16[384]{0:T(512)(128)(2,1)} %param.33) | copy-start | bytes 2308
  10.1 22.7 %copy-start.29 = (bf16[384]{0:T(512)(128)(2,1)S(1)}, bf16[384]{0:T(512)(128)(2,1)}, u32[]{:S(2)}) copy-start(bf16[384]{0:T(512)(128)(2,1)} %param.29) | copy-start | bytes 2308
  10.1 26.2 %copy-start.30 = (bf16[384]{0:T(512)(128)(2,1)S(1)}, bf16[384]{0:T(512)(128)(2,1)}, u32[]{:S(2)}) copy-start(bf16[384]{0:T(512)(128)(2,1)} %param.28) | copy-start | bytes 2308
  10.1 29.8 %copy-start.21 = (bf16[1536]{0:T(1024)(128)(2,1)S(1)}, bf16[1536]{0:T(1024)(128)(2,1)}, u32[]{:S(2)}) copy-start(bf16[1536]{0:T(1024)(128)(2,1)} %param.31) | copy-start | bytes 9220
  10.1 430.1 %reduce-scatter.7.cloned.1.call-start = ((), (), s32[]{:S(2)}) async-start(), calls=%async_computation.9 | async-start | bytes 1769472 | tf_op jit(solution)/shard_map/reduce_scatter | solution.py:625
  47.8 52.0 %copy-start.6 = (s32[10]{0:T(128)}, s32[10]{0:T(128)S(1)}, u32[]{:S(2)}) copy-start(s32[10]{0:T(128)S(1)} %pad_add_fusion.info) | copy-start | bytes 124
  48.3 10.1 %copy-start.16 = (bf16[512,768]{1,0:T(8,128)(2,1)}, bf16[512,768]{1,0:T(8,128)(2,1)S(1)}, u32[]{:S(2)}) copy-start(bf16[512,768]{1,0:T(8,128)(2,1)S(1)} %fusion.14) | copy-start | bytes 2359300
  99.8 32.4 %copy-start.1 = (bf16[8,192,256]{2,1,0:T(8,128)(2,1)}, bf16[8,192,256]{2,1,0:T(8,128)(2,1)S(1)}, u32[]{:S(2)}) copy-start(bf16[8,192,256]{2,1,0:T(8,128)(2,1)S(1)} %get-tuple-element.23.q) | copy-start | bytes 2359300
  99.8 32.3 %copy-start.4 = (s32[8,8,256]{2,1,0:T(8,128)}, s32[8,8,256]{2,1,0:T(8,128)S(1)}, u32[]{:S(2)}) copy-start(s32[8,8,256]{2,1,0:T(8,128)S(1)} %broadcast_in_dim.10.lo) | copy-start | bytes 196612
  132.2 1.1 copy-start.2
  133.3 0.6 copy-start.5
  168.4 60.3 %copy-start.13 = (f32[512,768]{1,0:T(8,128)}, f32[512,768]{1,0:T(8,128)S(1)}, u32[]{:S(2)}) copy-start(f32[512,768]{1,0:T(8,128)S(1)} %get-tuple-element.142) | copy-start | bytes 4718596
  207.4 7.6 copy-start.18
  207.4 9.8 %copy-start.32 = (f32[512,3072]{1,0:T(8,128)S(1)}, f32[512,3072]{1,0:T(8,128)}, u32[]{:S(2)}) copy-start(f32[512,3072]{1,0:T(8,128)} %fusion.31) | copy-start | bytes 18874372
  215.0 1.1 copy-start.12
  215.0 3.8 copy-start.31
  216.2 13.1 %copy-start.7 = (f32[2,256,768]{2,1,0:T(8,128)}, f32[2,256,768]{2,1,0:T(8,128)S(1)}, u32[]{:S(2)}) copy-start(f32[2,256,768]{2,1,0:T(8,128)S(1)} %get-tuple-element.124) | copy-start | bytes 4718596
  216.2 9.4 %slice-start = ((s8[4718592]{0:T(1024)(128)(4,1)}), s8[4194304]{0:T(1024)(128)(4,1)S(1)}, s32[]{:S(2)}) async-start(s8[4718592]{0:T(1024)(128)(4,1)} %bitcast.99), calls=%async_computation.12 | async-start | bytes 8388608
  217.2 8.4 %copy-start.15 = (bf16[512,768]{1,0:T(8,128)(2,1)}, bf16[512,768]{1,0:T(8,128)(2,1)S(1)}, u32[]{:S(2)}) copy-start(bf16[512,768]{1,0:T(8,128)(2,1)S(1)} %get-tuple-element.135) | copy-start | bytes 2359300
  218.8 6.8 slice-start.1
  225.6 3.0 copy-start.33
  229.3 1.2 copy-start.10
  232.3 208.0 %reduce-scatter.5.cloned.1.call-start = ((), (), s32[]{:S(2)}) async-start(), calls=%async_computation.8 | async-start | bytes 4423680 | tf_op jit(solution)/shard_map/reduce_scatter | solution.py:625
  250.6 0.9 copy-start
  288.6 1.1 copy-start.3
  289.7 52.5 %copy-start.17 = (bf16[512,768]{1,0:T(8,128)(2,1)S(1)}, bf16[512,768]{1,0:T(8,128)(2,1)}, u32[]{:S(2)}) copy-start(bf16[512,768]{1,0:T(8,128)(2,1)} %copy-done.16) | copy-start | bytes 2359300
  345.7 116.4 %reduce-scatter.9.cloned.1.call-start = ((), (), s32[]{:S(2)}) async-start(), calls=%async_computation.10 | async-start | bytes 7077888 | tf_op jit(solution)/shard_map/reduce_scatter | solution.py:625
  353.2 171.8 %reduce-scatter.11.cloned.1.call-start = ((), (), s32[]{:S(2)}) async-start(), calls=%async_computation.11 | async-start | bytes 7077888 | tf_op jit(solution)/shard_map/reduce_scatter | solution.py:625
  424.5 1.2 copy-start.14
  425.7 11.1 %copy-start.8 = (f32[2,256,768]{2,1,0:T(8,128)S(1)}, f32[2,256,768]{2,1,0:T(8,128)}, u32[]{:S(2)}) copy-start(f32[2,256,768]{2,1,0:T(8,128)} %copy-done.7) | copy-start | bytes 4718596
  434.0 2.8 copy-start.11
Sparse Core Ops, SparseCore 0:
  9.6 45.1 all-gather.11
  56.3 22.7 all-gather.13
  80.6 62.6 all-gather.15
  144.7 62.6 all-gather.17
  232.4 21.7 reduce-scatter.6
  345.8 52.2 reduce-scatter.4
  401.0 61.1 reduce-scatter.8
  465.1 59.9 reduce-scatter.10

commit v2 on v1

--- a/solution.py
+++ b/solution.py
@@ -45,7 +45,8 @@
     def same_core(other):
         return (base + 2 * other + core, wsh)
 
-    return chip, core, same_core, (base + 2 * chip + 1 - core, wsh)
+    sibling, partner = (base + 2 * chip + 1 - core, wsh), (index, 1 - wsh)
+    return chip, core, same_core, sibling, partner, wsh
 
 
 def greet(peers):
@@ -69,10 +70,62 @@
     return pl.ds(pl.multiple_of(first + chip % PER_SEQ * R, R), R)
 
 
-def scatter_kernel(src, q_all, kv_all, send, recv, fsend, frecv, own):
-    chip, core, same_core, sibling = where_am_i()
+def share_start(shard, full, sems, partner, core, wsh):
+    xs, xr, fs, fr, own = sems
+    sends = []
+    for k in range(shard.shape[1]):
+        sends.append(remote(shard.at[core, k], full.at[wsh, core, k], xs.at[k], xr.at[k], partner))
+        sends[-1].start()
+    local = pltpu.make_async_copy(shard, full.at[wsh], own)
+    local.start()
+    return sends, local
+
+
+def share_pass(state, k, full, sems, sibling, core, wsh):
+    xs, xr, fs, fr, own = sems
+    state[0][k].wait_recv()
+    piece = full.at[1 - wsh, core, k]
+    forward = remote(piece, piece, fs.at[k], fr.at[k], sibling)
+    forward.start()
+    return forward
+
+
+def share_end(state, forwards):
+    state[1].wait()
+    for copy in state[0]:
+        copy.wait_send()
+    for copy in forwards:
+        copy.wait()
+
+
+def share_scratch(shard):
+    chunks = shard.shape[1]
+    return [DMA((chunks,)), DMA((chunks,)), DMA((chunks,)), DMA((chunks,)), DMA]
+
+
+def full_of(shard):
+    return jax.ShapeDtypeStruct((2,) + shard.shape, shard.dtype)
+
+
+def first_kernel(weight, small, full, all_small, *sems):
+    chip, core, same_core, sibling, partner, wsh = where_am_i()
+    greet([sibling, partner])
+    pack = share_start(small, all_small, sems[5:], partner, core, wsh)
+    state = share_start(weight, full, sems[:5], partner, core, wsh)
+    passed = [share_pass(pack, 0, all_small, sems[5:], sibling, core, wsh)]
+    forwards = [
+        share_pass(state, k, full, sems[:5], sibling, core, wsh) for k in range(weight.shape[1])
+    ]
+    share_end(pack, passed)
+    share_end(state, forwards)
+
+
+def scatter_kernel(src, weight_a, weight_b, q_all, kv_all, full_a, full_b, *sems):
+    chip, core, same_core, sibling, partner, wsh = where_am_i()
+    send, recv, fsend, frecv, own = sems[:5]
+    sems_a, sems_b = sems[5:10], sems[10:]
     width = q_all.shape[2]
-    greet([same_core((chip + i) % CHIPS) for i in range(1, CHIPS)] + [sibling])
+    greet([same_core((chip + i) % CHIPS) for i in range(1, CHIPS)] + [sibling, partner])
     block = 2 * chip + core
 
     def pieces(target):
@@ -97,6 +150,8 @@
     local = [pltpu.make_async_copy(a, b, own.at[n]) for n, (a, b) in enumerate(pieces(chip))]
     for copy in local:
         copy.start()
+    state_a = share_start(weight_a, full_a, sems_a, partner, core, wsh)
+    state_b = share_start(weight_b, full_b, sems_b, partner, core, wsh)
     for copy in local:
         copy.wait()
     forwards = []
@@ -107,6 +162,14 @@
         came = 2 * ((chip + CHIPS - i) % CHIPS) + core
         forwards.append(remote(kv_all.at[came], kv_all.at[came], fsend.at[i], frecv.at[i], sibling))
         forwards[-1].start()
+    passed_a = [
+        share_pass(state_a, k, full_a, sems_a, sibling, core, wsh)
+        for k in range(weight_a.shape[1])
+    ]
+    passed_b = [
+        share_pass(state_b, k, full_b, sems_b, sibling, core, wsh)
+        for k in range(weight_b.shape[1])
+    ]
     for i in range(1, CHIPS):
         copies[i - 1][2].wait_recv()
     for batch in copies:
@@ -114,29 +177,109 @@
             copy.wait_send()
     for copy in forwards:
         copy.wait()
-
-
-def home_kernel(src, dst, send, recv, own):
-    chip, core, same_core, sibling = where_am_i()
+    share_end(state_a, passed_a)
+    share_end(state_b, passed_b)
+
+
+def home_kernel(src, weight, dst, full, send, recv, own, *sems):
+    chip, core, same_core, sibling, partner, wsh = where_am_i()
     width = src.shape[2]
-    greet([same_core((chip + i) % CHIPS) for i in range(1, CHIPS)])
+    greet([same_core((chip + i) % CHIPS) for i in range(1, CHIPS)] + [sibling, partner])
     place = dst.at[rows_of(chip, 0), lanes_of(chip, width)]
     copies = []
     for i in range(1, CHIPS):
         target = (chip + i) % CHIPS
         copies.append(remote(src.at[target], place, send.at[i], recv.at[i], same_core(target)))
         copies[-1].start()
+    state = share_start(weight, full, sems, partner, core, wsh)
     local = pltpu.make_async_copy(src.at[chip], place, own)
     local.start()
+    passed = [
+        share_pass(state, k, full, sems, sibling, core, wsh) for k in range(weight.shape[1])
+    ]
     local.wait()
     for copy in copies:
         copy.wait()
-
-
-def away_kernel(src, dst, send, recv, own):
-    chip, core, same_core, sibling = where_am_i()
+    share_end(state, passed)
+
+
+def add_into(dst, parts):
+    rows = dst.shape[0]
+    step = 16 if rows % 16 == 0 else 8
+
+    def one(i, unused):
+        at = pl.ds(pl.multiple_of(i * step, step), step)
+        total = parts[0][at, :].astype(jnp.float32)
+        for part in parts[1:]:
+            total = total + part[at, :].astype(jnp.float32)
+        dst[at, :] = total.astype(dst.dtype)
+        return unused
+
+    lax.fori_loop(0, rows // step, one, 0)
+
+
+def pair_start(terms, buffers, sems, sibling, core, wsh):
+    from_sibling, for_partner, from_partner = buffers
+    ss, sr, xs, xr = sems
+    gives = []
+    for half in range(2):
+        which = 1 - wsh if half == 0 else wsh
+        for k in range(terms.shape[2]):
+            gives.append(
+                remote(
+                    terms.at[which, 1 - core, k],
+                    from_sibling.at[half, k],
+                    ss.at[half, k],
+                    sr.at[half, k],
+                    sibling,
+                )
+            )
+            gives[-1].start()
+    return gives
+
+
+def pair_cross(terms, buffers, sems, gives, partner, core, wsh):
+    from_sibling, for_partner, from_partner = buffers
+    ss, sr, xs, xr = sems
+    sends = []
+    for k in range(terms.shape[2]):
+        gives[k].wait_recv()
+        add_into(for_partner.at[k], [terms.at[1 - wsh, core, k], from_sibling.at[0, k]])
+        sends.append(remote(for_partner.at[k], from_partner.at[k], xs.at[k], xr.at[k], partner))
+        sends[-1].start()
+    return sends
+
+
+def pair_end(terms, buffers, gives, sends, result, core, wsh):
+    from_sibling, for_partner, from_partner = buffers
+    chunks = terms.shape[2]
+    for k in range(chunks):
+        gives[chunks + k].wait_recv()
+        sends[k].wait_recv()
+        add_into(
+            result.at[k], [terms.at[wsh, core, k], from_sibling.at[1, k], from_partner.at[k]]
+        )
+    for copy in gives + sends:
+        copy.wait_send()
+
+
+def pair_scratch(terms):
+    chunks, rows, columns = terms.shape[2:]
+    return [
+        pltpu.VMEM((2, chunks, rows, columns), jnp.bfloat16),
+        pltpu.VMEM((chunks, rows, columns), jnp.bfloat16),
+        pltpu.VMEM((chunks, rows, columns), jnp.bfloat16),
+        DMA((2, chunks)),
+        DMA((2, chunks)),
+        DMA((chunks,)),
+        DMA((chunks,)),
+    ]
+
+
+def away_kernel(src, terms, dst, result, send, recv, own, *pair):
+    chip, core, same_core, sibling, partner, wsh = where_am_i()
     width = dst.shape[2]
-    greet([same_core((chip + i) % CHIPS) for i in range(1, CHIPS)])
+    greet([same_core((chip + i) % CHIPS) for i in range(1, CHIPS)] + [sibling, partner])
     copies = []
     for i in range(1, CHIPS):
         target = (chip + i) % CHIPS
@@ -147,15 +290,20 @@
         src.at[rows_of(chip, 0), lanes_of(chip, width)], dst.at[chip], own
     )
     local.start()
+    gives = pair_start(terms, pair[:3], pair[3:], sibling, core, wsh)
+    sends = pair_cross(terms, pair[:3], pair[3:], gives, partner, core, wsh)
+    pair_end(terms, pair[:3], gives, sends, result, core, wsh)
     local.wait()
     for copy in copies:
         copy.wait()
 
 
-def return_kernel(dq, dkv, dst, give, take, final, send, recv, fsend, frecv, own):
-    chip, core, same_core, sibling = where_am_i()
+def return_kernel(dq, dkv, terms_a, terms_b, dst, result_a, result_b, *scratch):
+    chip, core, same_core, sibling, partner, wsh = where_am_i()
+    give, take, final, send, recv, fsend, frecv, own = scratch[:8]
+    pair_a, pair_b = scratch[8:15], scratch[15:]
     width = dq.shape[2]
-    greet([same_core((chip + i) % CHIPS) for i in range(1, CHIPS)] + [sibling])
+    greet([same_core((chip + i) % CHIPS) for i in range(1, CHIPS)] + [sibling, partner])
     lanes = lanes_of(chip, width)
     halves = []
     for i in range(CHIPS):
@@ -180,6 +328,8 @@
         copies[-1].start()
     local = [pltpu.make_async_copy(dq.at[chip], dst.at[rows_of(chip, 0), lanes], own.at[0])]
     local[0].start()
+    gives_a = pair_start(terms_a, pair_a[:3], pair_a[3:], sibling, core, wsh)
+    gives_b = pair_start(terms_b, pair_b[:3], pair_b[3:], sibling, core, wsh)
     for i in list(range(1, CHIPS)) + [0]:
         target = (chip + i) % CHIPS
         halves[i].wait_recv()
@@ -197,6 +347,10 @@
             else:
                 local.append(pltpu.make_async_copy(piece, place, own.at[n]))
                 local[-1].start()
+    sends_a = pair_cross(terms_a, pair_a[:3], pair_a[3:], gives_a, partner, core, wsh)
+    sends_b = pair_cross(terms_b, pair_b[:3], pair_b[3:], gives_b, partner, core, wsh)
+    pair_end(terms_a, pair_a[:3], gives_a, sends_a, result_a, core, wsh)
+    pair_end(terms_b, pair_b[:3], gives_b, sends_b, result_b, core, wsh)
     for copy in local:
         copy.wait()
     for copy in halves:
@@ -205,72 +359,224 @@
         copy.wait()
 
 
+def finish_kernel(small, *refs):
+    chip, core, same_core, sibling, partner, wsh = where_am_i()
+    sums, terms = refs[:3], refs[3]
+    all_small, outs = refs[4], refs[5:9]
+    kept = refs[9]
+    pair = refs[10:17]
+    stages = [refs[17 + 11 * n : 28 + 11 * n] for n in range(4)]
+    small_take, small_send, small_recv = refs[61:]
+    a, b = chip // 2, chip % 2
+    along_a = [(a + i) % 4 for i in range(4)]
+    other_b = same_core(2 * a + 1 - b)
+    peers_a = [same_core(2 * other + b) for other in along_a]
+    greet([sibling, partner, other_b] + peers_a[1:])
+
+    gives = pair_start(terms, pair[:3], pair[3:], sibling, core, wsh)
+    mine = list(sums) + [kept]
+
+    def start_b(n):
+        took_b, added, took_a, bs, br, zs, zr, gs, gr, ks, kr = stages[n]
+        copy = remote(mine[n].at[pl.ds(pl.multiple_of(4 - 4 * b, 4), 4)], took_b, bs, br, other_b)
+        copy.start()
+        return copy
+
+    def start_a(n, swap):
+        took_b, added, took_a, bs, br, zs, zr, gs, gr, ks, kr = stages[n]
+        swap.wait_recv()
+        copies = []
+        for i in (1, 2, 3, 0):
+            other = along_a[i]
+            add_into(added.at[other], [mine[n].at[4 * b + other], took_b.at[other]])
+            if i:
+                copies.append(
+                    remote(added.at[other], took_a.at[i - 1], zs.at[i], zr.at[i], peers_a[i])
+                )
+                copies[-1].start()
+        return copies
+
+    def give_out(n, copies):
+        took_b, added, took_a, bs, br, zs, zr, gs, gr, ks, kr = stages[n]
+        out = outs[n]
+        for copy in copies:
+            copy.wait_recv()
+        piece = out.at[core, 4 * b + a]
+        add_into(piece, [added.at[a], took_a.at[0], took_a.at[1], took_a.at[2]])
+        news = []
+        for i in (1, 2, 3):
+            news.append(remote(piece, piece, gs.at[0, i], gr.at[0, i], peers_a[i]))
+        news.append(remote(piece, piece, gs.at[1, 0], gr.at[1, 0], other_b))
+        news.append(remote(piece, piece, ks.at[0, 0], kr.at[0, 0], sibling))
+        for copy in news:
+            copy.start()
+        return news
+
+    def hand_on(n, news):
+        took_b, added, took_a, bs, br, zs, zr, gs, gr, ks, kr = stages[n]
+        out = outs[n]
+        more = []
+        for i in (1, 2, 3):
+            news[i - 1].wait_recv()
+            piece = out.at[core, 4 * b + (a + 4 - i) % 4]
+            more.append(remote(piece, piece, gs.at[1, i], gr.at[1, i], other_b))
+            more.append(remote(piece, piece, ks.at[0, i], kr.at[0, i], sibling))
+            for copy in more[-2:]:
+                copy.start()
+        return more
+
+    def last_pass(n, news, more):
+        took_b, added, took_a, bs, br, zs, zr, gs, gr, ks, kr = stages[n]
+        out = outs[n]
+        final = []
+        for i in range(4):
+            (news[3] if i == 0 else more[2 * i - 2]).wait_recv()
+            piece = out.at[core, 4 - 4 * b + (a + 4 - i) % 4]
+            final.append(remote(piece, piece, ks.at[1, i], kr.at[1, i], sibling))
+            final[-1].start()
+        return final
+
+    swaps = [start_b(n) for n in range(3)]
+    sends = pair_cross(terms, pair[:3], pair[3:], gives, partner, core, wsh)
+
+    all_small[...] = small[...]
+    order = [sibling, partner, other_b]
+    for n, peer in enumerate(order):
+        small_take[3 + n] = all_small[...]
+        copy = remote(
+            small_take.at[3 + n], small_take.at[n], small_send.at[n], small_recv.at[n], peer
+        )
+        copy.start()
+        copy.wait()
+        all_small[...] = all_small[...] + small_take[n]
+    small_take[6 + a] = all_small[...]
+    smalls = []
+    for i in (1, 2, 3):
+        smalls.append(
+            remote(
+                small_take.at[6 + a],
+                small_take.at[6 + a],
+                small_send.at[2 + i],
+                small_recv.at[2 + i],
+                peers_a[i],
+            )
+        )
+        smalls[-1].start()
+
+    crossings = [start_a(n, swaps[n]) for n in range(3)]
+    pair_end(terms, pair[:3], gives, sends, kept, core, wsh)
+    swaps.append(start_b(3))
+    news = [give_out(n, crossings[n]) for n in range(3)]
+    crossings.append(start_a(3, swaps[3]))
+    more = [hand_on(n, news[n]) for n in range(3)]
+    news.append(give_out(3, crossings[3]))
+    final = [last_pass(n, news[n], more[n]) for n in range(3)]
+    more.append(hand_on(3, news[3]))
+    final.append(last_pass(3, news[3], more[3]))
+    for copy in smalls:
+        copy.wait()
+    all_small[...] = small_take[6] + small_take[7] + small_take[8] + small_take[9]
+    for n in range(4):
+        swaps[n].wait_send()
+        for copy in crossings[n] + news[n] + more[n] + final[n]:
+            copy.wait_send()
+        news[n][4].wait_recv()
+        for i in (1, 2, 3):
+            more[n][2 * i - 1].wait_recv()
+        for copy in final[n]:
+            copy.wait_recv()
+
+
 ANY = pl.BlockSpec(memory_space=pl.ANY)
 VMEM = pl.BlockSpec(memory_space=pltpu.VMEM)
 SMEM = pl.BlockSpec(memory_space=pltpu.SMEM)
 
 
-def comm_params(number):
+def comm_params(number, mib=48):
     return pltpu.CompilerParams(
-        collective_id=number, has_side_effects=True, vmem_limit_bytes=48 << 20
-    )
-
-
-def scatter_heads(src, width):
+        collective_id=number, has_side_effects=True, vmem_limit_bytes=mib << 20
+    )
+
+
+def gather_first(weight, small):
+    return pl.pallas_call(
+        first_kernel,
+        name="gather_first",
+        out_shape=(full_of(weight), full_of(small)),
+        in_specs=[ANY, ANY],
+        out_specs=(ANY, ANY),
+        scratch_shapes=share_scratch(weight) + share_scratch(small),
+        compiler_params=comm_params(4),
+    )(weight, small)
+
+
+def scatter_heads(src, weight_a, weight_b, width):
     return pl.pallas_call(
         scatter_kernel,
         name="scatter_heads",
         out_shape=(
             jax.ShapeDtypeStruct((CHIPS, R, width), jnp.bfloat16),
             jax.ShapeDtypeStruct((GROUP, 2 * R, width), jnp.bfloat16),
+            full_of(weight_a),
+            full_of(weight_b),
         ),
-        in_specs=[ANY],
-        out_specs=(ANY, ANY),
+        in_specs=[ANY] * 3,
+        out_specs=(ANY,) * 4,
         scratch_shapes=[
             DMA((3, CHIPS)),
             DMA((3, CHIPS)),
             DMA((CHIPS,)),
             DMA((CHIPS,)),
             DMA((3,)),
-        ],
+        ]
+        + share_scratch(weight_a)
+        + share_scratch(weight_b),
         compiler_params=comm_params(0),
-    )(src)
-
-
-def send_home(src):
+    )(src, weight_a, weight_b)
+
+
+def send_home(src, weight):
     width = src.shape[2]
     return pl.pallas_call(
         home_kernel,
         name="send_home",
-        out_shape=jax.ShapeDtypeStruct((D, SEQS * width), jnp.bfloat16),
-        in_specs=[ANY],
-        out_specs=ANY,
-        scratch_shapes=[DMA((CHIPS,)), DMA((CHIPS,)), DMA],
+        out_shape=(jax.ShapeDtypeStruct((D, SEQS * width), jnp.bfloat16), full_of(weight)),
+        in_specs=[ANY, ANY],
+        out_specs=(ANY, ANY),
+        scratch_shapes=[DMA((CHIPS,)), DMA((CHIPS,)), DMA] + share_scratch(weight),
         compiler_params=comm_params(1),
-    )(src)
-
-
-def send_away(src, width):
+    )(src, weight)
+
+
+def sum_of(terms):
+    return jax.ShapeDtypeStruct(terms.shape[2:], jnp.bfloat16)
+
+
+def send_away(src, terms, width):
     return pl.pallas_call(
         away_kernel,
         name="send_away",
-        out_shape=jax.ShapeDtypeStruct((CHIPS, R, width), jnp.bfloat16),
-        in_specs=[ANY],
-        out_specs=ANY,
-        scratch_shapes=[DMA((CHIPS,)), DMA((CHIPS,)), DMA],
+        out_shape=(jax.ShapeDtypeStruct((CHIPS, R, width), jnp.bfloat16), sum_of(terms)),
+        in_specs=[ANY, VMEM],
+        out_specs=(ANY, VMEM),
+        scratch_shapes=[DMA((CHIPS,)), DMA((CHIPS,)), DMA] + pair_scratch(terms),
         compiler_params=comm_params(2),
-    )(src)
-
-
-def return_heads(dq, dkv):
+    )(src, terms)
+
+
+def return_heads(dq, dkv, terms_a, terms_b):
     width = dq.shape[2]
     pair = pltpu.VMEM((CHIPS, 2 * R, width), jnp.bfloat16)
     return pl.pallas_call(
         return_kernel,
         name="return_heads",
-        out_shape=jax.ShapeDtypeStruct((3 * D, SEQS * width), jnp.bfloat16),
-        in_specs=[ANY, VMEM],
-        out_specs=ANY,
+        out_shape=(
+            jax.ShapeDtypeStruct((3 * D, SEQS * width), jnp.bfloat16),
+            sum_of(terms_a),
+            sum_of(terms_b),
+        ),
+        in_specs=[ANY, VMEM, VMEM, VMEM],
+        out_specs=(ANY, VMEM, VMEM),
         scratch_shapes=[
             pair,
             pair,
@@ -280,9 +586,50 @@
             DMA((CHIPS,)),
             DMA((CHIPS,)),
             DMA((3,)),
+        ]
+        + pair_scratch(terms_a)
+        + pair_scratch(terms_b),
+        compiler_params=comm_params(3, 56),
+    )(dq, dkv, terms_a, terms_b)
+
+
+def finish_sums(small, sums, terms):
+    def stage(total):
+        rows, columns = total.shape[1:]
+        four = pltpu.VMEM((4, rows, columns), jnp.bfloat16)
+        return [
+            four,
+            four,
+            pltpu.VMEM((3, rows, columns), jnp.bfloat16),
+            DMA,
+            DMA,
+            DMA((4,)),
+            DMA((4,)),
+            DMA((2, 4)),
+            DMA((2, 4)),
+            DMA((2, 4)),
+            DMA((2, 4)),
+        ]
+
+    kept = sum_of(terms)
+    whole = [*sums, kept]
+    return pl.pallas_call(
+        finish_kernel,
+        name="finish_sums",
+        out_shape=[jax.ShapeDtypeStruct(small.shape, small.dtype)]
+        + [jax.ShapeDtypeStruct((2,) + total.shape, total.dtype) for total in whole],
+        in_specs=[VMEM] * 5,
+        out_specs=[VMEM] * 5,
+        scratch_shapes=[pltpu.VMEM(kept.shape, kept.dtype)]
+        + pair_scratch(terms)
+        + [item for total in whole for item in stage(total)]
+        + [
+            pltpu.VMEM((10,) + small.shape, small.dtype),
+            DMA((6,)),
+            DMA((6,)),
         ],
-        compiler_params=comm_params(3),
-    )(dq, dkv)
+        compiler_params=comm_params(5, 56),
+    )(small, *sums, terms)
 
 
 def over_rows(left, right):
@@ -449,6 +796,10 @@
         ],
         compiler_params=pltpu.CompilerParams(vmem_limit_bytes=56 << 20),
     )(info, q, kv, lo, grad, wide, logs)
+
+
+def as_terms(grad, chunks):
+    return grad.astype(jnp.bfloat16).reshape(2, 2, chunks, -1, grad.shape[1])
 
 
 def local(
@@ -478,36 +829,30 @@
     halo = pl.cdiv(DOC_MAX - 1, width) if groups > 1 else 0
     assert seq_count == SEQS and ctx_size % GROUP == 0 and halo <= GROUP
     chip, core = ctx_index % GROUP // 2, ctx_index % 2
+    small_parts = (ln1_gain, ln1_bias, qv_bias, b_out, ln2_gain, ln2_bias, b_fc, b_proj)
+    small_sizes = [part.shape[0] for part in small_parts]
+    small_rows = pl.cdiv(sum(small_sizes), 2 * 16 * 128) * 16
+    packed = jnp.concatenate(small_parts)
+    packed = jnp.pad(packed, (0, 2 * small_rows * 128 - packed.shape[0]))
+    qkv_full, small_full = gather_first(
+        w_qkv.reshape(2, 4, w_qkv.shape[0] // 8, -1), packed.reshape(2, 1, small_rows, 128)
+    )
+    qkv_weight = qkv_full.reshape(D, -1)
+    small_full = small_full.reshape(2, -1)
+    vectors, at = [], 0
+    for size in small_sizes:
+        vectors.append(small_full[:, at : at + size].reshape(-1))
+        at += size
     (
         norm1_gain,
         norm1_shift,
-        qkv_weight,
         qv_shift,
-        out_weight,
         out_shift,
         norm2_gain,
         norm2_shift,
-        fc_weight,
         fc_shift,
-        proj_weight,
         proj_shift,
-    ) = (
-        lax.all_gather(part, "wsh", axis=0, tiled=True)
-        for part in (
-            ln1_gain,
-            ln1_bias,
-            w_qkv,
-            qv_bias,
-            w_out,
-            b_out,
-            ln2_gain,
-            ln2_bias,
-            w_fc,
-            b_fc,
-            w_proj,
-            b_proj,
-        )
-    )
+    ) = vectors
     query_pos = ctx_index * width + jnp.arange(width, dtype=jnp.int32)
 
     window = (halo + GROUP) * width
@@ -542,14 +887,21 @@
         ],
         axis=0,
     )
-    q_all, kv_all = scatter_heads(sent, width)
+    q_all, kv_all, out_full, fc_full = scatter_heads(
+        sent,
+        w_out.reshape(2, 1, w_out.shape[0] // 2, -1),
+        w_fc.reshape(2, 4, w_fc.shape[0] // 8, -1),
+        width,
+    )
+    out_weight, fc_weight = out_full.reshape(D, D), fc_full.reshape(D, -1)
     if halo:
         ahead = [(i, i + GROUP) for i in range(ctx_size - GROUP)]
         kv_all = jnp.concatenate(
             [lax.ppermute(kv_all[GROUP - halo :], "ctx", ahead), kv_all], axis=0
         )
     out_wide, out_low, logs = attention_forward(info, q_all, kv_all, lo, halo)
-    attended = send_home(out_low)
+    attended, proj_full = send_home(out_low, w_proj.reshape(2, 4, w_proj.shape[0] // 8, -1))
+    proj_weight = proj_full.reshape(-1, D)
     resid = inputs + over_rows(attended, out_weight) + out_shift.astype(jnp.float32)
     normed2, norm2_back = jax.vjp(
         norm_layer, resid, norm2_gain.astype(jnp.float32), norm2_shift.astype(jnp.float32)
@@ -569,10 +921,6 @@
     deviation = (
         result.reshape(seq_count, width, D) - teacher.astype(jnp.float32)
     ) * valid_rows[:, :, None]
-    squares, valid_count = lax.psum(
-        (jnp.sum(deviation * deviation), jnp.sum(valid_rows)), ("ctx", "wsh")
-    )
-    loss = squares / (valid_count * D)
     grad_output = deviation.reshape(row_count, D)
     grad_mixed = grad_output.astype(jnp.bfloat16)
     grad_proj_w = over_rows(activ_low, grad_mixed)
@@ -588,13 +936,15 @@
     grad_out_w = jnp.dot(attended, grad_branch, preferred_element_type=jnp.float32)
     grad_out_b = jnp.sum(grad_branch.astype(jnp.float32), axis=0)
     grad_attended = over_lanes(out_weight, grad_branch).astype(jnp.bfloat16)
-    grad_all = send_away(grad_attended, width)
+    grad_all, proj_sum = send_away(grad_attended, as_terms(grad_proj_w, 4), width)
     dq, dkv = attention_backward(info, q_all, kv_all, lo, grad_all, out_wide, logs, halo)
     if halo:
         behind = [(i + GROUP, i) for i in range(ctx_size - GROUP)]
         over = lax.ppermute(dkv[:halo].astype(jnp.bfloat16), "ctx", behind)
         dkv = dkv[halo:].at[GROUP - halo :].add(over.astype(jnp.float32))
-    grads_t = return_heads(dq, dkv)
+    grads_t, fc_sum, out_sum = return_heads(
+        dq, dkv, as_terms(grad_fc_w, 4), as_terms(grad_out_w, 1)
+    )
     grad_projected = grads_t[: 2 * D + VW]
     grad_first = grads_t[2 * D + VW :].T.astype(jnp.float32)
     grad_qkv_w = lax.dot_general(
@@ -607,33 +957,55 @@
     )
     grad_input_norm, grad_g1, grad_b1 = norm1_back(grad_normed1)
     grad_inputs = grad_resid + grad_input_norm
-    grads = (
-        grad_g1,
-        grad_b1,
-        grad_qkv_w,
-        grad_qv_b,
-        grad_out_w,
-        grad_out_b,
-        grad_g2,
-        grad_b2,
-        grad_fc_w,
-        grad_fc_b,
-        grad_proj_w,
-        grad_proj_b,
-    )
-    shares = tuple(
-        lax.psum_scatter(
-            part.astype(jnp.bfloat16), "wsh", scatter_dimension=0, tiled=True
-        ).astype(jnp.float32)
-        for part in grads
-    )
-    totals = tuple(lax.psum(shares, "ctx"))
+    small_grads = (grad_g1, grad_b1, grad_qv_b, grad_out_b, grad_g2, grad_b2, grad_fc_b, grad_proj_b)
+    small_grads = jnp.concatenate(
+        [part.reshape(2, -1) for part in small_grads], axis=1
+    ).reshape(-1)
+    scalars = jnp.stack([jnp.sum(deviation * deviation), jnp.sum(valid_rows)])
+    small_grads = jnp.concatenate([small_grads, scalars])
+    total_rows = pl.cdiv(small_grads.shape[0], 8 * 128) * 8
+    small_grads = jnp.pad(small_grads, (0, total_rows * 128 - small_grads.shape[0]))
+    small_all, proj_all, fc_all, out_all, qkv_all = finish_sums(
+        small_grads.reshape(total_rows, 128),
+        [part.reshape(CHIPS, -1, part.shape[-1]) for part in (proj_sum, fc_sum, out_sum)],
+        as_terms(grad_qkv_w, CHIPS),
+    )
+    small_all = small_all.reshape(-1)
+    large = [part.reshape(-1, part.shape[-1]) for part in (qkv_all, out_all, fc_all, proj_all)]
+    if groups > 1:
+        sets = [[first + GROUP * g for g in range(groups)] for first in range(GROUP)]
+        small_all = lax.psum(small_all, "ctx", axis_index_groups=sets)
+        large = [
+            lax.psum(part.astype(jnp.float32), "ctx", axis_index_groups=sets) for part in large
+        ]
+    large = [part.astype(jnp.float32) for part in large]
+    length_all = sum(small_sizes)
+    loss = small_all[2 * length_all] / (small_all[2 * length_all + 1] * D)
+    my_small = lax.dynamic_slice_in_dim(
+        small_all, lax.axis_index("wsh") * length_all, length_all
+    )
+    shares, at = [], 0
+    for size in small_sizes:
+        shares.append(my_small[at : at + size])
+        at += size
     return (
         loss,
         result.reshape(seq_count, width, D).astype(jnp.bfloat16),
         grad_inputs.reshape(seq_count, width, D),
         grad_first.reshape(seq_count, width, D - VW),
-    ) + totals
+        shares[0],
+        shares[1],
+        large[0],
+        shares[2],
+        large[1],
+        shares[3],
+        shares[4],
+        shares[5],
+        large[2],
+        shares[6],
+        large[3],
+        shares[7],
+    )
 
 
 def solution(mesh):

time: 831 us -> 559 us (0.67)
  blocking collectives: 376 us -> 0 us
  Pallas kernels: 211 us -> 422 us
  waiting for transfers between devices: 125 us -> 0 us
  other arithmetic: 16.8 us -> 38 us
  local copies, waits for them, and re-layouts: 13.9 us -> 30.9 us
  between operations: 21.1 us -> 5.2 us
    psum x2 -> x0, blocking collectives: 340 us -> none  [the longest x1 289 us: local(): totals = tuple(lax.psum(shares, 'ctx'))]
    pallas_call x3 -> x5, Pallas kernels: 101 us -> 269 us  [the longest x1 133 us: finish_sums(): pl.pallas_call(finish_kernel, name='finish_sums', out_shape=[jax.ShapeDty...]
    reduce_scatter x4 -> x0, waiting for transfers between devices: 84.8 us -> none  [local(): lax.psum_scatter(part.astype(jnp.bfloat16), 'wsh', scatter_dimension=0, t...]
    all_gather x4 -> x0, waiting for transfers between devices: 37.9 us -> none  [local(): lax.all_gather(part, 'wsh', axis=0, tiled=True)]
    pallas_call x1, Pallas kernels: 40.9 us -> 77.9 us  [scatter_heads(): pl.pallas_call(scatter_kernel, name='scatter_heads', out_shape=(jax.Shape...]
    all_gather x7 -> x0, blocking collectives: 24.4 us -> none  [local(): lax.all_gather(part, 'wsh', axis=0, tiled=True)]
    unnamed x2 -> x0, blocking collectives: 11.8 us -> none
  transfers between devices with their start and end apart: 8 -> 0, of which waited for: 4 -> 0; matrix products, arithmetic and copies ran while one was open for 7% -> 0% of each run, Pallas kernels for 26% -> 0%
where the time goes in v2:
time: 559 us; the launch traced here: 551 us
  Pallas kernels  422 us (75%)
  matrix products  55 us (10%)
  other arithmetic  38 us (7%)
  local copies, waits for them, and re-layouts  30.9 us (6%)
    pallas_call x1, Pallas kernels, finish_sums(): pl.pallas_call(finish_kernel, name='finish_sums', out_shape=[jax.ShapeDty...  133 us
    pallas_call x1, Pallas kernels, scatter_heads(): pl.pallas_call(scatter_kernel, name='scatter_heads', out_shape=(jax.Shape...  77.9 us
    pallas_call x1, Pallas kernels, return_heads(): pl.pallas_call(return_kernel, name='return_heads', out_shape=(jax.ShapeDt...  49.4 us
    pallas_call x1, Pallas kernels, attention_backward(): pl.pallas_call(functools.partial(backward_kernel, halo), name='attention_...  39.9 us
    pallas_call x1, Pallas kernels, send_away(): pl.pallas_call(away_kernel, name='send_away', out_shape=(jax.ShapeDtypeSt...  38.4 us
    pallas_call x1, Pallas kernels, attention_forward(): pl.pallas_call(functools.partial(forward_kernel, halo), name='attention_f...  35.1 us
    pallas_call x1, Pallas kernels, send_home(): pl.pallas_call(home_kernel, name='send_home', out_shape=(jax.ShapeDtypeSt...  27 us
    pallas_call x1, Pallas kernels, gather_first(): pl.pallas_call(first_kernel, name='gather_first', out_shape=(full_of(weig...  21.5 us

profile of v2, /device:TPU:1, one launch (start us, length us, event | category | flops | bytes accessed | tf_op | source)
XLA Modules:
  0.0 551.3 jit_solution(444102902939948527)
XLA Ops:
  0.8 1.4 dynamic_slice.18
  2.8 1.3 fusion.34
  4.1 1.3 compare_convert_fusion
  5.4 1.3 convert_reduce_fusion.3
  6.8 0.6 copy.43
  7.4 1.5 fusion.18
  8.9 0.6 copy.44
  9.5 5.6 %concatenate.19 = bf16[4416]{0:T(1024)(128)(2,1)S(1)} concatenate(bf16[384]{0:T(512)(128)(2,1)} %param.22, bf16[384]{0:T(512)(128)(2,1)} %param.23, bf16[576]{0:T(1024)(128)(2,1)} %param.25, bf16[384]{0:T(512)(128)(2,1)} %param.27, bf16[384]{0:T(512)(128)(2,1)} %param.28, bf16[384]{0:T(512)(128)(2,1)} %param.29, bf16[1536]{0:T(1024)(128)(2,1)} %param.31, bf16[384]{0:T(512)(128)(2,1)} %param.33), dimensions={0} | concatenate | bytes 17664 | tf_op jit(solution)/shard_map/concatenate | solution.py:835
  15.1 0.5 broadcast.210
  15.6 1.5 fusion.40
  17.1 3.4 convert_reduce_fusion
  20.9 21.5 %gather_first.1 = (bf16[2,2,4,48,1920]{4,3,2,1,0:T(8,128)(2,1)S(1)}, bf16[2,2,1,32,128]{4,3,2,1,0:T(8,128)(2,1)S(1)}) custom-call(bf16[2,4,48,1920]{3,2,1,0:T(8,128)(2,1)S(1)} %bitcast.118, bf16[2,1,32,128]{3,2,1,0:T(8,128)(2,1)S(1)} %bitcast.121), custom_call_target="tpu_custom_call" | custom-call | tf_op jit(solution)/shard_map/gather_first/pallas_call | solution.py:502
  42.4 1.6 copy-done.10
  44.8 3.6 fusion.45
  49.0 0.9 copy-done.7
  49.9 77.9 %scatter_heads.1 = (bf16[8,192,256]{2,1,0:T(8,128)(2,1)S(1)}, bf16[16,384,256]{2,1,0:T(8,128)(2,1)}, bf16[2,2,1,192,768]{4,3,2,1,0:T(8,128)(2,1)S(1)}, bf16[2,2,4,48,3072]{4,3,2,1,0:T(8,128)(2,1)}) custom-call(bf16[2304,512]{1,0:T(8,128)(2,1)S(1)} %pad_maximum_fusion.src, bf16[2,1,192,768]{3,2,1,0:T(8,128)(2,1)S(1)} %bitcast.120, ...), custom_call_target="tpu_custom_call" | custom-call | tf_op jit(solution)/shard_map/scatter_heads/pallas_call | solution.py:514
  127.9 35.1 %attention_forward.1 = (f32[8,192,256]{2,1,0:T(8,128)S(1)}, bf16[8,192,256]{2,1,0:T(8,128)(2,1)S(1)}, f32[8,8,256]{2,1,0:T(8,128)S(1)}) custom-call(s32[10]{0:T(128)S(1)} %pad_add_fusion.info, bf16[8,192,256]{2,1,0:T(8,128)(2,1)S(1)} %get-tuple-element.41.q, bf16[16,384,256]{2,1,0:T(8,128)(2,1)} %get-tuple-element.42.kv, s32[8,8,256]{2,1,0:T(8,128)S(1)} %broadcast_in_dim.10.lo), custom_call_target="tpu_custom_call" | custom-call | tf_op jit(solution)/shard_map/attention_forward/pallas_call | solution.py:713
  163.0 27.0 %send_home.1 = (bf16[768,512]{1,0:T(8,128)(2,1)S(1)}, bf16[2,2,4,192,768]{4,3,2,1,0:T(8,128)(2,1)}) custom-call(bf16[8,192,256]{2,1,0:T(8,128)(2,1)S(1)} %get-tuple-element.44.src, bf16[2,4,192,768]{3,2,1,0:T(8,128)(2,1)S(1)} %bitcast.117), custom_call_target="tpu_custom_call" | custom-call | tf_op jit(solution)/shard_map/send_home/pallas_call | solution.py:540
  190.0 0.9 fusion.44
  191.4 2.7 fusion.36
  194.2 4.0 add_add_fusion.3
  198.2 1.0 bitcast_convert_fusion.5
  199.1 0.4 copy-done.25
  199.6 1.2 multiply_reduce_fusion
  200.8 1.3 convert_reduce_fusion.4
  202.1 0.6 reshape.387
  202.7 10.0 %convert_reduce_fusion.1 = (f32[3072]{0:T(1024)}, bf16[512,3072]{1,0:T(8,128)(2,1)S(1)}) fusion(f32[512,3072]{1,0:T(8,128)} %copy-done.50, f32[3072]{0:T(1024)} %copy-done.41, bf16[512,768]{1,0:T(8,128)(2,1)} %bitcast.138, bf16[3072,768]{1,0:T(8,128)(2,1)} %bitcast.158), kind=kOutput, calls=%fused_computation.10 | convolution fusion | flops 2452091904 | bytes 14966784 | tf_op jit(solution)/shard_map/dot_general | solution.py:642
  212.7 9.8 %convolution_convert_fusion.1 = bf16[3072,768]{1,0:T(8,128)(2,1)} fusion(bf16[512,768]{1,0:T(8,128)(2,1)S(1)} %copy-done.24, f32[512,3072]{1,0:T(8,128)} %copy-done.50, f32[3072]{0:T(1024)S(1)} %copy-done.42), kind=kOutput, calls=%fused_computation.13 | convolution fusion | flops 2434007040 | bytes 11808768 | tf_op jit(solution)/shard_map/dot_general | solution.py:636
  222.5 7.0 %multiply_reduce_fusion.1 = (f32[768]{0:T(1024)}, f32[512]{0:T(512)}, f32[768]{0:T(1024)}, f32[512,768]{1,0:T(8,128)}) fusion(f32[512,768]{1,0:T(8,128)S(1)} %copy-done.16, f32[512]{0:T(512)S(1)} %copy-done.45, f32[512]{0:T(512)S(1)} %broadcast_multiply_fusion, f32[768]{0:T(1024)S(1)} %reshape.403, bf16[512,3072]{1,0:T(8,128)(2,1)S(1)} %get-tuple-element.121, ...), kind=kOutput, calls=%fused_computation.49 | convolution fusion | flops 2419062784 | bytes 11025408 | tf_op jit(solution)/shard_map/dot_general | solution.py:642
  229.5 0.7 reshape.386
  230.2 1.3 reshape.384
  231.5 0.7 multiply_multiply_fusion.3
  232.3 3.7 fusion.39
  236.0 4.8 convolution_convert_fusion
  240.8 0.6 negate_multiply_fusion.1
  241.4 1.3 reshape.385
  242.7 2.3 convert_reduce_fusion.5
  244.9 0.9 copy-done.22
  245.8 0.8 convolution_convert_fusion.4.src
  246.6 38.4 %send_away.1 = (bf16[8,192,256]{2,1,0:T(8,128)(2,1)S(1)}, bf16[4,192,768]{2,1,0:T(8,128)(2,1)S(1)}) custom-call(bf16[768,512]{1,0:T(8,128)(2,1)S(1)} %convolution_convert_fusion.4.src, bf16[2,2,4,192,768]{4,3,2,1,0:T(8,128)(2,1)} %bitcast.129), custom_call_target="tpu_custom_call" | custom-call | tf_op jit(solution)/shard_map/send_away/pallas_call | solution.py:556
  285.0 1.0 copy-done.4
  286.0 0.9 copy-done.5
  286.9 0.6 reshape.383
  287.5 1.8 convolution_convert_fusion.3
  289.3 39.9 %attention_backward.1 = (bf16[8,192,256]{2,1,0:T(8,128)(2,1)}, f32[16,384,256]{2,1,0:T(8,128)}) custom-call(s32[10]{0:T(128)} %copy-done.9, bf16[8,192,256]{2,1,0:T(8,128)(2,1)} %copy-done, bf16[16,384,256]{2,1,0:T(8,128)(2,1)} %get-tuple-element.42.kv, s32[8,8,256]{2,1,0:T(8,128)} %copy-done.6, bf16[8,192,256]{2,1,0:T(8,128)(2,1)} %copy-done.5, ...), custom_call_target="tpu_custom_call" | custom-call | tf_op jit(solution)/shard_map/attention_backward/pallas_call | solution.py:784
  329.2 49.4 %return_heads.1 = (bf16[2304,512]{1,0:T(8,128)(2,1)}, bf16[4,48,3072]{2,1,0:T(8,128)(2,1)}, bf16[1,192,768]{2,1,0:T(8,128)(2,1)}) custom-call(bf16[8,192,256]{2,1,0:T(8,128)(2,1)} %get-tuple-element.51.dq, f32[16,384,256]{2,1,0:T(8,128)} %get-tuple-element.52.dkv, bf16[2,2,4,48,3072]{4,3,2,1,0:T(8,128)(2,1)} %bitcast.128, bf16[2,2,1,192,768]{4,3,2,1,0:T(8,128)(2,1)} %bitcast.134), custom_call_target="tpu_custom_call" | custom-call | tf_op jit(solution)/shard_map/return_heads/pallas_call | solution.py:570
  378.7 4.7 fusion.22
  384.0 2.3 fusion.35
  386.4 3.6 add_add_fusion.2
  390.2 1.3 concatenate.23
  391.5 0.6 pad_bitcast_fusion.small
  392.2 1.1 convert_bitcast_fusion
  393.3 5.0 convolution_convert_fusion.2
  398.2 1.1 copy.41
  399.4 132.9 %finish_sums.1 = (f32[72,128]{1,0:T(8,128)}, bf16[2,8,96,768]{3,2,1,0:T(8,128)(2,1)}, bf16[2,8,24,3072]{3,2,1,0:T(8,128)(2,1)}, bf16[2,8,24,768]{3,2,1,0:T(8,128)(2,1)}, bf16[2,8,24,1920]{3,2,1,0:T(8,128)(2,1)}) custom-call(f32[72,128]{1,0:T(8,128)} %pad_bitcast_fusion.small, bf16[8,96,768]{2,1,0:T(8,128)(2,1)} %bitcast.119, bf16[8,24,3072]{2,1,0:T(8,128)(2,1)} %bitcast.135, ...), custom_call_target="tpu_custom_call" | custom-call | tf_op jit(solution)/shard_map/finish_sums/pallas_call | solution.py:616
  532.3 1.4 fusion.42
  535.0 1.4 dynamic-slice.2
  536.4 1.4 dynamic-slice.6
  537.8 1.5 fusion.41
  539.3 2.2 bitcast_convert_fusion.4
  541.5 1.9 bitcast_convert_fusion.3
  543.4 0.8 copy-done.19
  544.1 2.9 bitcast_convert_fusion.1
  547.0 2.7 bitcast_convert_fusion
  (153 shorter events, 3.0 us)
Async XLA Ops:
  0.6 20.3 %copy-start.3 = (bf16[384,1920]{1,0:T(8,128)(2,1)S(1)}, bf16[384,1920]{1,0:T(8,128)(2,1)}, u32[]{:S(2)}) copy-start(bf16[384,1920]{1,0:T(8,128)(2,1)} %param.24) | copy-start | bytes 4423684
  0.7 20.1 %copy-start.26 = (bf16[2,256,384]{2,1,0:T(8,128)(2,1)S(1)}, bf16[2,256,384]{2,1,0:T(8,128)(2,1)}, u32[]{:S(2)}) copy-start(bf16[2,256,384]{2,1,0:T(8,128)(2,1)} %param.18) | copy-start | bytes 1179652
  6.7 37.7 %copy-start.12 = (bf16[2,256,768]{2,1,0:T(8,128)(2,1)S(1)}, bf16[2,256,768]{2,1,0:T(8,128)(2,1)}, u32[]{:S(2)}) copy-start(bf16[2,256,768]{2,1,0:T(8,128)(2,1)} %param.17) | copy-start | bytes 2359300
  20.7 107.1 %copy-start.9 = (s32[10]{0:T(128)}, s32[10]{0:T(128)S(1)}, u32[]{:S(2)}) copy-start(s32[10]{0:T(128)S(1)} %pad_add_fusion.info) | copy-start | bytes 124
  20.7 107.1 %copy-start.6 = (s32[8,8,256]{2,1,0:T(8,128)}, s32[8,8,256]{2,1,0:T(8,128)S(1)}, u32[]{:S(2)}) copy-start(s32[8,8,256]{2,1,0:T(8,128)S(1)} %broadcast_in_dim.10.lo) | copy-start | bytes 196612
  42.4 1.6 copy-start.10
  44.3 149.8 %copy-start.41 = (f32[3072]{0:T(1024)}, f32[3072]{0:T(1024)S(1)}, u32[]{:S(2)}) copy-start(f32[3072]{0:T(1024)S(1)} %reshape.405) | copy-start | bytes 36868
  44.4 178.1 %copy-start.34 = (f32[768]{0:T(1024)}, f32[768]{0:T(1024)S(1)}, u32[]{:S(2)}) copy-start(f32[768]{0:T(1024)S(1)} %reshape.403) | copy-start | bytes 9220
  44.4 147.0 %copy-start.48 = (f32[768]{0:T(1024)}, f32[768]{0:T(1024)S(1)}, u32[]{:S(2)}) copy-start(f32[768]{0:T(1024)S(1)} %reshape.404) | copy-start | bytes 9220
  44.4 4.0 copy-start.27
  48.8 1.1 copy-start.7
  127.8 35.2 %copy-start = (bf16[8,192,256]{2,1,0:T(8,128)(2,1)}, bf16[8,192,256]{2,1,0:T(8,128)(2,1)S(1)}, u32[]{:S(2)}) copy-start(bf16[8,192,256]{2,1,0:T(8,128)(2,1)S(1)} %get-tuple-element.41.q) | copy-start | bytes 2359300
  127.8 35.2 %copy-start.1 = (bf16[1536,768]{1,0:T(8,128)(2,1)S(1)}, bf16[1536,768]{1,0:T(8,128)(2,1)}, u32[]{:S(2)}) copy-start(bf16[1536,768]{1,0:T(8,128)(2,1)} %param.32) | copy-start | bytes 7077892
  127.8 63.5 %slice-start = ((s8[4718592]{0:T(1024)(128)(4,1)}), s8[4194304]{0:T(1024)(128)(4,1)S(1)}, s32[]{:S(2)}) async-start(s8[4718592]{0:T(1024)(128)(4,1)} %bitcast.155), calls=%async_computation | async-start | bytes 8388608
  163.0 28.0 %copy-start.2 = (f32[8,192,256]{2,1,0:T(8,128)}, f32[8,192,256]{2,1,0:T(8,128)S(1)}, u32[]{:S(2)}) copy-start(f32[8,192,256]{2,1,0:T(8,128)S(1)} %get-tuple-element.49.wide) | copy-start | bytes 4718596
  163.0 28.0 %copy-start.8 = (f32[8,8,256]{2,1,0:T(8,128)}, f32[8,8,256]{2,1,0:T(8,128)S(1)}, u32[]{:S(2)}) copy-start(f32[8,8,256]{2,1,0:T(8,128)S(1)} %get-tuple-element.50.logs) | copy-start | bytes 196612
  163.0 28.4 %slice-start.1 = ((s8[4718592]{0:T(1024)(128)(4,1)}), s8[524288]{0:T(1024)(128)(4,1)S(1)}, s32[]{:S(2)}) async-start(s8[4718592]{0:T(1024)(128)(4,1)} %bitcast.155), calls=%async_computation.1 | async-start | bytes 1048576
  191.0 3.1 copy-start.15
  191.0 31.5 %copy-start.31 = (f32[512]{0:T(512)}, f32[512]{0:T(512)S(1)}, u32[]{:S(2)}) copy-start(f32[512]{0:T(512)S(1)} %broadcast_multiply_fusion) | copy-start | bytes 6148
  191.0 3.1 slice-start.2
  191.3 2.8 copy-start.33
  191.4 2.7 copy-start.44
  191.4 2.8 slice-start.3
  194.2 4.0 copy-start.50
  198.2 1.4 copy-start.25
  198.2 1.4 copy-start.43
  202.7 10.0 %copy-start.24 = (bf16[512,768]{1,0:T(8,128)(2,1)S(1)}, bf16[512,768]{1,0:T(8,128)(2,1)}, u32[]{:S(2)}) copy-start(bf16[512,768]{1,0:T(8,128)(2,1)} %get-tuple-element.130) | copy-start | bytes 2359300
  202.7 10.0 %copy-start.42 = (f32[3072]{0:T(1024)S(1)}, f32[3072]{0:T(1024)}, u32[]{:S(2)}) copy-start(f32[3072]{0:T(1024)} %copy-done.41) | copy-start | bytes 36868
  212.6 9.8 %copy-start.51 = (bf16[512,3072]{1,0:T(8,128)(2,1)}, bf16[512,3072]{1,0:T(8,128)(2,1)S(1)}, u32[]{:S(2)}) copy-start(bf16[512,3072]{1,0:T(8,128)(2,1)S(1)} %get-tuple-element.121) | copy-start | bytes 9437188
  212.6 9.9 %copy-start.16 = (f32[512,768]{1,0:T(8,128)S(1)}, f32[512,768]{1,0:T(8,128)}, u32[]{:S(2)}) copy-start(f32[512,768]{1,0:T(8,128)} %copy-done.15) | copy-start | bytes 4718596
  212.7 9.9 %copy-start.45 = (f32[512]{0:T(512)S(1)}, f32[512]{0:T(512)}, u32[]{:S(2)}) copy-start(f32[512]{0:T(512)} %copy-done.44) | copy-start | bytes 6148
  232.2 3.8 copy-start.17
  232.2 3.8 copy-start.32
  232.2 3.8 copy-start.35
  232.2 3.8 copy-start.46
  232.3 3.8 copy-start.49
  232.3 3.8 copy-start.52
  244.9 0.9 copy-start.22
  246.6 40.3 %copy-start.36 = (f32[768]{0:T(1024)S(1)}, f32[768]{0:T(1024)}, u32[]{:S(2)}) copy-start(f32[768]{0:T(1024)} %get-tuple-element.122) | copy-start | bytes 9220
  246.6 40.9 %copy-start.23 = (bf16[512,768]{1,0:T(8,128)(2,1)S(1)}, bf16[512,768]{1,0:T(8,128)(2,1)}, u32[]{:S(2)}) copy-start(bf16[512,768]{1,0:T(8,128)(2,1)} %copy-done.22) | copy-start | bytes 2359300
  285.0 1.0 copy-start.4
  286.0 0.9 copy-start.5
  329.2 49.5 %copy-start.11 = (bf16[2,2,4,48,1920]{4,3,2,1,0:T(8,128)(2,1)S(1)}, bf16[2,2,4,48,1920]{4,3,2,1,0:T(8,128)(2,1)}, u32[]{:S(2)}) copy-start(bf16[2,2,4,48,1920]{4,3,2,1,0:T(8,128)(2,1)} %copy-done.10) | copy-start | bytes 8847364
  329.2 49.5 %copy-start.13 = (bf16[2,256,768]{2,1,0:T(8,128)(2,1)S(1)}, bf16[2,256,768]{2,1,0:T(8,128)(2,1)}, u32[]{:S(2)}) copy-start(bf16[2,256,768]{2,1,0:T(8,128)(2,1)} %param.17) | copy-start | bytes 2359300
  329.2 49.5 %copy-start.29 = (f32[1,2,2,128]{3,1,2,0:T(2,128)S(1)}, f32[1,2,2,128]{3,1,2,0:T(2,128)}, u32[]{:S(2)}) copy-start(f32[1,2,2,128]{3,1,2,0:T(2,128)} %copy.43) | copy-start | bytes 6148
  378.7 4.7 copy-start.47
  378.7 4.7 copy-start.20
  383.5 2.8 copy-start.28
  383.5 2.8 copy-start.30
  384.0 2.4 copy-start.14
  386.4 3.6 copy-start.37
  386.4 3.6 copy-start.38
  386.4 3.6 copy-start.39
  386.4 3.6 copy-start.40
  532.3 9.1 %copy-start.21 = (bf16[2,8,24,1920]{3,2,1,0:T(8,128)(2,1)S(1)}, bf16[2,8,24,1920]{3,2,1,0:T(8,128)(2,1)}, u32[]{:S(2)}) copy-start(bf16[2,8,24,1920]{3,2,1,0:T(8,128)(2,1)} %get-tuple-element.58) | copy-start | bytes 4423684
  541.5 2.7 copy-start.19
  544.1 2.9 copy-start.18

commit v3 on v2

--- a/solution.py
+++ b/solution.py
@@ -70,19 +70,19 @@
     return pl.ds(pl.multiple_of(first + chip % PER_SEQ * R, R), R)
 
 
-def share_start(shard, full, sems, partner, core, wsh):
-    xs, xr, fs, fr, own = sems
+def share_start(shard, full, sems, sibling, partner, core, wsh):
+    xs, xr, fs, fr, own_send, own_recv = sems
     sends = []
     for k in range(shard.shape[1]):
         sends.append(remote(shard.at[core, k], full.at[wsh, core, k], xs.at[k], xr.at[k], partner))
         sends[-1].start()
-    local = pltpu.make_async_copy(shard, full.at[wsh], own)
-    local.start()
-    return sends, local
+    same = remote(shard, full.at[wsh], own_send, own_recv, sibling)
+    same.start()
+    return sends, same
 
 
 def share_pass(state, k, full, sems, sibling, core, wsh):
-    xs, xr, fs, fr, own = sems
+    xs, xr, fs, fr, own_send, own_recv = sems
     state[0][k].wait_recv()
     piece = full.at[1 - wsh, core, k]
     forward = remote(piece, piece, fs.at[k], fr.at[k], sibling)
@@ -100,7 +100,7 @@
 
 def share_scratch(shard):
     chunks = shard.shape[1]
-    return [DMA((chunks,)), DMA((chunks,)), DMA((chunks,)), DMA((chunks,)), DMA]
+    return [DMA((chunks,)), DMA((chunks,)), DMA((chunks,)), DMA((chunks,)), DMA, DMA]
 
 
 def full_of(shard):
@@ -110,20 +110,21 @@
 def first_kernel(weight, small, full, all_small, *sems):
     chip, core, same_core, sibling, partner, wsh = where_am_i()
     greet([sibling, partner])
-    pack = share_start(small, all_small, sems[5:], partner, core, wsh)
-    state = share_start(weight, full, sems[:5], partner, core, wsh)
-    passed = [share_pass(pack, 0, all_small, sems[5:], sibling, core, wsh)]
+    pack = share_start(small, all_small, sems[6:], sibling, partner, core, wsh)
+    state = share_start(weight, full, sems[:6], sibling, partner, core, wsh)
+    passed = [share_pass(pack, 0, all_small, sems[6:], sibling, core, wsh)]
     forwards = [
-        share_pass(state, k, full, sems[:5], sibling, core, wsh) for k in range(weight.shape[1])
+        share_pass(state, k, full, sems[:6], sibling, core, wsh) for k in range(weight.shape[1])
     ]
     share_end(pack, passed)
     share_end(state, forwards)
 
 
-def scatter_kernel(src, weight_a, weight_b, q_all, kv_all, full_a, full_b, *sems):
+def scatter_kernel(src, *refs):
     chip, core, same_core, sibling, partner, wsh = where_am_i()
-    send, recv, fsend, frecv, own = sems[:5]
-    sems_a, sems_b = sems[5:10], sems[10:]
+    weights, (q_all, kv_all), fulls, refs = refs[:3], refs[3:5], refs[5:8], refs[8:]
+    send, recv, fsend, frecv, own = refs[:5]
+    sems = [refs[5 + 6 * n : 11 + 6 * n] for n in range(3)]
     width = q_all.shape[2]
     greet([same_core((chip + i) % CHIPS) for i in range(1, CHIPS)] + [sibling, partner])
     block = 2 * chip + core
@@ -150,8 +151,9 @@
     local = [pltpu.make_async_copy(a, b, own.at[n]) for n, (a, b) in enumerate(pieces(chip))]
     for copy in local:
         copy.start()
-    state_a = share_start(weight_a, full_a, sems_a, partner, core, wsh)
-    state_b = share_start(weight_b, full_b, sems_b, partner, core, wsh)
+    states = [
+        share_start(weights[n], fulls[n], sems[n], sibling, partner, core, wsh) for n in range(3)
+    ]
     for copy in local:
         copy.wait()
     forwards = []
@@ -162,13 +164,12 @@
         came = 2 * ((chip + CHIPS - i) % CHIPS) + core
         forwards.append(remote(kv_all.at[came], kv_all.at[came], fsend.at[i], frecv.at[i], sibling))
         forwards[-1].start()
-    passed_a = [
-        share_pass(state_a, k, full_a, sems_a, sibling, core, wsh)
-        for k in range(weight_a.shape[1])
-    ]
-    passed_b = [
-        share_pass(state_b, k, full_b, sems_b, sibling, core, wsh)
-        for k in range(weight_b.shape[1])
+    passed = [
+        [
+            share_pass(states[n], k, fulls[n], sems[n], sibling, core, wsh)
+            for k in range(weights[n].shape[1])
+        ]
+        for n in range(3)
     ]
     for i in range(1, CHIPS):
         copies[i - 1][2].wait_recv()
@@ -177,30 +178,25 @@
             copy.wait_send()
     for copy in forwards:
         copy.wait()
-    share_end(state_a, passed_a)
-    share_end(state_b, passed_b)
-
-
-def home_kernel(src, weight, dst, full, send, recv, own, *sems):
+    for n in range(3):
+        share_end(states[n], passed[n])
+
+
+def home_kernel(src, dst, send, recv, own):
     chip, core, same_core, sibling, partner, wsh = where_am_i()
     width = src.shape[2]
-    greet([same_core((chip + i) % CHIPS) for i in range(1, CHIPS)] + [sibling, partner])
+    greet([same_core((chip + i) % CHIPS) for i in range(1, CHIPS)])
     place = dst.at[rows_of(chip, 0), lanes_of(chip, width)]
     copies = []
     for i in range(1, CHIPS):
         target = (chip + i) % CHIPS
         copies.append(remote(src.at[target], place, send.at[i], recv.at[i], same_core(target)))
         copies[-1].start()
-    state = share_start(weight, full, sems, partner, core, wsh)
     local = pltpu.make_async_copy(src.at[chip], place, own)
     local.start()
-    passed = [
-        share_pass(state, k, full, sems, sibling, core, wsh) for k in range(weight.shape[1])
-    ]
     local.wait()
     for copy in copies:
         copy.wait()
-    share_end(state, passed)
 
 
 def add_into(dst, parts):
@@ -276,10 +272,10 @@
     ]
 
 
-def away_kernel(src, terms, dst, result, send, recv, own, *pair):
+def away_kernel(src, dst, send, recv, own):
     chip, core, same_core, sibling, partner, wsh = where_am_i()
     width = dst.shape[2]
-    greet([same_core((chip + i) % CHIPS) for i in range(1, CHIPS)] + [sibling, partner])
+    greet([same_core((chip + i) % CHIPS) for i in range(1, CHIPS)])
     copies = []
     for i in range(1, CHIPS):
         target = (chip + i) % CHIPS
@@ -290,18 +286,16 @@
         src.at[rows_of(chip, 0), lanes_of(chip, width)], dst.at[chip], own
     )
     local.start()
-    gives = pair_start(terms, pair[:3], pair[3:], sibling, core, wsh)
-    sends = pair_cross(terms, pair[:3], pair[3:], gives, partner, core, wsh)
-    pair_end(terms, pair[:3], gives, sends, result, core, wsh)
     local.wait()
     for copy in copies:
         copy.wait()
 
 
-def return_kernel(dq, dkv, terms_a, terms_b, dst, result_a, result_b, *scratch):
+def return_kernel(dq, dkv, *refs):
     chip, core, same_core, sibling, partner, wsh = where_am_i()
-    give, take, final, send, recv, fsend, frecv, own = scratch[:8]
-    pair_a, pair_b = scratch[8:15], scratch[15:]
+    terms, dst, results, refs = refs[:3], refs[3], refs[4:7], refs[7:]
+    give, take, final, send, recv, fsend, frecv, own = refs[:8]
+    pairs = [refs[8 + 7 * n : 15 + 7 * n] for n in range(3)]
     width = dq.shape[2]
     greet([same_core((chip + i) % CHIPS) for i in range(1, CHIPS)] + [sibling, partner])
     lanes = lanes_of(chip, width)
@@ -328,8 +322,7 @@
         copies[-1].start()
     local = [pltpu.make_async_copy(dq.at[chip], dst.at[rows_of(chip, 0), lanes], own.at[0])]
     local[0].start()
-    gives_a = pair_start(terms_a, pair_a[:3], pair_a[3:], sibling, core, wsh)
-    gives_b = pair_start(terms_b, pair_b[:3], pair_b[3:], sibling, core, wsh)
+    gives = [pair_start(terms[n], pairs[n][:3], pairs[n][3:], sibling, core, wsh) for n in range(3)]
     for i in list(range(1, CHIPS)) + [0]:
         target = (chip + i) % CHIPS
         halves[i].wait_recv()
@@ -347,10 +340,12 @@
             else:
                 local.append(pltpu.make_async_copy(piece, place, own.at[n]))
                 local[-1].start()
-    sends_a = pair_cross(terms_a, pair_a[:3], pair_a[3:], gives_a, partner, core, wsh)
-    sends_b = pair_cross(terms_b, pair_b[:3], pair_b[3:], gives_b, partner, core, wsh)
-    pair_end(terms_a, pair_a[:3], gives_a, sends_a, result_a, core, wsh)
-    pair_end(terms_b, pair_b[:3], gives_b, sends_b, result_b, core, wsh)
+    sends = [
+        pair_cross(terms[n], pairs[n][:3], pairs[n][3:], gives[n], partner, core, wsh)
+        for n in range(3)
+    ]
+    for n in range(3):
+        pair_end(terms[n], pairs[n][:3], gives[n], sends[n], results[n], core, wsh)
     for copy in local:
         copy.wait()
     for copy in halves:
@@ -359,132 +354,134 @@
         copy.wait()
 
 
-def finish_kernel(small, *refs):
+CUT = 24
+
+
+def cuts_of(shapes):
+    cuts = []
+    for n, (pieces, rows, columns) in enumerate(shapes):
+        width = next(w for w in (768, 640, columns) if columns % w == 0)
+        cuts += [
+            (n, row, column, width)
+            for row in range(0, rows, CUT)
+            for column in range(0, columns, width)
+        ]
+    return cuts
+
+
+def finish_kernel(cuts, small, *refs):
     chip, core, same_core, sibling, partner, wsh = where_am_i()
     sums, terms = refs[:3], refs[3]
     all_small, outs = refs[4], refs[5:9]
-    kept = refs[9]
-    pair = refs[10:17]
-    stages = [refs[17 + 11 * n : 28 + 11 * n] for n in range(4)]
-    small_take, small_send, small_recv = refs[61:]
+    kept, pair, refs = refs[9], refs[10:17], refs[17:]
+    small_take, small_send, small_recv, refs = refs[0], refs[1], refs[2], refs[3:]
+    took_b, added, took_a = refs[: len(cuts)], refs[len(cuts) : 2 * len(cuts)], refs[2 * len(cuts) :]
+    took_a, (bs, br, zs, zr, gs, gr, hs, hr, ks, kr) = took_a[: len(cuts)], took_a[len(cuts) :]
     a, b = chip // 2, chip % 2
     along_a = [(a + i) % 4 for i in range(4)]
     other_b = same_core(2 * a + 1 - b)
     peers_a = [same_core(2 * other + b) for other in along_a]
     greet([sibling, partner, other_b] + peers_a[1:])
-
-    gives = pair_start(terms, pair[:3], pair[3:], sibling, core, wsh)
     mine = list(sums) + [kept]
-
-    def start_b(n):
-        took_b, added, took_a, bs, br, zs, zr, gs, gr, ks, kr = stages[n]
-        copy = remote(mine[n].at[pl.ds(pl.multiple_of(4 - 4 * b, 4), 4)], took_b, bs, br, other_b)
+    here, there = pl.multiple_of(4 * b, 4), pl.multiple_of(4 - 4 * b, 4)
+    flying = []
+
+    def go(*args):
+        copy = remote(*args)
         copy.start()
+        flying.append(copy)
         return copy
 
-    def start_a(n, swap):
-        took_b, added, took_a, bs, br, zs, zr, gs, gr, ks, kr = stages[n]
-        swap.wait_recv()
+    def whole(n, *where):
+        ref, row, column, width = (outs, mine)[len(where) == 1][cuts[n][0]], *cuts[n][1:]
+        return ref.at[(*where, pl.ds(row, CUT), pl.ds(column, width))]
+
+    def swap(n):
+        return go(whole(n, pl.ds(there, 4)), took_b[n], bs.at[n], br.at[n], other_b)
+
+    def spread(n, copy):
+        copy.wait_recv()
         copies = []
-        for i in (1, 2, 3, 0):
+        for i in (2, 1, 3, 0):
             other = along_a[i]
-            add_into(added.at[other], [mine[n].at[4 * b + other], took_b.at[other]])
+            add_into(added[n].at[other], [whole(n, here + other), took_b[n].at[other]])
             if i:
                 copies.append(
-                    remote(added.at[other], took_a.at[i - 1], zs.at[i], zr.at[i], peers_a[i])
+                    go(
+                        added[n].at[other],
+                        took_a[n].at[i - 1],
+                        zs.at[n, i - 1],
+                        zr.at[n, i - 1],
+                        peers_a[i],
+                    )
                 )
-                copies[-1].start()
         return copies
 
-    def give_out(n, copies):
-        took_b, added, took_a, bs, br, zs, zr, gs, gr, ks, kr = stages[n]
-        out = outs[n]
+    def give(n, copies):
         for copy in copies:
             copy.wait_recv()
-        piece = out.at[core, 4 * b + a]
-        add_into(piece, [added.at[a], took_a.at[0], took_a.at[1], took_a.at[2]])
-        news = []
-        for i in (1, 2, 3):
-            news.append(remote(piece, piece, gs.at[0, i], gr.at[0, i], peers_a[i]))
-        news.append(remote(piece, piece, gs.at[1, 0], gr.at[1, 0], other_b))
-        news.append(remote(piece, piece, ks.at[0, 0], kr.at[0, 0], sibling))
-        for copy in news:
-            copy.start()
-        return news
-
-    def hand_on(n, news):
-        took_b, added, took_a, bs, br, zs, zr, gs, gr, ks, kr = stages[n]
-        out = outs[n]
-        more = []
-        for i in (1, 2, 3):
-            news[i - 1].wait_recv()
-            piece = out.at[core, 4 * b + (a + 4 - i) % 4]
-            more.append(remote(piece, piece, gs.at[1, i], gr.at[1, i], other_b))
-            more.append(remote(piece, piece, ks.at[0, i], kr.at[0, i], sibling))
-            for copy in more[-2:]:
-                copy.start()
-        return more
-
-    def last_pass(n, news, more):
-        took_b, added, took_a, bs, br, zs, zr, gs, gr, ks, kr = stages[n]
-        out = outs[n]
-        final = []
-        for i in range(4):
-            (news[3] if i == 0 else more[2 * i - 2]).wait_recv()
-            piece = out.at[core, 4 - 4 * b + (a + 4 - i) % 4]
-            final.append(remote(piece, piece, ks.at[1, i], kr.at[1, i], sibling))
-            final[-1].start()
-        return final
-
-    swaps = [start_b(n) for n in range(3)]
+        piece = whole(n, core, here + a)
+        add_into(piece, [added[n].at[a]] + [took_a[n].at[i] for i in range(3)])
+        return [
+            go(piece, piece, gs.at[n, i - 1], gr.at[n, i - 1], peers_a[i]) for i in (2, 1, 3)
+        ]
+
+    def cross(n, copies):
+        for copy in copies:
+            copy.wait_recv()
+        half = whole(n, core, pl.ds(here, 4))
+        copies = [go(half, half, hs.at[n], hr.at[n], other_b)]
+        return copies + [go(half, half, ks.at[n, 0], kr.at[n, 0], sibling)]
+
+    def close(n, copies):
+        copies[0].wait_recv()
+        half = whole(n, core, pl.ds(there, 4))
+        return [copies[1], go(half, half, ks.at[n, 1], kr.at[n, 1], sibling)]
+
+    def small_start(n):
+        if n < 3:
+            small_take[3 + n] = all_small[...]
+            peer = (sibling, partner, other_b)[n]
+            place = small_take.at[3 + n], small_take.at[n], small_send.at[n], small_recv.at[n]
+            return [go(*place, peer)]
+        place = small_take.at[6 + a]
+        place[...] = all_small[...]
+        return [
+            go(place, place, small_send.at[2 + i], small_recv.at[2 + i], peers_a[i])
+            for i in (1, 2, 3)
+        ]
+
+    def small_end(n, copies):
+        for copy in copies:
+            copy.wait_recv()
+        if n < 3:
+            all_small[...] = all_small[...] + small_take[n]
+        else:
+            all_small[...] = (small_take[6] + small_take[7]) + (small_take[8] + small_take[9])
+
+    gives = pair_start(terms, pair[:3], pair[3:], sibling, core, wsh)
+    state = {0: swap(0), 1: swap(1)}
+    all_small[...] = small[...]
+    small_copies = small_start(0)
     sends = pair_cross(terms, pair[:3], pair[3:], gives, partner, core, wsh)
-
-    all_small[...] = small[...]
-    order = [sibling, partner, other_b]
-    for n, peer in enumerate(order):
-        small_take[3 + n] = all_small[...]
-        copy = remote(
-            small_take.at[3 + n], small_take.at[n], small_send.at[n], small_recv.at[n], peer
-        )
-        copy.start()
-        copy.wait()
-        all_small[...] = all_small[...] + small_take[n]
-    small_take[6 + a] = all_small[...]
-    smalls = []
-    for i in (1, 2, 3):
-        smalls.append(
-            remote(
-                small_take.at[6 + a],
-                small_take.at[6 + a],
-                small_send.at[2 + i],
-                small_recv.at[2 + i],
-                peers_a[i],
-            )
-        )
-        smalls[-1].start()
-
-    crossings = [start_a(n, swaps[n]) for n in range(3)]
-    pair_end(terms, pair[:3], gives, sends, kept, core, wsh)
-    swaps.append(start_b(3))
-    news = [give_out(n, crossings[n]) for n in range(3)]
-    crossings.append(start_a(3, swaps[3]))
-    more = [hand_on(n, news[n]) for n in range(3)]
-    news.append(give_out(3, crossings[3]))
-    final = [last_pass(n, news[n], more[n]) for n in range(3)]
-    more.append(hand_on(3, news[3]))
-    final.append(last_pass(3, news[3], more[3]))
-    for copy in smalls:
-        copy.wait()
-    all_small[...] = small_take[6] + small_take[7] + small_take[8] + small_take[9]
-    for n in range(4):
-        swaps[n].wait_send()
-        for copy in crossings[n] + news[n] + more[n] + final[n]:
-            copy.wait_send()
-        news[n][4].wait_recv()
-        for i in (1, 2, 3):
-            more[n][2 * i - 1].wait_recv()
-        for copy in final[n]:
+    late = next(n for n, cut in enumerate(cuts) if cut[0] == 3)
+    for tick in range(len(cuts) + 4):
+        if tick == late - 2:
+            pair_end(terms, pair[:3], gives, sends, kept, core, wsh)
+        if 2 <= tick + 2 < len(cuts):
+            state[tick + 2] = swap(tick + 2)
+        for lag, stage in enumerate((spread, give, cross, close)):
+            if 0 <= tick - lag < len(cuts):
+                state[tick - lag] = stage(tick - lag, state[tick - lag])
+        if tick < 4:
+            small_end(tick, small_copies)
+            if tick < 3:
+                small_copies = small_start(tick + 1)
+    for n in range(len(cuts)):
+        for copy in state[n]:
             copy.wait_recv()
+    for copy in flying:
+        copy.wait_send()
 
 
 ANY = pl.BlockSpec(memory_space=pl.ANY)
@@ -510,18 +507,17 @@
     )(weight, small)
 
 
-def scatter_heads(src, weight_a, weight_b, width):
+def scatter_heads(src, weights, width):
     return pl.pallas_call(
         scatter_kernel,
         name="scatter_heads",
-        out_shape=(
+        out_shape=[
             jax.ShapeDtypeStruct((CHIPS, R, width), jnp.bfloat16),
             jax.ShapeDtypeStruct((GROUP, 2 * R, width), jnp.bfloat16),
-            full_of(weight_a),
-            full_of(weight_b),
-        ),
-        in_specs=[ANY] * 3,
-        out_specs=(ANY,) * 4,
+        ]
+        + [full_of(weight) for weight in weights],
+        in_specs=[ANY] * 4,
+        out_specs=[ANY] * 5,
         scratch_shapes=[
             DMA((3, CHIPS)),
             DMA((3, CHIPS)),
@@ -529,54 +525,50 @@
             DMA((CHIPS,)),
             DMA((3,)),
         ]
-        + share_scratch(weight_a)
-        + share_scratch(weight_b),
+        + [item for weight in weights for item in share_scratch(weight)],
         compiler_params=comm_params(0),
-    )(src, weight_a, weight_b)
-
-
-def send_home(src, weight):
+    )(src, *weights)
+
+
+def send_home(src):
     width = src.shape[2]
     return pl.pallas_call(
         home_kernel,
         name="send_home",
-        out_shape=(jax.ShapeDtypeStruct((D, SEQS * width), jnp.bfloat16), full_of(weight)),
-        in_specs=[ANY, ANY],
-        out_specs=(ANY, ANY),
-        scratch_shapes=[DMA((CHIPS,)), DMA((CHIPS,)), DMA] + share_scratch(weight),
+        out_shape=jax.ShapeDtypeStruct((D, SEQS * width), jnp.bfloat16),
+        in_specs=[ANY],
+        out_specs=ANY,
+        scratch_shapes=[DMA((CHIPS,)), DMA((CHIPS,)), DMA],
         compiler_params=comm_params(1),
-    )(src, weight)
+    )(src)
 
 
 def sum_of(terms):
     return jax.ShapeDtypeStruct(terms.shape[2:], jnp.bfloat16)
 
 
-def send_away(src, terms, width):
+def send_away(src, width):
     return pl.pallas_call(
         away_kernel,
         name="send_away",
-        out_shape=(jax.ShapeDtypeStruct((CHIPS, R, width), jnp.bfloat16), sum_of(terms)),
-        in_specs=[ANY, VMEM],
-        out_specs=(ANY, VMEM),
-        scratch_shapes=[DMA((CHIPS,)), DMA((CHIPS,)), DMA] + pair_scratch(terms),
+        out_shape=jax.ShapeDtypeStruct((CHIPS, R, width), jnp.bfloat16),
+        in_specs=[ANY],
+        out_specs=ANY,
+        scratch_shapes=[DMA((CHIPS,)), DMA((CHIPS,)), DMA],
         compiler_params=comm_params(2),
-    )(src, terms)
-
-
-def return_heads(dq, dkv, terms_a, terms_b):
+    )(src)
+
+
+def return_heads(dq, dkv, terms):
     width = dq.shape[2]
     pair = pltpu.VMEM((CHIPS, 2 * R, width), jnp.bfloat16)
     return pl.pallas_call(
         return_kernel,
         name="return_heads",
-        out_shape=(
-            jax.ShapeDtypeStruct((3 * D, SEQS * width), jnp.bfloat16),
-            sum_of(terms_a),
-            sum_of(terms_b),
-        ),
-        in_specs=[ANY, VMEM, VMEM, VMEM],
-        out_specs=(ANY, VMEM, VMEM),
+        out_shape=[jax.ShapeDtypeStruct((3 * D, SEQS * width), jnp.bfloat16)]
+        + [sum_of(part) for part in terms],
+        in_specs=[ANY] + [VMEM] * 4,
+        out_specs=[ANY] + [VMEM] * 3,
         scratch_shapes=[
             pair,
             pair,
@@ -587,34 +579,18 @@
             DMA((CHIPS,)),
             DMA((3,)),
         ]
-        + pair_scratch(terms_a)
-        + pair_scratch(terms_b),
+        + [item for part in terms for item in pair_scratch(part)],
         compiler_params=comm_params(3, 56),
-    )(dq, dkv, terms_a, terms_b)
+    )(dq, dkv, *terms)
 
 
 def finish_sums(small, sums, terms):
-    def stage(total):
-        rows, columns = total.shape[1:]
-        four = pltpu.VMEM((4, rows, columns), jnp.bfloat16)
-        return [
-            four,
-            four,
-            pltpu.VMEM((3, rows, columns), jnp.bfloat16),
-            DMA,
-            DMA,
-            DMA((4,)),
-            DMA((4,)),
-            DMA((2, 4)),
-            DMA((2, 4)),
-            DMA((2, 4)),
-            DMA((2, 4)),
-        ]
-
     kept = sum_of(terms)
     whole = [*sums, kept]
+    cuts = cuts_of([total.shape for total in whole])
+    count = len(cuts)
     return pl.pallas_call(
-        finish_kernel,
+        functools.partial(finish_kernel, cuts),
         name="finish_sums",
         out_shape=[jax.ShapeDtypeStruct(small.shape, small.dtype)]
         + [jax.ShapeDtypeStruct((2,) + total.shape, total.dtype) for total in whole],
@@ -622,12 +598,13 @@
         out_specs=[VMEM] * 5,
         scratch_shapes=[pltpu.VMEM(kept.shape, kept.dtype)]
         + pair_scratch(terms)
-        + [item for total in whole for item in stage(total)]
-        + [
-            pltpu.VMEM((10,) + small.shape, small.dtype),
-            DMA((6,)),
-            DMA((6,)),
-        ],
+        + [pltpu.VMEM((10,) + small.shape, small.dtype), DMA((6,)), DMA((6,))]
+        + [pltpu.VMEM((4, CUT, cut[3]), jnp.bfloat16) for cut in cuts] * 2
+        + [pltpu.VMEM((3, CUT, cut[3]), jnp.bfloat16) for cut in cuts]
+        + [DMA((count,)), DMA((count,))]
+        + [DMA((count, 3)) for _ in range(4)]
+        + [DMA((count,)), DMA((count,))]
+        + [DMA((count, 2)), DMA((count, 2))],
         compiler_params=comm_params(5, 56),
     )(small, *sums, terms)
 
@@ -887,21 +864,23 @@
         ],
         axis=0,
     )
-    q_all, kv_all, out_full, fc_full = scatter_heads(
+    q_all, kv_all, out_full, fc_full, proj_full = scatter_heads(
         sent,
-        w_out.reshape(2, 1, w_out.shape[0] // 2, -1),
-        w_fc.reshape(2, 4, w_fc.shape[0] // 8, -1),
+        [
+            part.reshape(2, chunks, part.shape[0] // (2 * chunks), -1)
+            for part, chunks in ((w_out, 1), (w_fc, 4), (w_proj, 4))
+        ],
         width,
     )
     out_weight, fc_weight = out_full.reshape(D, D), fc_full.reshape(D, -1)
+    proj_weight = proj_full.reshape(-1, D)
     if halo:
         ahead = [(i, i + GROUP) for i in range(ctx_size - GROUP)]
         kv_all = jnp.concatenate(
             [lax.ppermute(kv_all[GROUP - halo :], "ctx", ahead), kv_all], axis=0
         )
     out_wide, out_low, logs = attention_forward(info, q_all, kv_all, lo, halo)
-    attended, proj_full = send_home(out_low, w_proj.reshape(2, 4, w_proj.shape[0] // 8, -1))
-    proj_weight = proj_full.reshape(-1, D)
+    attended = send_home(out_low)
     resid = inputs + over_rows(attended, out_weight) + out_shift.astype(jnp.float32)
     normed2, norm2_back = jax.vjp(
         norm_layer, resid, norm2_gain.astype(jnp.float32), norm2_shift.astype(jnp.float32)
@@ -936,14 +915,14 @@
     grad_out_w = jnp.dot(attended, grad_branch, preferred_element_type=jnp.float32)
     grad_out_b = jnp.sum(grad_branch.astype(jnp.float32), axis=0)
     grad_attended = over_lanes(out_weight, grad_branch).astype(jnp.bfloat16)
-    grad_all, proj_sum = send_away(grad_attended, as_terms(grad_proj_w, 4), width)
+    grad_all = send_away(grad_attended, width)
     dq, dkv = attention_backward(info, q_all, kv_all, lo, grad_all, out_wide, logs, halo)
     if halo:
         behind = [(i + GROUP, i) for i in range(ctx_size - GROUP)]
         over = lax.ppermute(dkv[:halo].astype(jnp.bfloat16), "ctx", behind)
         dkv = dkv[halo:].at[GROUP - halo :].add(over.astype(jnp.float32))
-    grads_t, fc_sum, out_sum = return_heads(
-        dq, dkv, as_terms(grad_fc_w, 4), as_terms(grad_out_w, 1)
+    grads_t, proj_sum, fc_sum, out_sum = return_heads(
+        dq, dkv, [as_terms(grad_proj_w, 4), as_terms(grad_fc_w, 4), as_terms(grad_out_w, 1)]
     )
     grad_projected = grads_t[: 2 * D + VW]
     grad_first = grads_t[2 * D + VW :].T.astype(jnp.float32)

time: 559 us -> 516 us (0.923)
  Pallas kernels: 422 us -> 378 us
    pallas_call x5, Pallas kernels: 326 us -> 291 us  [the longest x1 102 us: finish_sums(): pl.pallas_call(functools.partial(finish_kernel, cuts), name='finish_sums'...]
where the time goes in v3:
time: 516 us; the launch traced here: 510 us
  Pallas kernels  378 us (73%)
  matrix products  57.8 us (11%)
  other arithmetic  38.1 us (7%)
  local copies, waits for them, and re-layouts  31.1 us (6%)
    pallas_call x1, Pallas kernels, finish_sums(): pl.pallas_call(functools.partial(finish_kernel, cuts), name='finish_sums'...  102 us
    pallas_call x1, Pallas kernels, return_heads(): pl.pallas_call(return_kernel, name='return_heads', out_shape=[jax.ShapeDt...  89.8 us
    pallas_call x1, Pallas kernels, scatter_heads(): pl.pallas_call(scatter_kernel, name='scatter_heads', out_shape=[jax.Shape...  66.3 us
    pallas_call x1, Pallas kernels, attention_backward(): pl.pallas_call(functools.partial(backward_kernel, halo), name='attention_...  35.1 us
    pallas_call x1, Pallas kernels, attention_forward(): pl.pallas_call(functools.partial(forward_kernel, halo), name='attention_f...  30.4 us
    pallas_call x1, Pallas kernels, gather_first(): pl.pallas_call(first_kernel, name='gather_first', out_shape=(full_of(weig...  21.5 us
    dot_general x3, matrix products, over_lanes(): lax.dot_general(left, right, (((1,), (1,)), ((), ())), preferred_element_...  19 us
    pallas_call x1, Pallas kernels, send_away(): pl.pallas_call(away_kernel, name='send_away', out_shape=jax.ShapeDtypeStr...  16.8 us

profile of v3, /device:TPU:1, one launch (start us, length us, event | category | flops | bytes accessed | tf_op | source)
XLA Modules:
  0.0 509.9 jit_solution(12094101234249098560)
XLA Ops:
  0.8 1.4 dynamic_slice.18
  2.8 1.3 fusion.34
  4.1 1.3 compare_convert_fusion
  5.4 1.3 convert_reduce_fusion.3
  6.8 0.6 copy.43
  7.3 1.5 fusion.18
  8.9 0.6 copy.44
  9.4 5.6 %concatenate.19 = bf16[4416]{0:T(1024)(128)(2,1)S(1)} concatenate(bf16[384]{0:T(512)(128)(2,1)} %param.22, bf16[384]{0:T(512)(128)(2,1)} %param.23, bf16[576]{0:T(1024)(128)(2,1)} %param.25, bf16[384]{0:T(512)(128)(2,1)} %param.27, bf16[384]{0:T(512)(128)(2,1)} %param.28, bf16[384]{0:T(512)(128)(2,1)} %param.29, bf16[1536]{0:T(1024)(128)(2,1)} %param.31, bf16[384]{0:T(512)(128)(2,1)} %param.33), dimensions={0} | concatenate | bytes 17664 | tf_op jit(solution)/shard_map/concatenate | solution.py:812
  15.1 0.5 broadcast.210
  15.6 1.5 fusion.40
  17.1 3.4 convert_reduce_fusion
  20.9 21.5 %gather_first.1 = (bf16[2,2,4,48,1920]{4,3,2,1,0:T(8,128)(2,1)S(1)}, bf16[2,2,1,32,128]{4,3,2,1,0:T(8,128)(2,1)S(1)}) custom-call(bf16[2,4,48,1920]{3,2,1,0:T(8,128)(2,1)S(1)} %bitcast.117, bf16[2,1,32,128]{3,2,1,0:T(8,128)(2,1)S(1)} %bitcast.119), custom_call_target="tpu_custom_call" | custom-call | tf_op jit(solution)/shard_map/gather_first/pallas_call | solution.py:499
  42.5 1.6 copy-done.8
  44.5 0.4 fusion.21
  44.8 3.6 fusion.45
  49.0 0.9 copy-done.5
  49.9 66.3 %scatter_heads.1 = (bf16[8,192,256]{2,1,0:T(8,128)(2,1)S(1)}, bf16[16,384,256]{2,1,0:T(8,128)(2,1)}, bf16[2,2,1,192,768]{4,3,2,1,0:T(8,128)(2,1)S(1)}, bf16[2,2,...) custom-call(bf16[2304,512]{1,0:T(8,128)(2,1)S(1)} %pad_maximum_fusion.src, bf16[2,1,192,768]{3,2,1,0:T(8,128)(2,1)S(1)} %bitcast.118, ...), custom_call_target="tpu_custom_call" | custom-call | tf_op jit(solution)/shard_map/scatter_heads/pallas_call | solution.py:511
  116.3 30.4 %attention_forward.1 = (f32[8,192,256]{2,1,0:T(8,128)S(1)}, bf16[8,192,256]{2,1,0:T(8,128)(2,1)S(1)}, f32[8,8,256]{2,1,0:T(8,128)S(1)}) custom-call(s32[10]{0:T(128)S(1)} %pad_add_fusion.info, bf16[8,192,256]{2,1,0:T(8,128)(2,1)S(1)} %get-tuple-element.39.q, bf16[16,384,256]{2,1,0:T(8,128)(2,1)} %get-tuple-element.40.kv, s32[8,8,256]{2,1,0:T(8,128)S(1)} %broadcast_in_dim.10.lo), custom_call_target="tpu_custom_call" | custom-call | tf_op jit(solution)/shard_map/attention_forward/pallas_call | solution.py:690
  146.7 1.1 copy-done.2
  147.9 16.4 %send_home.1 = bf16[768,512]{1,0:T(8,128)(2,1)S(1)} custom-call(bf16[8,192,256]{2,1,0:T(8,128)(2,1)S(1)} %get-tuple-element.42.src), custom_call_target="tpu_custom_call" | custom-call | tf_op jit(solution)/shard_map/send_home/pallas_call | solution.py:535
  164.3 0.9 fusion.44
  165.6 1.6 copy-done.48
  167.2 2.7 fusion.36
  170.0 4.0 add_add_fusion.3
  174.0 1.0 bitcast_convert_fusion.5
  174.9 0.4 copy-done.24
  175.4 1.1 multiply_reduce_fusion
  176.5 1.4 convert_reduce_fusion.4
  177.9 0.6 reshape.387
  178.5 11.2 %convert_reduce_fusion.1 = (f32[3072]{0:T(1024)}, bf16[512,3072]{1,0:T(8,128)(2,1)S(1)}) fusion(f32[512,3072]{1,0:T(8,128)} %copy-done.49, f32[3072]{0:T(1024)} %copy-done.39, bf16[512,768]{1,0:T(8,128)(2,1)} %bitcast.138, bf16[3072,768]{1,0:T(8,128)(2,1)} %bitcast.156), kind=kOutput, calls=%fused_computation.10 | convolution fusion | flops 2452091904 | bytes 14966784 | tf_op jit(solution)/shard_map/dot_general | solution.py:619
  189.8 9.8 %convolution_convert_fusion.1 = bf16[3072,768]{1,0:T(8,128)(2,1)} fusion(bf16[512,768]{1,0:T(8,128)(2,1)S(1)} %copy-done.22, f32[512,3072]{1,0:T(8,128)} %copy-done.49, f32[3072]{0:T(1024)S(1)} %copy-done.40), kind=kOutput, calls=%fused_computation.13 | convolution fusion | flops 2434007040 | bytes 11808768 | tf_op jit(solution)/shard_map/dot_general | solution.py:613
  199.7 7.0 %multiply_reduce_fusion.1 = (f32[768]{0:T(1024)}, f32[512]{0:T(512)}, f32[768]{0:T(1024)}, f32[512,768]{1,0:T(8,128)}) fusion(f32[512,768]{1,0:T(8,128)S(1)} %copy-done.16, f32[512]{0:T(512)S(1)} %copy-done.43, f32[512]{0:T(512)S(1)} %broadcast_multiply_fusion, f32[768]{0:T(1024)S(1)} %reshape.403, bf16[512,3072]{1,0:T(8,128)(2,1)S(1)} %get-tuple-element.117, ...), kind=kOutput, calls=%fused_computation.49 | convolution fusion | flops 2419062784 | bytes 11025408 | tf_op jit(solution)/shard_map/dot_general | solution.py:619
  206.6 0.7 reshape.386
  207.4 1.3 reshape.384
  208.6 0.7 multiply_multiply_fusion.3
  209.4 3.7 fusion.39
  213.2 5.2 %convolution_convert_fusion = bf16[768,3072]{1,0:T(8,128)(2,1)} fusion(bf16[512,3072]{1,0:T(8,128)(2,1)S(1)} %copy-done.51, f32[512,768]{1,0:T(8,128)S(1)} %copy-done.17, f32[768]{0:T(1024)S(1)} %copy-done.47, f32[768]{0:T(1024)S(1)} %copy-done.34, f32[512]{0:T(512)S(1)} %copy-done.44, f32[512]{0:T(512)S(1)} %copy-done.31), kind=kOutput, calls=%fused_computation.12 | convolution fusion | flops 2420244480 | bytes 9447424 | tf_op jit(solution)/shard_map/dot_general | solution.py:613
  218.3 0.6 negate_multiply_fusion.1
  218.9 1.3 reshape.385
  220.2 2.3 convert_reduce_fusion.5
  222.5 0.8 convolution_convert_fusion.4.src
  223.3 16.8 %send_away.1.grad = bf16[8,192,256]{2,1,0:T(8,128)(2,1)S(1)} custom-call(bf16[768,512]{1,0:T(8,128)(2,1)S(1)} %convolution_convert_fusion.4.src), custom_call_target="tpu_custom_call" | custom-call | tf_op jit(solution)/shard_map/send_away/pallas_call | solution.py:551
  240.2 0.9 copy-done
  241.1 2.9 convolution_convert_fusion.3
  244.0 35.1 %attention_backward.1 = (bf16[8,192,256]{2,1,0:T(8,128)(2,1)}, f32[16,384,256]{2,1,0:T(8,128)}) custom-call(s32[10]{0:T(128)} %copy-done.7, bf16[8,192,256]{2,1,0:T(8,128)(2,1)} %copy-done.1, bf16[16,384,256]{2,1,0:T(8,128)(2,1)} %get-tuple-element.40.kv, s32[8,8,256]{2,1,0:T(8,128)} %copy-done.4, bf16[8,192,256]{2,1,0:T(8,128)(2,1)} %copy-done, ...), custom_call_target="tpu_custom_call" | custom-call | tf_op jit(solution)/shard_map/attention_backward/pallas_call | solution.py:761
  279.1 89.8 %return_heads.1 = (bf16[2304,512]{1,0:T(8,128)(2,1)}, bf16[4,192,768]{2,1,0:T(8,128)(2,1)}, bf16[4,48,3072]{2,1,0:T(8,128)(2,1)}, bf16[1,192,768]{2,1,0:T(8,128)(2,1)}) custom-call(bf16[8,192,256]{2,1,0:T(8,128)(2,1)} %get-tuple-element.47.dq, f32[16,384,256]{2,1,0:T(8,128)} %get-tuple-element.48.dkv, bf16[2,2,4,192,768]{4,3,2,1,0:T(8,128)(2,1)} %bitcast.126, ...), custom_call_target="tpu_custom_call" | custom-call | tf_op jit(solution)/shard_map/return_heads/pallas_call | solution.py:565
  369.0 4.7 fusion.22
  374.2 2.3 fusion.35
  376.6 3.6 add_add_fusion.2
  380.5 1.3 concatenate.23
  381.7 0.6 pad_bitcast_fusion.small
  382.3 1.1 convert_bitcast_fusion
  383.4 5.0 convolution_convert_fusion.2
  388.4 1.1 copy.41
  389.6 101.6 %finish_sums.1 = (f32[72,128]{1,0:T(8,128)}, bf16[2,8,96,768]{3,2,1,0:T(8,128)(2,1)}, bf16[2,8,24,3072]{3,2,1,0:T(8,128)(2,1)}, bf16[2,8,24,768]{3,2,1,0:T(8,128)(2,1)}, bf16[2,8,24,1920]{3,2,1,0:T(8,128)(2,1)}) custom-call(f32[72,128]{1,0:T(8,128)} %pad_bitcast_fusion.small, bf16[8,96,768]{2,1,0:T(8,128)(2,1)} %bitcast.134, bf16[8,24,3072]{2,1,0:T(8,128)(2,1)} %bitcast.135, ...), custom_call_target="tpu_custom_call" | custom-call | tf_op jit(solution)/shard_map/finish_sums/pallas_call | solution.py:592
  491.2 1.4 fusion.42
  493.9 1.4 dynamic-slice.2
  495.3 1.4 dynamic-slice.6
  496.6 1.5 fusion.41
  498.2 2.2 bitcast_convert_fusion.4
  500.3 1.9 bitcast_convert_fusion.3
  502.2 0.8 copy-done.19
  503.0 2.9 bitcast_convert_fusion.1
  505.9 2.7 bitcast_convert_fusion
  (146 shorter events, 2.7 us)
Async XLA Ops:
  0.6 20.3 %copy-start.3 = (bf16[384,1920]{1,0:T(8,128)(2,1)S(1)}, bf16[384,1920]{1,0:T(8,128)(2,1)}, u32[]{:S(2)}) copy-start(bf16[384,1920]{1,0:T(8,128)(2,1)} %param.24) | copy-start | bytes 4423684
  0.7 20.1 %copy-start.25 = (bf16[2,256,384]{2,1,0:T(8,128)(2,1)S(1)}, bf16[2,256,384]{2,1,0:T(8,128)(2,1)}, u32[]{:S(2)}) copy-start(bf16[2,256,384]{2,1,0:T(8,128)(2,1)} %param.18) | copy-start | bytes 1179652
  6.7 37.7 %copy-start.12 = (bf16[2,256,768]{2,1,0:T(8,128)(2,1)S(1)}, bf16[2,256,768]{2,1,0:T(8,128)(2,1)}, u32[]{:S(2)}) copy-start(bf16[2,256,768]{2,1,0:T(8,128)(2,1)} %param.17) | copy-start | bytes 2359300
  20.7 95.6 %copy-start.7 = (s32[10]{0:T(128)}, s32[10]{0:T(128)S(1)}, u32[]{:S(2)}) copy-start(s32[10]{0:T(128)S(1)} %pad_add_fusion.info) | copy-start | bytes 124
  20.7 95.5 %copy-start.4 = (s32[8,8,256]{2,1,0:T(8,128)}, s32[8,8,256]{2,1,0:T(8,128)S(1)}, u32[]{:S(2)}) copy-start(s32[8,8,256]{2,1,0:T(8,128)S(1)} %broadcast_in_dim.10.lo) | copy-start | bytes 196612
  42.4 1.6 copy-start.8
  44.4 125.5 %copy-start.39 = (f32[3072]{0:T(1024)}, f32[3072]{0:T(1024)S(1)}, u32[]{:S(2)}) copy-start(f32[3072]{0:T(1024)S(1)} %reshape.405) | copy-start | bytes 36868
  44.4 155.3 %copy-start.33 = (f32[768]{0:T(1024)}, f32[768]{0:T(1024)S(1)}, u32[]{:S(2)}) copy-start(f32[768]{0:T(1024)S(1)} %reshape.403) | copy-start | bytes 9220
  44.4 121.2 %copy-start.46 = (f32[768]{0:T(1024)}, f32[768]{0:T(1024)S(1)}, u32[]{:S(2)}) copy-start(f32[768]{0:T(1024)S(1)} %reshape.404) | copy-start | bytes 9220
  44.4 4.0 copy-start.26
  48.9 1.1 copy-start.5
  116.2 30.5 %copy-start.1 = (bf16[8,192,256]{2,1,0:T(8,128)(2,1)}, bf16[8,192,256]{2,1,0:T(8,128)(2,1)S(1)}, u32[]{:S(2)}) copy-start(bf16[8,192,256]{2,1,0:T(8,128)(2,1)S(1)} %get-tuple-element.39.q) | copy-start | bytes 2359300
  146.7 1.1 copy-start.2
  147.9 17.4 %copy-start.6 = (f32[8,8,256]{2,1,0:T(8,128)}, f32[8,8,256]{2,1,0:T(8,128)S(1)}, u32[]{:S(2)}) copy-start(f32[8,8,256]{2,1,0:T(8,128)S(1)} %get-tuple-element.46.logs) | copy-start | bytes 196612
  164.3 2.9 copy-start.48
  165.2 4.7 copy-start.15
  165.3 34.4 %copy-start.30 = (f32[512]{0:T(512)}, f32[512]{0:T(512)S(1)}, u32[]{:S(2)}) copy-start(f32[512]{0:T(512)S(1)} %broadcast_multiply_fusion) | copy-start | bytes 6148
  165.3 4.7 slice-start
  165.6 4.3 copy-start.32
  167.2 2.7 copy-start.42
  167.2 2.7 slice-start.1
  170.0 4.0 copy-start.49
  173.9 1.4 copy-start.24
  174.0 1.4 copy-start.41
  176.5 43.7 %copy-start.10 = (f32[2,256,768]{2,1,0:T(8,128)}, f32[2,256,768]{2,1,0:T(8,128)S(1)}, u32[]{:S(2)}) copy-start(f32[2,256,768]{2,1,0:T(8,128)S(1)} %get-tuple-element.113) | copy-start | bytes 4718596
  178.5 11.3 %copy-start.22 = (bf16[512,768]{1,0:T(8,128)(2,1)S(1)}, bf16[512,768]{1,0:T(8,128)(2,1)}, u32[]{:S(2)}) copy-start(bf16[512,768]{1,0:T(8,128)(2,1)} %get-tuple-element.126) | copy-start | bytes 2359300
  178.5 11.3 %copy-start.40 = (f32[3072]{0:T(1024)S(1)}, f32[3072]{0:T(1024)}, u32[]{:S(2)}) copy-start(f32[3072]{0:T(1024)} %copy-done.39) | copy-start | bytes 36868
  189.8 9.8 %copy-start.50 = (bf16[512,3072]{1,0:T(8,128)(2,1)}, bf16[512,3072]{1,0:T(8,128)(2,1)S(1)}, u32[]{:S(2)}) copy-start(bf16[512,3072]{1,0:T(8,128)(2,1)S(1)} %get-tuple-element.117) | copy-start | bytes 9437188
  189.8 9.9 %copy-start.16 = (f32[512,768]{1,0:T(8,128)S(1)}, f32[512,768]{1,0:T(8,128)}, u32[]{:S(2)}) copy-start(f32[512,768]{1,0:T(8,128)} %copy-done.15) | copy-start | bytes 4718596
  189.8 9.9 %copy-start.43 = (f32[512]{0:T(512)S(1)}, f32[512]{0:T(512)}, u32[]{:S(2)}) copy-start(f32[512]{0:T(512)} %copy-done.42) | copy-start | bytes 6148
  209.3 3.8 copy-start.17
  209.3 3.8 copy-start.31
  209.4 3.8 copy-start.34
  209.4 3.8 copy-start.44
  209.4 3.8 copy-start.47
  209.4 3.8 copy-start.51
  222.4 0.9 copy-start.23
  222.5 0.9 copy-start.35
  240.2 0.9 copy-start
  279.1 89.8 %copy-start.9 = (bf16[2,2,4,48,1920]{4,3,2,1,0:T(8,128)(2,1)S(1)}, bf16[2,2,4,48,1920]{4,3,2,1,0:T(8,128)(2,1)}, u32[]{:S(2)}) copy-start(bf16[2,2,4,48,1920]{4,3,2,1,0:T(8,128)(2,1)} %copy-done.8) | copy-start | bytes 8847364
  279.1 89.8 %copy-start.13 = (bf16[2,256,768]{2,1,0:T(8,128)(2,1)S(1)}, bf16[2,256,768]{2,1,0:T(8,128)(2,1)}, u32[]{:S(2)}) copy-start(bf16[2,256,768]{2,1,0:T(8,128)(2,1)} %param.17) | copy-start | bytes 2359300
  279.1 89.8 %copy-start.28 = (f32[1,2,2,128]{3,1,2,0:T(2,128)S(1)}, f32[1,2,2,128]{3,1,2,0:T(2,128)}, u32[]{:S(2)}) copy-start(f32[1,2,2,128]{3,1,2,0:T(2,128)} %copy.43) | copy-start | bytes 6148
  368.9 4.7 copy-start.45
  369.0 4.7 copy-start.20
  373.7 2.9 copy-start.11
  373.7 2.9 copy-start.27
  373.7 2.9 copy-start.29
  374.2 2.4 copy-start.14
  376.6 3.6 copy-start.36
  376.6 3.6 copy-start.37
  376.6 3.6 copy-start.38
  491.2 9.1 %copy-start.21 = (bf16[2,8,24,1920]{3,2,1,0:T(8,128)(2,1)S(1)}, bf16[2,8,24,1920]{3,2,1,0:T(8,128)(2,1)}, u32[]{:S(2)}) copy-start(bf16[2,8,24,1920]{3,2,1,0:T(8,128)(2,1)} %get-tuple-element.54) | copy-start | bytes 4423684
  500.3 2.7 copy-start.19
  503.0 2.9 copy-start.18
